TPU v7x, 128 devices: a whole 4x4x4 slice. The times are simulated.
128 devices in a mesh: grp: 4 (over y_hi, core), ctx: 32 (over x, y_lo, z).
Axes of the slice: x: 4, y: 4 (y_hi: 2, y_lo: 2; y = y_hi * 2 + y_lo), z: 4, core: 2. Of those that a mesh axis runs over, the one named last changes fastest.
Arguments:
- clip_queries: bfloat16 [4, 4096, 4096], P('grp', 'ctx'), may hold values from -6 to 6
- clip_keys: bfloat16 [4, 4096, 4096], P('grp', 'ctx'), may hold values from -6 to 6
- clip_values: bfloat16 [4, 4096, 4096], P('grp', 'ctx'), may hold values from -6 to 6
- cache_keys: bfloat16 [4, 4, 4096, 4096], P('grp', None, 'ctx'), may hold values from -6 to 6
- cache_values: bfloat16 [4, 4, 4096, 4096], P('grp', None, 'ctx'), may hold values from -6 to 6
- clip_pick: int32 [4, 2], P('grp'), may hold values from 0 to 3
- noisy_latent: bfloat16 [4, 128, 2, 1024], P('grp', 'ctx'), may hold values from -6 to 6
- prev_latent: bfloat16 [4, 128, 2, 1024], P('grp', 'ctx'), may hold values from -6 to 6
- velocity_weight: bfloat16 [4096, 64], replicated, may hold values from -0.09375 to 0.09375
- tile_owner: int32 [4, 128], P('grp', 'ctx'), may hold values from 0 to 3, as said below
- conv_in_weight: bfloat16 [432, 512], replicated, may hold values from -0.3125 to 0.3125
- conv_in_bias: float32 [512], replicated, may hold values from -4 to 4
- conv_out_weight: bfloat16 [9, 512, 128], replicated, may hold values from -0.09375 to 0.09375
- conv_out_bias: float32 [128], replicated, may hold values from -4 to 4
Outputs:
- decoded: bfloat16 [4, 32, 4, 2, 2, 256, 128], P('grp', 'ctx')
Inputs may be any that keep to these rules, and one draw needn't show every extreme that they name: `tile_owner`: of one device's 4 tiles at most 2 name the same owner; in every draw some device names one owner 2 times, and some owner is named 2 times by every device with its ctx index.
All inputs are finite; a program needn't handle non-finite values.
Results may differ from a plain program's by a relative error of at most 0.007.
Values may be sent and summed in bfloat16 or wider, within the bound.
No kernel may reach another device: no remote copies, remote signals or barrier semaphores. Data moves between devices by JAX's collectives and lax.ppermute only.
A program may use at most 192 MiB of HBM per device.

v0:
```python
import math

import jax
import jax.numpy as jnp
from jax import lax
from jax.sharding import PartitionSpec as P

LFR = 2
TP = 4
HEADS = 32
HD = 128
LAT = 16


def first_frame(rows):
    shape = rows.shape
    grouped = rows.reshape((shape[0] // (LFR * TP * TP), LFR, TP * TP) + shape[1:])
    return grouped[:, 0].reshape((-1,) + shape[1:])


def to_tiles(per_token):
    count = per_token.shape[0] // (LFR * TP * TP)
    split = per_token.reshape(count, LFR, TP, TP, 2, 2, LAT)
    return split.transpose(0, 1, 2, 4, 3, 5, 6).reshape(count, LFR, 4 * TP * TP * LAT)


def decode_tiles(stacked, conv_in_weight, conv_in_bias, conv_out_weight, conv_out_bias):
    count = stacked.shape[0]
    side = 2 * TP
    middle = conv_in_weight.shape[1]
    outer = conv_out_weight.shape[2]
    latent = stacked.reshape(count, LFR + 2, side, side, LAT)
    padded = jnp.pad(latent, ((0, 0), (0, 0), (1, 1), (1, 1), (0, 0)))
    columns = []
    for time_off in range(3):
        for row_off in range(3):
            for col_off in range(3):
                columns.append(
                    padded[
                        :,
                        time_off : time_off + LFR,
                        row_off : row_off + side,
                        col_off : col_off + side,
                        :,
                    ]
                )
    patches = jnp.stack(columns, axis=4).reshape(count * LFR * side * side, 27 * LAT)
    hidden = jax.nn.silu(
        jnp.dot(patches, conv_in_weight, preferred_element_type=jnp.float32) + conv_in_bias
    )
    hidden = hidden.astype(jnp.bfloat16).reshape(count, LFR, side, side, middle)
    larger = jnp.repeat(jnp.repeat(hidden, 2, axis=2), 2, axis=3)
    big_side = 2 * side
    larger = jnp.pad(larger, ((0, 0), (0, 0), (1, 1), (1, 1), (0, 0)))
    total = jnp.zeros((count * LFR * big_side * big_side, outer), jnp.float32)
    for row_off in range(3):
        for col_off in range(3):
            window = larger[
                :, :, row_off : row_off + big_side, col_off : col_off + big_side, :
            ].reshape(-1, middle)
            total = total + jnp.dot(
                window, conv_out_weight[row_off * 3 + col_off], preferred_element_type=jnp.float32
            )
    return (
        (total + conv_out_bias).astype(jnp.bfloat16).reshape(count, LFR, big_side * big_side, outer)
    )


def tile_slots(owners, owner_count):
    count = owners.shape[0]
    slot_count = count // 2
    same = owners[:, None] == owners[None, :]
    earlier = (
        jnp.arange(count, dtype=jnp.int32)[None, :] < jnp.arange(count, dtype=jnp.int32)[:, None]
    )
    rank = jnp.sum(jnp.where(same & earlier, 1, 0), axis=1).astype(jnp.int32)
    target = jnp.arange(owner_count * slot_count, dtype=jnp.int32)
    return (owners[None, :] == (target // slot_count)[:, None]) & (
        rank[None, :] == (target % slot_count)[:, None]
    )


def local(
    clip_queries,
    clip_keys,
    clip_values,
    cache_keys,
    cache_values,
    clip_pick,
    noisy_latent,
    prev_latent,
    velocity_weight,
    tile_owner,
    conv_in_weight,
    conv_in_bias,
    conv_out_weight,
    conv_out_bias,
):
    tokens = clip_queries.shape[1]
    width = clip_queries.shape[2]
    query_heads, key_heads, value_heads = (
        lax.all_to_all(
            clip_queries[0].reshape(tokens, HEADS, HD),
            "ctx",
            split_axis=1,
            concat_axis=0,
            tiled=True,
        ),
        lax.all_to_all(
            clip_keys[0].reshape(tokens, HEADS, HD), "ctx", split_axis=1, concat_axis=0, tiled=True
        ),
        lax.all_to_all(
            clip_values[0].reshape(tokens, HEADS, HD),
            "ctx",
            split_axis=1,
            concat_axis=0,
            tiled=True,
        ),
    )

    def pick(table, index):
        return lax.dynamic_index_in_dim(table[0], index, 0, keepdims=False).reshape(
            tokens, HEADS, HD
        )

    sink_keys = pick(cache_keys, clip_pick[0, 0])
    sink_values = pick(cache_values, clip_pick[0, 0])
    window_keys = pick(cache_keys, clip_pick[0, 1])
    window_values = pick(cache_values, clip_pick[0, 1])
    sink_keys, sink_values, window_keys, window_values = (
        lax.all_to_all(sink_keys, "ctx", split_axis=1, concat_axis=0, tiled=True),
        lax.all_to_all(sink_values, "ctx", split_axis=1, concat_axis=0, tiled=True),
        lax.all_to_all(window_keys, "ctx", split_axis=1, concat_axis=0, tiled=True),
        lax.all_to_all(window_values, "ctx", split_axis=1, concat_axis=0, tiled=True),
    )
    sink_keys = first_frame(sink_keys)
    sink_values = first_frame(sink_values)
    all_keys = jnp.concatenate([sink_keys, window_keys, key_heads], axis=0)
    all_values = jnp.concatenate([sink_values, window_values, value_heads], axis=0)
    rows = query_heads.shape[0]
    heads_here = query_heads.shape[1]
    block = min(512, rows)
    blocks = query_heads.reshape(rows // block, block, heads_here, HD)
    scale = 1.0 / math.sqrt(HD)

    def attend(query_block):
        scores = (
            jnp.einsum("qhd,khd->hqk", query_block, all_keys, preferred_element_type=jnp.float32)
            * scale
        )
        raised = jnp.exp(scores - jnp.max(scores, axis=2, keepdims=True))
        totals = jnp.sum(raised, axis=2)
        mixed = jnp.einsum(
            "hqk,khd->qhd",
            raised.astype(jnp.bfloat16),
            all_values,
            preferred_element_type=jnp.float32,
        )
        return (mixed / totals.T[:, :, None]).astype(jnp.bfloat16)

    attended = lax.map(attend, blocks).reshape(rows, heads_here, HD)
    by_token = lax.all_to_all(attended, "ctx", split_axis=0, concat_axis=1, tiled=True).reshape(
        tokens, width
    )
    squares = jnp.mean(by_token.astype(jnp.float32) ** 2, axis=1, keepdims=True)
    velocity = jnp.dot(by_token, velocity_weight, preferred_element_type=jnp.float32) / jnp.sqrt(
        squares + 1e-06
    )
    clean = (noisy_latent[0].astype(jnp.float32) - to_tiles(velocity)).astype(jnp.bfloat16)
    stacked = jnp.concatenate([prev_latent[0], clean], axis=1)
    owner_count = lax.axis_size("grp")
    slot_count = stacked.shape[0] // 2
    selector = jnp.where(tile_slots(tile_owner[0], owner_count), 1.0, 0.0).astype(jnp.bfloat16)
    outgoing = jnp.einsum(
        "st,tfc->sfc", selector, stacked, preferred_element_type=jnp.float32
    ).astype(jnp.bfloat16)
    outgoing = outgoing.reshape((owner_count, slot_count) + stacked.shape[1:])
    present = (
        jnp.sum(selector.astype(jnp.float32), axis=1)
        .astype(jnp.bfloat16)
        .reshape(owner_count, slot_count)
    )
    arrived, arrived_flags = (
        lax.all_to_all(outgoing, "grp", split_axis=0, concat_axis=0, tiled=True),
        lax.all_to_all(present, "grp", split_axis=0, concat_axis=0, tiled=True),
    )
    remote_out = decode_tiles(
        arrived.reshape((owner_count * slot_count,) + stacked.shape[1:]),
        conv_in_weight,
        conv_in_bias,
        conv_out_weight,
        conv_out_bias,
    )
    remote_out = jnp.where(
        arrived_flags.reshape(-1)[:, None, None, None] > 0, remote_out, jnp.zeros_like(remote_out)
    )
    received = remote_out.reshape((owner_count, slot_count) + remote_out.shape[1:])
    return received[None, None]


def solution(mesh):
    in_specs = (
        P("grp", "ctx", None),
        P("grp", "ctx", None),
        P("grp", "ctx", None),
        P("grp", None, "ctx", None),
        P("grp", None, "ctx", None),
        P("grp", None),
        P("grp", "ctx", None, None),
        P("grp", "ctx", None, None),
        P(),
        P("grp", "ctx"),
        P(),
        P(),
        P(),
        P(),
    )
    out_specs = P("grp", "ctx", None, None, None, None, None)
    return jax.shard_map(local, mesh=mesh, in_specs=in_specs, out_specs=out_specs, check_vma=False)
```

profile of v0, /device:TPU:1, one launch (start us, length us, event | category | flops | bytes accessed | tf_op | source)
XLA Modules:
  0.0 538.4 jit_solution(3915582983328852542)
XLA Ops:
  11.6 9.9 %all-to-all-start.5 = ((bf16[128,32,128]{0,2,1:T(8,128)(2,1)}), bf16[128,32,128]{0,2,1:T(8,128)(2,1)}, u32[]{:S(2)}, u32[]{:S(2)}) async-start(bf16[128,32,128]{0,2,1:T(8,128)(2,1)} %bitcast.301), calls=%async_computation.5 | async-start | bytes 2097152 | tf_op jit(solution)/shard_map/all_to_all | solution.py:132
  23.7 12.4 %all-to-all-done.5 = bf16[128,32,128]{0,2,1:T(8,128)(2,1)} async-done(((bf16[128,32,128]{0,2,1:T(8,128)(2,1)}), bf16[128,32,128]{0,2,1:T(8,128)(2,1)}, u32[]{:S(2)}, u32[]{:S(2)}) %all-to-all-start.5) | async-done | bytes 1048608 | tf_op jit(solution)/shard_map/all_to_all | solution.py:132
  44.5 11.9 %all-to-all-done.6 = bf16[128,32,128]{0,2,1:T(8,128)(2,1)} async-done(((bf16[128,32,128]{0,2,1:T(8,128)(2,1)}), bf16[128,32,128]{0,2,1:T(8,128)(2,1)}, u32[]{:S(2)}, u32[]{:S(2)}) %all-to-all-start.6) | async-done | bytes 1048608 | tf_op jit(solution)/shard_map/all_to_all | solution.py:134
  64.5 12.8 %all-to-all-done.7 = bf16[128,32,128]{0,2,1:T(8,128)(2,1)} async-done(((bf16[128,32,128]{0,2,1:T(8,128)(2,1)}), bf16[128,32,128]{0,2,1:T(8,128)(2,1)}, u32[]{:S(2)}, u32[]{:S(2)}) %all-to-all-start.7) | async-done | bytes 1048608 | tf_op jit(solution)/shard_map/all_to_all | solution.py:112
  85.3 12.9 %all-to-all-done.2 = bf16[128,32,128]{0,2,1:T(8,128)(2,1)S(1)} async-done(((bf16[128,32,128]{0,2,1:T(8,128)(2,1)}), bf16[128,32,128]{0,2,1:T(8,128)(2,1)S(1)}, u32[]{:S(2)}, u32[]{:S(2)}) %all-to-all-start.2) | async-done | bytes 1048608 | tf_op jit(solution)/shard_map/all_to_all | solution.py:131
  107.1 11.9 %all-to-all-done.3 = bf16[128,32,128]{0,2,1:T(8,128)(2,1)S(1)} async-done(((bf16[128,32,128]{0,2,1:T(8,128)(2,1)}), bf16[128,32,128]{0,2,1:T(8,128)(2,1)S(1)}, u32[]{:S(2)}, u32[]{:S(2)}) %all-to-all-start.3) | async-done | bytes 1048608 | tf_op jit(solution)/shard_map/all_to_all | solution.py:133
  128.1 11.9 %all-to-all-done.4 = bf16[128,32,128]{0,2,1:T(8,128)(2,1)} async-done(((bf16[128,32,128]{0,2,1:T(8,128)(2,1)}), bf16[128,32,128]{0,2,1:T(8,128)(2,1)}, u32[]{:S(2)}, u32[]{:S(2)}) %all-to-all-start.4) | async-done | bytes 1048608 | tf_op jit(solution)/shard_map/all_to_all | solution.py:109
  163.7 12.7 %pad_maximum_fusion.1 = bf16[10240,1,128]{2,0,1:T(8,128)(2,1)} fusion(bf16[4096,1,128]{2,0,1:T(8,128)(2,1)S(1)} %bitcast.290, bf16[4096,1,128]{2,0,1:T(8,128)(2,1)S(1)} %bitcast.289, bf16[2048,1,128]{2,0,1:T(8,128)(2,1)S(1)} %bitcast.306), kind=kLoop, calls=%fused_computation.60 | loop fusion | flops 7864320 | bytes 5242880 | tf_op jit(solution)/shard_map/concatenate | solution.py:139
  176.4 11.8 %pad_maximum_fusion = bf16[10240,1,128]{2,0,1:T(8,128)(2,1)S(1)} fusion(bf16[4096,1,128]{2,0,1:T(8,128)(2,1)S(1)} %bitcast.292, bf16[4096,1,128]{2,0,1:T(8,128)(2,1)S(1)} %bitcast.291, bf16[2048,1,128]{2,0,1:T(8,128)(2,1)S(1)} %bitcast.307), kind=kLoop, calls=%fused_computation.59 | loop fusion | flops 7864320 | bytes 5242880 | tf_op jit(solution)/shard_map/concatenate | solution.py:138
  188.2 181.2 %while.10 = (s32[]{:T(128)}, bf16[8,512,1,128]{3,1,2,0:T(8,128)(2,1)}, bf16[8,512,1,128]{3,1,2,0:T(8,128)(2,1)}, bf16[10240,1,128]{2,0,1:T(8,128)(2,1)S(1)}, bf16[10240,1,128]{2,0,1:T(8,128)(2,1)}, /*index=5*/s32[]{:T(128)}) while((s32[]{:T(128)}, bf16[8,512,1,128]{3,1,2,0:T(8,128)(2,1)}, bf16[8,512,1,128]{3,1,2,0:T(8,128)(2,1)}, ...), condition=%wide.region_5.6_spmd, body=%wide.region_2.5_spmd.sunk | while | flops 2726427648 | bytes 162802816 | solution.py:161
  200.2 10.9 %fusion.137 = bf16[8,512,1,128]{3,1,2,0:T(8,128)(2,1)} fusion(bf16[8,512,1,128]{3,1,2,0:T(8,128)(2,1)} %get-tuple-element.135, s32[]{:T(128)} %get-tuple-element.134, bf16[10240,1,128]{2,0,1:T(8,128)(2,1)S(1)} %copy-done.14, f32[512,10240]{1,0:T(8,128)} %copy-done.1, f32[512]{0:T(512)S(1)} %get-tuple-element.127, f32[512]{0:T(512)S(1)} %fusion.136), kind=kOutput, calls=%fused_computation.12.clone.1 | convolution fusion | flops 1358036992 | bytes 23728640 | tf_op jit(solution)/shard_map/while/body/eval_jaxpr/hqk,khd->qhd/dot_general | solution.py:153
  222.8 10.9 %fusion.137 = bf16[8,512,1,128]{3,1,2,0:T(8,128)(2,1)} fusion(bf16[8,512,1,128]{3,1,2,0:T(8,128)(2,1)} %get-tuple-element.135, s32[]{:T(128)} %get-tuple-element.134, bf16[10240,1,128]{2,0,1:T(8,128)(2,1)S(1)} %copy-done.14, f32[512,10240]{1,0:T(8,128)} %copy-done.1, f32[512]{0:T(512)S(1)} %get-tuple-element.127, f32[512]{0:T(512)S(1)} %fusion.136), kind=kOutput, calls=%fused_computation.12.clone.1 | convolution fusion | flops 1358036992 | bytes 23728640 | tf_op jit(solution)/shard_map/while/body/eval_jaxpr/hqk,khd->qhd/dot_general | solution.py:153
  245.4 10.9 %fusion.137 = bf16[8,512,1,128]{3,1,2,0:T(8,128)(2,1)} fusion(bf16[8,512,1,128]{3,1,2,0:T(8,128)(2,1)} %get-tuple-element.135, s32[]{:T(128)} %get-tuple-element.134, bf16[10240,1,128]{2,0,1:T(8,128)(2,1)S(1)} %copy-done.14, f32[512,10240]{1,0:T(8,128)} %copy-done.1, f32[512]{0:T(512)S(1)} %get-tuple-element.127, f32[512]{0:T(512)S(1)} %fusion.136), kind=kOutput, calls=%fused_computation.12.clone.1 | convolution fusion | flops 1358036992 | bytes 23728640 | tf_op jit(solution)/shard_map/while/body/eval_jaxpr/hqk,khd->qhd/dot_general | solution.py:153
  268.0 10.9 %fusion.137 = bf16[8,512,1,128]{3,1,2,0:T(8,128)(2,1)} fusion(bf16[8,512,1,128]{3,1,2,0:T(8,128)(2,1)} %get-tuple-element.135, s32[]{:T(128)} %get-tuple-element.134, bf16[10240,1,128]{2,0,1:T(8,128)(2,1)S(1)} %copy-done.14, f32[512,10240]{1,0:T(8,128)} %copy-done.1, f32[512]{0:T(512)S(1)} %get-tuple-element.127, f32[512]{0:T(512)S(1)} %fusion.136), kind=kOutput, calls=%fused_computation.12.clone.1 | convolution fusion | flops 1358036992 | bytes 23728640 | tf_op jit(solution)/shard_map/while/body/eval_jaxpr/hqk,khd->qhd/dot_general | solution.py:153
  290.6 10.9 %fusion.137 = bf16[8,512,1,128]{3,1,2,0:T(8,128)(2,1)} fusion(bf16[8,512,1,128]{3,1,2,0:T(8,128)(2,1)} %get-tuple-element.135, s32[]{:T(128)} %get-tuple-element.134, bf16[10240,1,128]{2,0,1:T(8,128)(2,1)S(1)} %copy-done.14, f32[512,10240]{1,0:T(8,128)} %copy-done.1, f32[512]{0:T(512)S(1)} %get-tuple-element.127, f32[512]{0:T(512)S(1)} %fusion.136), kind=kOutput, calls=%fused_computation.12.clone.1 | convolution fusion | flops 1358036992 | bytes 23728640 | tf_op jit(solution)/shard_map/while/body/eval_jaxpr/hqk,khd->qhd/dot_general | solution.py:153
  313.2 10.9 %fusion.137 = bf16[8,512,1,128]{3,1,2,0:T(8,128)(2,1)} fusion(bf16[8,512,1,128]{3,1,2,0:T(8,128)(2,1)} %get-tuple-element.135, s32[]{:T(128)} %get-tuple-element.134, bf16[10240,1,128]{2,0,1:T(8,128)(2,1)S(1)} %copy-done.14, f32[512,10240]{1,0:T(8,128)} %copy-done.1, f32[512]{0:T(512)S(1)} %get-tuple-element.127, f32[512]{0:T(512)S(1)} %fusion.136), kind=kOutput, calls=%fused_computation.12.clone.1 | convolution fusion | flops 1358036992 | bytes 23728640 | tf_op jit(solution)/shard_map/while/body/eval_jaxpr/hqk,khd->qhd/dot_general | solution.py:153
  335.9 10.9 %fusion.137 = bf16[8,512,1,128]{3,1,2,0:T(8,128)(2,1)} fusion(bf16[8,512,1,128]{3,1,2,0:T(8,128)(2,1)} %get-tuple-element.135, s32[]{:T(128)} %get-tuple-element.134, bf16[10240,1,128]{2,0,1:T(8,128)(2,1)S(1)} %copy-done.14, f32[512,10240]{1,0:T(8,128)} %copy-done.1, f32[512]{0:T(512)S(1)} %get-tuple-element.127, f32[512]{0:T(512)S(1)} %fusion.136), kind=kOutput, calls=%fused_computation.12.clone.1 | convolution fusion | flops 1358036992 | bytes 23728640 | tf_op jit(solution)/shard_map/while/body/eval_jaxpr/hqk,khd->qhd/dot_general | solution.py:153
  358.5 10.9 %fusion.137 = bf16[8,512,1,128]{3,1,2,0:T(8,128)(2,1)} fusion(bf16[8,512,1,128]{3,1,2,0:T(8,128)(2,1)} %get-tuple-element.135, s32[]{:T(128)} %get-tuple-element.134, bf16[10240,1,128]{2,0,1:T(8,128)(2,1)S(1)} %copy-done.14, f32[512,10240]{1,0:T(8,128)} %copy-done.1, f32[512]{0:T(512)S(1)} %get-tuple-element.127, f32[512]{0:T(512)S(1)} %fusion.136), kind=kOutput, calls=%fused_computation.12.clone.1 | convolution fusion | flops 1358036992 | bytes 23728640 | tf_op jit(solution)/shard_map/while/body/eval_jaxpr/hqk,khd->qhd/dot_general | solution.py:153
  373.8 7.4 %all-to-all-start.8 = ((bf16[32,2,8192]{2,1,0:T(2,128)(2,1)}), bf16[32,2,8192]{2,1,0:T(2,128)(2,1)S(1)}, u32[]{:S(2)}, u32[]{:S(2)}) async-start(bf16[32,2,8192]{2,1,0:T(2,128)(2,1)} %reshape.213), calls=%async_computation.8 | async-start | bytes 2097152 | tf_op jit(solution)/shard_map/all_to_all | solution.py:162
  382.1 13.7 %all-to-all-done.8 = bf16[32,2,8192]{2,1,0:T(2,128)(2,1)S(1)} async-done(((bf16[32,2,8192]{2,1,0:T(2,128)(2,1)}), bf16[32,2,8192]{2,1,0:T(2,128)(2,1)S(1)}, u32[]{:S(2)}, u32[]{:S(2)}) %all-to-all-start.8) | async-done | bytes 1048608 | tf_op jit(solution)/shard_map/all_to_all | solution.py:162
  442.4 17.5 %copy.178 = bf16[8,2,8,8,27,16]{5,4,3,2,1,0:T(8,128)(2,1)} copy(bf16[8,2,8,8,27,16]{5,3,2,1,0,4:T(8,128)(2,1)} %fusion.85) | data formatting | bytes 1769472 | tf_op jit(solution)/shard_map/stack | solution.py:47
  459.9 12.7 %reshape.197 = bf16[1024,432]{1,0:T(8,128)(2,1)S(1)} reshape(bf16[8,2,8,8,27,16]{5,4,3,2,1,0:T(8,128)(2,1)} %copy.178) | data formatting | bytes 1769472 | tf_op jit(solution)/shard_map/reshape | solution.py:47
  475.9 7.4 %pad_slice_fusion.31 = (bf16[8,2,16,16,512]{4,0,3,2,1:T(8,128)(2,1)}, bf16[8,2,16,16,512]{4,0,3,2,1:T(8,128)(2,1)}, bf16[8,2,16,16,512]{4,0,3,2,1:T(8,128)(2,1)S...) fusion(bf16[8,2,16,16,512]{4,0,3,2,1:T(8,128)(2,1)S(1)} %bitcas, ...), kind=kLoop, calls=%fused_computation.58 | loop fusion | bytes 37748736 | tf_op jit(solution)/shard_map/slice | solution.py:58
  504.1 7.4 %reshape.205 = bf16[4096,512]{1,0:T(8,128)(2,1)} reshape(bf16[8,2,16,8,2,512]{5,4,3,2,1,0:T(2,128)(2,1)} %broadcast_in_dim.56) | data formatting | bytes 8388608 | tf_op jit(solution)/shard_map/reshape | solution.py:60
  (196 shorter events, 272.0 us)
Async XLA Ops:
  0.0 409.2 %copy-start = (bf16[4096,64]{0,1:T(8,128)(2,1)S(1)}, bf16[4096,64]{0,1:T(8,128)(2,1)}, u32[]{:S(2)}) copy-start(bf16[4096,64]{0,1:T(8,128)(2,1)} %param.24) | copy-start | bytes 1572868
  11.6 24.6 %all-to-all-start.5 = ((bf16[128,32,128]{0,2,1:T(8,128)(2,1)}), bf16[128,32,128]{0,2,1:T(8,128)(2,1)}, u32[]{:S(2)}, u32[]{:S(2)}) async-start(bf16[128,32,128]{0,2,1:T(8,128)(2,1)} %bitcast.301), calls=%async_computation.5 | async-start | bytes 2097152 | tf_op jit(solution)/shard_map/all_to_all | solution.py:132
  36.1 20.2 %all-to-all-start.6 = ((bf16[128,32,128]{0,2,1:T(8,128)(2,1)}), bf16[128,32,128]{0,2,1:T(8,128)(2,1)}, u32[]{:S(2)}, u32[]{:S(2)}) async-start(bf16[128,32,128]{0,2,1:T(8,128)(2,1)} %bitcast.297), calls=%async_computation.6 | async-start | bytes 2097152 | tf_op jit(solution)/shard_map/all_to_all | solution.py:134
  56.4 21.0 %all-to-all-start.7 = ((bf16[128,32,128]{0,2,1:T(8,128)(2,1)}), bf16[128,32,128]{0,2,1:T(8,128)(2,1)}, u32[]{:S(2)}, u32[]{:S(2)}) async-start(bf16[128,32,128]{0,2,1:T(8,128)(2,1)} %bitcast.298), calls=%async_computation.7 | async-start | bytes 2097152 | tf_op jit(solution)/shard_map/all_to_all | solution.py:112
  77.3 20.9 %all-to-all-start.2 = ((bf16[128,32,128]{0,2,1:T(8,128)(2,1)}), bf16[128,32,128]{0,2,1:T(8,128)(2,1)S(1)}, u32[]{:S(2)}, u32[]{:S(2)}) async-start(bf16[128,32,128]{0,2,1:T(8,128)(2,1)} %bitcast.296), calls=%async_computation.2 | async-start | bytes 2097152 | tf_op jit(solution)/shard_map/all_to_all | solution.py:131
  98.2 29.9 %copy-start.12 = (bf16[128,32,128]{0,2,1:T(8,128)(2,1)}, bf16[128,32,128]{0,2,1:T(8,128)(2,1)S(1)}, u32[]{:S(2)}) copy-start(bf16[128,32,128]{0,2,1:T(8,128)(2,1)S(1)} %all-to-all-done.2) | copy-start | bytes 3145732
  98.2 20.8 %all-to-all-start.3 = ((bf16[128,32,128]{0,2,1:T(8,128)(2,1)}), bf16[128,32,128]{0,2,1:T(8,128)(2,1)S(1)}, u32[]{:S(2)}, u32[]{:S(2)}) async-start(bf16[128,32,128]{0,2,1:T(8,128)(2,1)} %bitcast.299), calls=%async_computation.3 | async-start | bytes 2097152 | tf_op jit(solution)/shard_map/all_to_all | solution.py:133
  119.0 29.9 %copy-start.13 = (bf16[128,32,128]{0,2,1:T(8,128)(2,1)}, bf16[128,32,128]{0,2,1:T(8,128)(2,1)S(1)}, u32[]{:S(2)}) copy-start(bf16[128,32,128]{0,2,1:T(8,128)(2,1)S(1)} %all-to-all-done.3) | copy-start | bytes 3145732
  119.0 21.0 %all-to-all-start.4 = ((bf16[128,32,128]{0,2,1:T(8,128)(2,1)}), bf16[128,32,128]{0,2,1:T(8,128)(2,1)}, u32[]{:S(2)}, u32[]{:S(2)}) async-start(bf16[128,32,128]{0,2,1:T(8,128)(2,1)} %bitcast.300), calls=%async_computation.4 | async-start | bytes 2097152 | tf_op jit(solution)/shard_map/all_to_all | solution.py:109
  140.0 21.5 %all-to-all-start.1 = ((bf16[128,32,128]{0,2,1:T(8,128)(2,1)}), bf16[128,32,128]{0,2,1:T(8,128)(2,1)}, u32[]{:S(2)}, u32[]{:S(2)}) async-start(bf16[128,32,128]{0,2,1:T(8,128)(2,1)} %bitcast.295), calls=%async_computation.1 | async-start | bytes 2097152 | tf_op jit(solution)/shard_map/all_to_all | solution.py:102
  163.7 12.7 %copy-start.10 = (bf16[32,128,1,128]{3,1,0,2:T(8,128)(2,1)S(1)}, bf16[32,128,1,128]{3,1,0,2:T(8,128)(2,1)}, u32[]{:S(2)}) copy-start(bf16[32,128,1,128]{3,1,0,2:T(8,128)(2,1)} %copy.162) | copy-start | bytes 3145732
  163.7 12.7 %copy-start.11 = (bf16[32,128,1,128]{3,1,0,2:T(8,128)(2,1)S(1)}, bf16[32,128,1,128]{3,1,0,2:T(8,128)(2,1)}, u32[]{:S(2)}) copy-start(bf16[32,128,1,128]{3,1,0,2:T(8,128)(2,1)} %copy.164) | copy-start | bytes 3145732
  163.7 12.7 %copy-start.15 = (bf16[128,1,16,1,128]{4,2,1,0,3:T(8,128)(2,1)S(1)}, bf16[128,1,16,1,128]{4,2,1,0,3:T(8,128)(2,1)}, u32[]{:S(2)}) copy-start(bf16[128,1,16,1,128]{4,2,1,0,3:T(8,128)(2,1)} %slice.198) | copy-start | bytes 1572868
  192.3 7.9 %copy-start.1 = (f32[512,10240]{1,0:T(8,128)}, f32[512,10240]{1,0:T(8,128)S(1)}, u32[]{:S(2)}) copy-start(f32[512,10240]{1,0:T(8,128)S(1)} %get-tuple-element.126) | copy-start | bytes 62914564 | tf_op jit(solution)/shard_map/while
  214.9 7.9 %copy-start.1 = (f32[512,10240]{1,0:T(8,128)}, f32[512,10240]{1,0:T(8,128)S(1)}, u32[]{:S(2)}) copy-start(f32[512,10240]{1,0:T(8,128)S(1)} %get-tuple-element.126) | copy-start | bytes 62914564 | tf_op jit(solution)/shard_map/while
  237.5 7.9 %copy-start.1 = (f32[512,10240]{1,0:T(8,128)}, f32[512,10240]{1,0:T(8,128)S(1)}, u32[]{:S(2)}) copy-start(f32[512,10240]{1,0:T(8,128)S(1)} %get-tuple-element.126) | copy-start | bytes 62914564 | tf_op jit(solution)/shard_map/while
  260.1 7.9 %copy-start.1 = (f32[512,10240]{1,0:T(8,128)}, f32[512,10240]{1,0:T(8,128)S(1)}, u32[]{:S(2)}) copy-start(f32[512,10240]{1,0:T(8,128)S(1)} %get-tuple-element.126) | copy-start | bytes 62914564 | tf_op jit(solution)/shard_map/while
  369.4 11.8 %copy-start.17 = (bf16[1,4,2,1024]{3,2,1,0:T(2,128)(2,1)S(1)}, bf16[1,4,2,1024]{3,2,1,0:T(2,128)(2,1)}, u32[]{:S(2)}) copy-start(bf16[1,4,2,1024]{3,2,1,0:T(2,128)(2,1)} %param.23) | copy-start | bytes 49156
  369.4 11.8 %copy-start.20 = (s32[1,4]{1,0:T(1,128)S(1)}, s32[1,4]{1,0:T(1,128)}, u32[]{:S(2)}) copy-start(s32[1,4]{1,0:T(1,128)} %param.25) | copy-start | bytes 52
  373.8 22.1 %all-to-all-start.8 = ((bf16[32,2,8192]{2,1,0:T(2,128)(2,1)}), bf16[32,2,8192]{2,1,0:T(2,128)(2,1)S(1)}, u32[]{:S(2)}, u32[]{:S(2)}) async-start(bf16[32,2,8192]{2,1,0:T(2,128)(2,1)} %reshape.213), calls=%async_computation.8 | async-start | bytes 2097152 | tf_op jit(solution)/shard_map/all_to_all | solution.py:162
  395.8 15.5 %all-to-all-start = ((bf16[4,1,2]{2,1,0:T(2,128)(2,1)}), bf16[4,1,2]{2,1,0:T(2,128)(2,1)S(1)}, u32[]{:S(2)}, u32[]{:S(2)}) async-start(bf16[4,1,2]{2,1,0:T(2,128)(2,1)} %all_to_all.136), calls=%async_computation | async-start | bytes 4096 | tf_op jit(solution)/shard_map/all_to_all | solution.py:185
  411.3 9.6 %all-to-all-start.9 = ((bf16[4,2,4,1024]{3,1,2,0:T(2,128)(2,1)}), bf16[4,2,4,1024]{3,1,2,0:T(2,128)(2,1)S(1)}, u32[]{:S(2)}, u32[]{:S(2)}) async-start(bf16[4,2,4,1024]{3,1,2,0:T(2,128)(2,1)} %copy.176), calls=%async_computation.9 | async-start | bytes 131072 | tf_op jit(solution)/shard_map/all_to_all | solution.py:184
  459.9 12.8 %copy-start.21 = (bf16[432,512]{1,0:T(8,128)(2,1)S(1)}, bf16[432,512]{1,0:T(8,128)(2,1)}, u32[]{:S(2)}) copy-start(bf16[432,512]{1,0:T(8,128)(2,1)} %param.26) | copy-start | bytes 1327108
  459.9 12.8 %copy-start.22 = (f32[512]{0:T(512)S(1)}, f32[512]{0:T(512)}, u32[]{:S(2)}) copy-start(f32[512]{0:T(512)} %param.27) | copy-start | bytes 6148
  (23 other events, 121.6 us)
where the time goes:
time: 545 us; the launch traced here: 538 us
  local copies, waits for them, and re-layouts  178 us (33%)
  matrix products  131 us (24%)
  waiting for transfers between devices  92.3 us (17%)
  starting transfers between devices  70 us (13%)
  other arithmetic  61.6 us (11%)
    dot_general x8, matrix products, attend(): jnp.einsum('hqk,khd->qhd', raised.astype(jnp.bfloat16), all_values, prefe...  87 us
    unnamed x89, local copies, waits for them, and re-layouts  72.1 us
    reduce_sum x8, other arithmetic, attend(): totals = jnp.sum(raised, axis=2)  32.7 us
    dot_general x8, matrix products, attend(): jnp.einsum('qhd,khd->hqk', query_block, all_keys, preferred_element_type=...  30.9 us
    while x32, local copies, waits for them, and re-layouts  30.1 us
    another operation x2, local copies, waits for them, and re-layouts, decode_tiles(): jnp.stack(columns, axis=4).reshape(count * LFR * side * side, 27 * LAT)  18.3 us
    all_to_all x1, waiting for transfers between devices, local(): lax.all_to_all(attended, 'ctx', split_axis=0, concat_axis=1, tiled=True)  13.7 us
    all_to_all x1, waiting for transfers between devices, local(): lax.all_to_all(sink_keys, 'ctx', split_axis=1, concat_axis=0, tiled=True)  12.9 us
  transfers between devices with their start and end apart: 10, of which 9 were waited for; matrix products, arithmetic and copies ran while one was open for 6% of the time, Pallas kernels for 0%

commit v1 on v0

v1 whole, which is shorter than its diff:
```python
import functools
import math

import jax
import jax.numpy as jnp
from jax import lax
from jax.experimental import pallas as pl
from jax.experimental.pallas import tpu as pltpu
from jax.sharding import PartitionSpec as P

HEADS = 32
HD = 128
TOK = 128
F32 = jnp.float32
BF16 = jnp.bfloat16
SCALE = math.log2(math.e) / math.sqrt(HD)
HEADS_STEP = 8
BQ = 512
BK = 2048


def params(mib, axes=1):
    return pltpu.CompilerParams(
        vmem_limit_bytes=mib << 20, dimension_semantics=("arbitrary",) * axes
    )


def pack_clip_kernel(q_ref, k_ref, v_ref, out_ref):
    for head in range(HEADS_STEP):
        lanes = slice(head * HD, (head + 1) * HD)
        out_ref[head, 0:TOK, :] = q_ref[:, lanes]
        out_ref[head, TOK : 2 * TOK, :] = k_ref[:, lanes]
        out_ref[head, 2 * TOK : 3 * TOK, :] = v_ref[:, lanes]


def pack_clip(q, k, v):
    spec = pl.BlockSpec((TOK, HEADS_STEP * HD), lambda i: (0, i))
    return pl.pallas_call(
        pack_clip_kernel,
        grid=(HEADS // HEADS_STEP,),
        in_specs=[spec] * 3,
        out_specs=pl.BlockSpec((HEADS_STEP, 3 * TOK, HD), lambda i: (i, 0, 0)),
        out_shape=jax.ShapeDtypeStruct((HEADS, 3 * TOK, HD), BF16),
        compiler_params=params(24),
        name="pack_clip",
    )(q, k, v)


def pack_window_kernel(pick_ref, k_ref, v_ref, out_ref):
    for head in range(HEADS_STEP):
        lanes = slice(head * HD, (head + 1) * HD)
        out_ref[head, 0:TOK, :] = k_ref[0, :, lanes]
        out_ref[head, TOK : 2 * TOK, :] = v_ref[0, :, lanes]


def pack_sink_kernel(pick_ref, k_ref, v_ref, out_ref):
    for head in range(HEADS_STEP):
        lanes = slice(head * HD, (head + 1) * HD)
        for tile in range(4):
            rows = slice(tile * 32, tile * 32 + 16)
            out_ref[head, tile * 16 : tile * 16 + 16, :] = k_ref[0, rows, lanes]
            out_ref[head, 64 + tile * 16 : 80 + tile * 16, :] = v_ref[0, rows, lanes]


def pack_cache(pick, keys, values, which):
    body = pack_window_kernel if which == 1 else pack_sink_kernel
    rows = 2 * TOK if which == 1 else TOK
    spec = pl.BlockSpec((1, TOK, HEADS_STEP * HD), lambda i, pick: (pick[which], 0, i))
    return pl.pallas_call(
        body,
        grid_spec=pltpu.PrefetchScalarGridSpec(
            num_scalar_prefetch=1,
            grid=(HEADS // HEADS_STEP,),
            in_specs=[spec] * 2,
            out_specs=pl.BlockSpec((HEADS_STEP, rows, HD), lambda i, pick: (i, 0, 0)),
        ),
        out_shape=jax.ShapeDtypeStruct((HEADS, rows, HD), BF16),
        compiler_params=params(24),
        name="pack_window" if which == 1 else "pack_sink",
    )(pick, keys, values)


def attend_block(q, k_ref, v_ref, top, acc):
    sources, rows = k_ref.shape[0], k_ref.shape[1]
    step = min(BK // rows, sources)
    count = sources // step
    width = step * rows
    ones = jnp.ones((width, HD), BF16)

    def score(j):
        k = k_ref[j * step : (j + 1) * step].reshape(width, HD)
        return lax.dot_general(q, k, (((1,), (1,)), ((), ())), preferred_element_type=F32)

    following = score(0)
    for j in range(count):
        scores = following
        if j + 1 < count:
            following = score(j + 1)
        high = jnp.max(scores, axis=1, keepdims=True)
        if top is not None:
            high = jnp.maximum(top, high)
        raised = jnp.exp2((scores - high) * SCALE).astype(BF16)
        v = v_ref[j * step : (j + 1) * step].reshape(width, HD)
        mixed = jnp.dot(raised, jnp.concatenate([v, ones], axis=1), preferred_element_type=F32)
        if top is None:
            acc = mixed
        else:
            acc = acc * jnp.exp2((top - high) * SCALE) + mixed
        top = high
    return top, acc


def attend_first_kernel(q_ref, k_ref, v_ref, top_ref, acc_ref):
    q = q_ref[...].reshape(BQ, HD)
    top, acc = attend_block(q, k_ref, v_ref, None, None)
    top_ref[...] = jnp.broadcast_to(top, (BQ, HD))
    acc_ref[...] = acc


def attend_next_kernel(q_ref, k_ref, v_ref, top_in_ref, acc_in_ref, top_ref, acc_ref):
    q = q_ref[...].reshape(BQ, HD)
    top, acc = attend_block(q, k_ref, v_ref, top_in_ref[:, :1], acc_in_ref[...])
    top_ref[...] = jnp.broadcast_to(top, (BQ, HD))
    acc_ref[...] = acc


def attend_last_kernel(
    q_ref, k_ref, v_ref, top_in_ref, acc_in_ref, weight_ref, gather_ref, out_ref, rows_ref
):
    q = q_ref[...].reshape(BQ, HD)
    _, acc = attend_block(q, k_ref, v_ref, top_in_ref[:, :1], acc_in_ref[...])
    rows_ref[...] = acc[:, :HD] / acc[:, HD:]
    parts = [rows_ref[pl.ds(px, BQ // 4, stride=4), :].astype(BF16) for px in range(4)]
    attended = jnp.concatenate(parts, axis=1)
    moved = jnp.dot(attended, weight_ref[...], preferred_element_type=F32).astype(BF16)
    wide = attended.astype(F32)
    squares = jnp.dot((wide * wide).astype(BF16), gather_ref[...], preferred_element_type=F32)
    dests = BQ // TOK
    out_ref[:, 0:32, :] = moved[:, :HD].reshape(dests, 32, HD)
    out_ref[:, 32:64, :] = moved[:, HD:].reshape(dests, 32, HD)
    out_ref[:, 64:96, :] = squares.astype(BF16).reshape(dests, 32, HD)


def attend(kind, first, keys_values, k_rows, k_place, state=(), extra=()):
    sources = HEADS
    total = sources * TOK
    blocks = BQ // TOK
    q_spec = pl.BlockSpec((blocks, TOK, HD), lambda i: (i, 0, 0))
    k_spec = pl.BlockSpec((sources, k_rows, HD), lambda i: (0, k_place, 0))
    v_spec = pl.BlockSpec((sources, k_rows, HD), lambda i: (0, k_place + 1, 0))
    state_specs = [
        pl.BlockSpec((BQ, HD), lambda i: (i, 0)),
        pl.BlockSpec((BQ, 2 * HD), lambda i: (i, 0)),
    ]
    state_shapes = [
        jax.ShapeDtypeStruct((total, HD), F32),
        jax.ShapeDtypeStruct((total, 2 * HD), F32),
    ]
    in_specs = [q_spec, k_spec, v_spec] + (state_specs if state else [])
    scratch = []
    if kind == "last":
        body = attend_last_kernel
        in_specs += [pl.BlockSpec(x.shape, lambda i: (0, 0)) for x in extra]
        out_specs = pl.BlockSpec((blocks, 96, HD), lambda i: (i, 0, 0))
        out_shape = jax.ShapeDtypeStruct((sources, 96, HD), BF16)
        scratch = [pltpu.VMEM((BQ, HD), F32)]
    else:
        body = attend_next_kernel if state else attend_first_kernel
        out_specs, out_shape = state_specs, state_shapes
    keys = sources * k_rows
    return pl.pallas_call(
        body,
        grid=(total // BQ,),
        in_specs=in_specs,
        out_specs=out_specs,
        out_shape=out_shape,
        scratch_shapes=scratch,
        compiler_params=params(48),
        cost_estimate=pl.CostEstimate(
            flops=8 * total * keys * HD,
            transcendentals=total * keys,
            bytes_accessed=8 << 20,
        ),
        name="attend_" + kind,
    )(first, keys_values, keys_values, *state, *extra)


def clean_kernel(owner_ref, parts_ref, noisy_ref, prev_ref, out_ref):
    width = HEADS * HD
    sums = jnp.sum(parts_ref[...].astype(F32), axis=0)
    scale = 1.0 / jnp.sqrt(sums[64:96] * (1.0 / width) + 1e-06)
    noisy = noisy_ref[...].astype(F32)
    prev = prev_ref[...].astype(F32)
    clean = [noisy[i * 32 : i * 32 + 32] - sums[i * 32 : i * 32 + 32] * scale for i in range(2)]
    owners = [owner_ref[t] for t in range(4)]
    ranks = []
    for t in range(4):
        rank = jnp.int32(0)
        for earlier in range(t):
            rank = rank + jnp.where(owners[earlier] == owners[t], 1, 0)
        ranks.append(rank)
    zero = jnp.zeros((8, HD), F32)
    for owner in range(4):
        rows = []
        for slot in range(2):
            picked = [zero] * 5
            for t in range(4):
                here = (owners[t] == owner) & (ranks[t] == slot)
                piece = slice(t * 8, t * 8 + 8)
                pieces = (
                    prev[0:32][piece],
                    prev[32:64][piece],
                    clean[0][piece],
                    clean[1][piece],
                    jnp.ones((8, HD), F32),
                )
                picked = [jnp.where(here, new, old) for new, old in zip(pieces, picked)]
            rows += picked
        out_ref[owner] = jnp.concatenate(rows, axis=0).astype(BF16)


def clean_and_place(owner, parts, noisy, prev):
    vmem = pl.BlockSpec(memory_space=pltpu.VMEM)
    return pl.pallas_call(
        clean_kernel,
        in_specs=[pl.BlockSpec(memory_space=pltpu.SMEM), vmem, vmem, vmem],
        out_specs=vmem,
        out_shape=jax.ShapeDtypeStruct((4, 80, HD), BF16),
        compiler_params=pltpu.CompilerParams(vmem_limit_bytes=16 << 20),
        name="clean_and_place",
    )(owner, parts, noisy, prev)


def shift_rows(x, by):
    moved = pltpu.roll(x, by % 8, axis=1)
    y = lax.broadcasted_iota(jnp.int32, x.shape, 1)
    return jnp.where((y >= by) if by > 0 else (y < 8 + by), moved, 0.0)


def decode_kernel(
    in_ref, w_in_ref, b_in_ref, w_out_ref, b_out_ref, out_ref, latent_ref, part_ref, wide_ref
):
    tiles = 8
    flags = []
    for tile in range(tiles):
        block = in_ref[tile // 2, (tile % 2) * 40 : (tile % 2) * 40 + 40, :].astype(F32)
        for frames in range(2):
            for i in range(2):
                at = frames * 16 + i * 8
                latent_ref[pl.ds(tile * 32 + frames * 16 + i, 8, stride=2), :] = block[at : at + 8]
        flags.append(block[32:33])
    latent = latent_ref[...].reshape(tiles * 4, 8, HD)
    by_row = [shift_rows(latent, 1), latent, shift_rows(latent, -1)]
    by_row = [x.reshape(tiles * 32, HD) for x in by_row]
    lane = lax.broadcasted_iota(jnp.int32, (tiles * 32, HD), 1)
    low = lane < 64
    hidden = []
    for x in range(8):
        turn = (16 - 16 * x) % HD
        pair = [
            pltpu.roll(by_row[0], turn, axis=1) if turn else by_row[0],
            pltpu.roll(by_row[1], (turn + 64) % HD, axis=1) if turn != 64 else by_row[1],
            pltpu.roll(by_row[2], turn, axis=1) if turn else by_row[2],
        ]
        left = jnp.where(low, pair[0], pair[1])
        right = jnp.where(low, pair[2], 0.0)
        if x == 0:
            keep = (lane & 63) >= 16
            left, right = jnp.where(keep, left, 0.0), jnp.where(keep, right, 0.0)
        if x == 7:
            keep = (lane & 63) < 32
            left, right = jnp.where(keep, left, 0.0), jnp.where(keep, right, 0.0)
        taps = jnp.concatenate([left, right], axis=1).reshape(tiles, 4, 8, 2 * HD)
        columns = jnp.concatenate(
            [taps[:, dt : dt + 2].reshape(TOK, 2 * HD).astype(BF16) for dt in range(3)], axis=1
        )
        mid = jnp.dot(columns, w_in_ref[...], preferred_element_type=F32) + b_in_ref[...]
        hidden.append(mid / (1.0 + jnp.exp(-mid)))
    bias = b_out_ref[...]
    for a in range(2):
        for x in range(8):
            here = hidden[x]
            grouped = here.reshape(16, 8, 512)
            other = shift_rows(grouped, 1 if a == 0 else -1).reshape(TOK, 512)
            pair = [other, here] if a == 0 else [here, other]
            rows = jnp.concatenate([p.astype(BF16) for p in pair], axis=1)
            part_ref[x * TOK : (x + 1) * TOK, :] = jnp.dot(
                rows, w_out_ref[a], preferred_element_type=F32
            )
        for x in range(8):
            at = x * TOK
            first = part_ref[at : at + TOK, 128:256] + bias
            if x > 0:
                first = first + part_ref[at - TOK : at, 0:128]
            second = part_ref[at : at + TOK, 256:384] + bias
            if x < 7:
                second = second + part_ref[at + TOK : at + 2 * TOK, 384:512]
            wide_ref[pl.ds(a * 16 + 2 * x, TOK, stride=32), :] = first
            wide_ref[pl.ds(a * 16 + 2 * x + 1, TOK, stride=32), :] = second
    for tile in range(tiles):
        rows = slice(tile * 512, tile * 512 + 512)
        out_ref[rows, :] = jnp.where(flags[tile] > 0.5, wide_ref[rows, :], 0.0).astype(BF16)


def decode(arrived, w_in, b_in, w_out, b_out):
    vmem = pl.BlockSpec(memory_space=pltpu.VMEM)
    return pl.pallas_call(
        decode_kernel,
        in_specs=[vmem] * 5,
        out_specs=vmem,
        out_shape=jax.ShapeDtypeStruct((8 * 512, HD), BF16),
        scratch_shapes=[
            pltpu.VMEM((256, HD), F32),
            pltpu.VMEM((8 * TOK, 512), F32),
            pltpu.VMEM((8 * 512, HD), F32),
        ],
        compiler_params=pltpu.CompilerParams(vmem_limit_bytes=48 << 20),
        name="decode",
    )(arrived, w_in, b_in, w_out, b_out)


def place_velocity_weight(velocity_weight):
    head = lax.axis_index("ctx")
    mine = lax.dynamic_slice_in_dim(velocity_weight, head * HD, HD, 0).reshape(HD, 2, 32)
    same = jnp.eye(4, dtype=BF16)
    placed = mine[None, :, :, None, :] * same[:, None, None, :, None]
    gather = jnp.broadcast_to(same[:, None, :, None], (4, HD, 4, 32))
    return placed.reshape(4 * HD, 2 * HD), gather.reshape(4 * HD, HD)


def place_in_weight(weight):
    split = weight.reshape(3, 3, 48, 512)
    return jnp.pad(split, ((0, 0), (0, 1), (0, 16), (0, 0))).reshape(3 * 4 * 64, 512)


def place_out_weight(weight):
    w = weight.reshape(3, 3, 512, 128).astype(F32)
    rows = [[w[0], w[1] + w[2]], [w[0] + w[1], w[2]]]
    phases = []
    for a in range(2):
        halves = []
        for r in rows[a]:
            halves.append(jnp.concatenate([r[0], r[1] + r[2], r[0] + r[1], r[2]], axis=1))
        phases.append(jnp.concatenate(halves, axis=0))
    return jnp.stack(phases).astype(BF16)


def latent_rows(latent):
    return latent.reshape(4, 2, 4, 2, HD).transpose(3, 0, 1, 2, 4).reshape(64, HD)


def exchange(x, axis):
    return lax.all_to_all(x, axis, split_axis=0, concat_axis=0, tiled=True)


def local(
    clip_queries,
    clip_keys,
    clip_values,
    cache_keys,
    cache_values,
    clip_pick,
    noisy_latent,
    prev_latent,
    velocity_weight,
    tile_owner,
    conv_in_weight,
    conv_in_bias,
    conv_out_weight,
    conv_out_bias,
):
    pick = clip_pick[0]
    clip = exchange(pack_clip(clip_queries[0], clip_keys[0], clip_values[0]), "ctx")
    window = pack_cache(pick, cache_keys[0], cache_values[0], 1)
    sink = pack_cache(pick, cache_keys[0], cache_values[0], 0)
    weight, gather = place_velocity_weight(velocity_weight)
    w_in = place_in_weight(conv_in_weight)
    w_out = place_out_weight(conv_out_weight)
    noisy = latent_rows(noisy_latent[0])
    prev = latent_rows(prev_latent[0])

    clip, window, sink, weight, gather, w_in, w_out, noisy, prev = lax.optimization_barrier(
        (clip, window, sink, weight, gather, w_in, w_out, noisy, prev)
    )
    window = exchange(window, "ctx")
    state = attend("first", clip, clip, TOK, 1)
    window, sink = lax.optimization_barrier((window, sink))
    sink = exchange(sink, "ctx")
    state = attend("next", clip, window, TOK, 0, state)
    parts = attend("last", clip, sink, TOK // 2, 0, state, (weight, gather))
    parts = exchange(parts, "ctx")
    outgoing = clean_and_place(tile_owner[0], parts, noisy, prev)
    arrived = exchange(outgoing, "grp")
    decoded = decode(
        arrived, w_in, conv_in_bias.reshape(1, -1), w_out, conv_out_bias.reshape(1, -1)
    )
    return decoded.reshape(1, 1, 4, 2, 2, 256, 128)


def solution(mesh):
    in_specs = (
        P("grp", "ctx", None),
        P("grp", "ctx", None),
        P("grp", "ctx", None),
        P("grp", None, "ctx", None),
        P("grp", None, "ctx", None),
        P("grp", None),
        P("grp", "ctx", None, None),
        P("grp", "ctx", None, None),
        P(),
        P("grp", "ctx"),
        P(),
        P(),
        P(),
        P(),
    )
    out_specs = P("grp", "ctx", None, None, None, None, None)
    return jax.shard_map(local, mesh=mesh, in_specs=in_specs, out_specs=out_specs, check_vma=False)
```

time: 545 us -> 194 us (0.36); the launches traced: 538 us -> 193 us
  local copies, waits for them, and re-layouts: 178 us -> 22.7 us
  matrix products: 131 us -> 0 us
  Pallas kernels: 0 us -> 84.8 us
  waiting for transfers between devices: 92.3 us -> 25.3 us
  other arithmetic: 61.6 us -> 3.85 us
  starting transfers between devices: 70 us -> 25.3 us
  blocking collectives: 0 us -> 31.2 us
    dot_general x28 -> x0, matrix products: 131 us -> none  [the longest x8 87 us: attend(): jnp.einsum('hqk,khd->qhd', raised.astype(jnp.bfloat16), all_values, prefe...]
    pallas_call x0 -> x8, Pallas kernels: none -> 84.8 us  [the longest x3 75.1 us: attend(): pl.pallas_call(body, grid=(total // BQ,), in_specs=in_specs, out_specs=ou...]
    all_to_all x10 -> x3, waiting for transfers between devices: 92.3 us -> 25.3 us  [exchange(): return lax.all_to_all(x, axis, split_axis=0, concat_axis=0, tiled=True)]
    unnamed x89 -> x46, local copies, waits for them, and re-layouts: 72.1 us -> 18.9 us
    all_to_all x10 -> x3, starting transfers between devices: 70 us -> 25.3 us  [exchange(): return lax.all_to_all(x, axis, split_axis=0, concat_axis=0, tiled=True)]
    reduce_sum x11 -> x0, other arithmetic: 33.3 us -> none  [the longest x8 32.7 us: attend(): totals = jnp.sum(raised, axis=2)]
    all_to_all x0 -> x2, blocking collectives: none -> 31.2 us  [exchange(): return lax.all_to_all(x, axis, split_axis=0, concat_axis=0, tiled=True)]
    while x32 -> x0, local copies, waits for them, and re-layouts: 30.1 us -> none
  transfers between devices with their start and end apart: 10 -> 3, of which waited for: 9 -> 2; matrix products, arithmetic and copies ran while one was open for 6% -> 5% of each run, Pallas kernels for 0% -> 26%
where the time goes in v1:
time: 194 us; the launch traced here: 193 us
  Pallas kernels  84.8 us (44%)
  blocking collectives  31.2 us (16%)
  starting transfers between devices  25.3 us (13%)
  waiting for transfers between devices  25.3 us (13%)
  local copies, waits for them, and re-layouts  22.7 us (12%)
  other arithmetic  3.85 us (2%)
    pallas_call x3, Pallas kernels, attend(): pl.pallas_call(body, grid=(total // BQ,), in_specs=in_specs, out_specs=ou...  75.1 us
    all_to_all x2, blocking collectives, exchange(): return lax.all_to_all(x, axis, split_axis=0, concat_axis=0, tiled=True)  31.2 us
    all_to_all x3, starting transfers between devices, exchange(): return lax.all_to_all(x, axis, split_axis=0, concat_axis=0, tiled=True)  25.3 us
    all_to_all x3, waiting for transfers between devices, exchange(): return lax.all_to_all(x, axis, split_axis=0, concat_axis=0, tiled=True)  25.3 us
    unnamed x46, local copies, waits for them, and re-layouts  18.9 us
    pallas_call x1, Pallas kernels, decode(): pl.pallas_call(decode_kernel, in_specs=[vmem] * 5, out_specs=vmem, out_sh...  5.93 us
  transfers between devices with their start and end apart: 3, of which 2 were waited for; matrix products, arithmetic and copies ran while one was open for 5% of the time, Pallas kernels for 26%

profile of v1, /device:TPU:1, one launch (start us, length us, event | category | flops | bytes accessed | tf_op | source)
XLA Modules:
  0.0 193.5 jit_solution(13494225086302777512)
XLA Ops:
  0.0 1.3 copy-done.6
  1.3 1.2 copy-done.7
  2.5 1.2 copy-done.8
  4.6 1.6 copy-done.3
  6.3 10.0 %all-to-all-start = ((bf16[32,384,128]{2,1,0:T(8,128)(2,1)}), bf16[32,384,128]{2,1,0:T(8,128)(2,1)}, u32[]{:S(2)}, u32[]{:S(2)}) async-start(bf16[32,384,128]{2,1,0:T(8,128)(2,1)} %copy-done.3), calls=%async_computation | async-start | bytes 6291456 | tf_op jit(solution)/shard_map/all_to_all | solution.py:353
  16.3 2.2 %copy-done.1 = bf16[1,4,128,4096]{3,2,1,0:T(8,128)(2,1)S(1)} copy-done((bf16[1,4,128,4096]{3,2,1,0:T(8,128)(2,1)S(1)}, bf16[1,4,128,4096]{3,2,1,0:T(8,128)(2,1)}, u32[]{:S(2)}) %copy-start.1) | copy-done | bytes 4194328
  18.4 2.2 %copy-done.2 = bf16[1,4,128,4096]{3,2,1,0:T(8,128)(2,1)S(1)} copy-done((bf16[1,4,128,4096]{3,2,1,0:T(8,128)(2,1)S(1)}, bf16[1,4,128,4096]{3,2,1,0:T(8,128)(2,1)}, u32[]{:S(2)}) %copy-start.2) | copy-done | bytes 4194328
  22.6 1.2 pack_window.1
  23.8 1.4 copy-done.4
  28.6 3.0 %maximum_bitcast_fusion = (bf16[1,1024,512]{2,1,0:T(8,128)(2,1)S(1)}, bf16[1,1024,512]{2,1,0:T(8,128)(2,1)S(1)}) fusion(bf16[512,128]{1,0:T(8,128)(2,1)S(1)} %get-tuple-element.46, bf16[512,128]{1,0:T(8,128)(2,1)S(1)} %get-tuple-element.48, bf16[512,128]{1,0:T(8,128)(2,1)S(1)} %get-tuple-element.47, bf16[512,128]{1,0:T(8,128)(2,1)S(1)} %get-tuple-element.45, ...), kind=kLoop, calls=%fused_computation.1 | loop fusion | flops 16777216 | bytes 4194304 | tf_op jit(solution)/shard_map/stack | solution.py:345
  31.8 24.8 %all-to-all-done.q_ref.k_ref.v_ref = bf16[32,384,128]{2,1,0:T(8,128)(2,1)} async-done(((bf16[32,384,128]{2,1,0:T(8,128)(2,1)}), bf16[32,384,128]{2,1,0:T(8,128)(2,1)}, u32[]{:S(2)}, u32[]{:S(2)}) %all-to-all-start) | async-done | bytes 3145760 | tf_op jit(solution)/shard_map/all_to_all | solution.py:353
  56.6 7.8 %all-to-all-start.1 = ((bf16[32,256,128]{2,1,0:T(8,128)(2,1)}), bf16[32,256,128]{2,1,0:T(8,128)(2,1)}, u32[]{:S(2)}, u32[]{:S(2)}) async-start(bf16[32,256,128]{2,1,0:T(8,128)(2,1)} %copy-done.4), calls=%async_computation.1 | async-start | bytes 4194304 | tf_op jit(solution)/shard_map/all_to_all | solution.py:353
  64.4 1.0 copy.20.gather_ref
  65.5 1.8 copy.19.weight_ref
  67.2 22.3 %attend_first.1 = (f32[4096,128]{1,0:T(8,128)S(1)}, f32[4096,256]{1,0:T(8,128)}) custom-call(bf16[32,384,128]{2,1,0:T(8,128)(2,1)} %all-to-all-done.q_ref.k_ref.v_ref, bf16[32,384,128]{2,1,0:T(8,128)(2,1)} %all-to-all-done.q_ref.k_ref.v_ref, bf16[32,384,128]{2,1,0:T(8,128)(2,1)} %all-to-all-done.q_ref.k_ref.v_ref), custom_call_target="tpu_custom_call" | custom-call | flops 17179869184 | bytes 8388608 | tf_op jit(solution)/shard_map/attend_first/pallas_call | solution.py:171
  89.5 1.3 copy-done.17
  91.3 7.5 %all-to-all-start.2 = ((bf16[32,128,128]{2,1,0:T(8,128)(2,1)}), bf16[32,128,128]{2,1,0:T(8,128)(2,1)}, u32[]{:S(2)}, u32[]{:S(2)}) async-start(bf16[32,128,128]{2,1,0:T(8,128)(2,1)} %copy-done.5), calls=%async_computation.2 | async-start | bytes 2097152 | tf_op jit(solution)/shard_map/all_to_all | solution.py:353
  98.8 26.8 %attend_next.1 = (f32[4096,128]{1,0:T(8,128)S(1)}, f32[4096,256]{1,0:T(8,128)}) custom-call(bf16[32,384,128]{2,1,0:T(8,128)(2,1)} %all-to-all-done.q_ref.k_ref.v_ref, bf16[32,256,128]{2,1,0:T(8,128)(2,1)} %all-to-all-done.1.k_ref.v_ref, bf16[32,256,128]{2,1,0:T(8,128)(2,1)} %all-to-all-done.1.k_ref.v_ref, f32[4096,128]{1,0:T(8,128)} %copy-done.17, ...), custom_call_target="tpu_custom_call" | custom-call | flops 17179869184 | bytes 8388608 | tf_op jit(solution)/shard_map/attend_next/pallas_call | solution.py:171
  125.6 1.4 copy-done.15
  127.9 1.6 copy-done.16
  129.5 26.1 %attend_last.1 = bf16[32,96,128]{2,1,0:T(8,128)(2,1)S(1)} custom-call(bf16[32,384,128]{2,1,0:T(8,128)(2,1)} %all-to-all-done.q_ref.k_ref.v_ref, bf16[32,128,128]{2,1,0:T(8,128)(2,1)} %all-to-all-done.2.k_ref.v_ref, bf16[32,128,128]{2,1,0:T(8,128)(2,1)} %all-to-all-done.2.k_ref.v_ref, f32[4096,128]{1,0:T(8,128)S(1)} %copy-done.16, ...), custom_call_target="tpu_custom_call" | custom-call | flops 8589934592 | bytes 8388608 | tf_op jit(solution)/shard_map/attend_last/pallas_call | solution.py:171
  155.6 18.7 %all_to_all.25.parts_ref = bf16[32,96,128]{2,1,0:T(8,128)(2,1)S(1)} all-to-all(bf16[32,96,128]{2,1,0:T(8,128)(2,1)S(1)} %attend_last.1), channel_id=1, replica_groups=mesh['grp'=4,'ctx'=32] {'ctx'}, dimensions={0} | all-to-all | bytes 1572864 | tf_op jit(solution)/shard_map/all_to_all | solution.py:353
  175.0 12.5 %all_to_all.26.in_ref = bf16[4,80,128]{2,1,0:T(8,128)(2,1)S(1)} all-to-all(bf16[4,80,128]{2,1,0:T(8,128)(2,1)S(1)} %clean_and_place.1), channel_id=1, replica_groups=mesh['grp'=4,'ctx'=32] {'grp'}, dimensions={0} | all-to-all | bytes 163840 | tf_op jit(solution)/shard_map/all_to_all | solution.py:353
  187.5 5.9 %decode.1 = bf16[4096,128]{1,0:T(8,128)(2,1)} custom-call(bf16[4,80,128]{2,1,0:T(8,128)(2,1)S(1)} %all_to_all.26.in_ref, bf16[768,512]{1,0:T(8,128)(2,1)S(1)} %bitcast.78, f32[1,512]{1,0:T(1,128)S(1)} %bitcast.84, bf16[2,1024,512]{2,1,0:T(8,128)(2,1)S(1)} %pad_maximum_fusion.w_out_ref, f32[1,128]{1,0:T(1,128)S(1)} %bitcast.88), custom_call_target="tpu_custom_call" | custom-call | tf_op jit(solution)/shard_map/decode/pallas_call | solution.py:307
  (59 shorter events, 8.4 us)
Async XLA Ops:
  0.0 26.7 %copy-start = (bf16[4096,64]{0,1:T(8,128)(2,1)S(1)}, bf16[4096,64]{0,1:T(8,128)(2,1)}, u32[]{:S(2)}) copy-start(bf16[4096,64]{0,1:T(8,128)(2,1)} %param.22) | copy-start | bytes 1572868
  0.0 1.3 copy-start.6
  1.3 1.2 copy-start.7
  2.5 1.2 copy-start.8
  4.6 1.6 copy-start.3
  6.2 10.0 %copy-start.12 = (s32[1,2]{1,0:T(1,128)S(1)}, s32[1,2]{1,0:T(1,128)}, u32[]{:S(2)}) copy-start(s32[1,2]{1,0:T(1,128)} %param.19) | copy-start | bytes 28
  6.3 50.3 %all-to-all-start = ((bf16[32,384,128]{2,1,0:T(8,128)(2,1)}), bf16[32,384,128]{2,1,0:T(8,128)(2,1)}, u32[]{:S(2)}, u32[]{:S(2)}) async-start(bf16[32,384,128]{2,1,0:T(8,128)(2,1)} %copy-done.3), calls=%async_computation | async-start | bytes 6291456 | tf_op jit(solution)/shard_map/all_to_all | solution.py:353
  16.2 2.2 %copy-start.1 = (bf16[1,4,128,4096]{3,2,1,0:T(8,128)(2,1)S(1)}, bf16[1,4,128,4096]{3,2,1,0:T(8,128)(2,1)}, u32[]{:S(2)}) copy-start(bf16[1,4,128,4096]{3,2,1,0:T(8,128)(2,1)} %param.17) | copy-start | bytes 12582916
  18.4 2.2 %copy-start.2 = (bf16[1,4,128,4096]{3,2,1,0:T(8,128)(2,1)S(1)}, bf16[1,4,128,4096]{3,2,1,0:T(8,128)(2,1)}, u32[]{:S(2)}) copy-start(bf16[1,4,128,4096]{3,2,1,0:T(8,128)(2,1)} %param.18) | copy-start | bytes 12582916
  21.6 1.0 copy-start.5
  22.6 2.6 %copy-start.20 = (bf16[1,4,2,1024]{3,2,1,0:T(2,128)(2,1)S(1)}, bf16[1,4,2,1024]{3,2,1,0:T(2,128)(2,1)}, u32[]{:S(2)}) copy-start(bf16[1,4,2,1024]{3,2,1,0:T(2,128)(2,1)} %param.20) | copy-start | bytes 49156
  22.6 2.6 %copy-start.21 = (bf16[1,4,2,1024]{3,2,1,0:T(2,128)(2,1)S(1)}, bf16[1,4,2,1024]{3,2,1,0:T(2,128)(2,1)}, u32[]{:S(2)}) copy-start(bf16[1,4,2,1024]{3,2,1,0:T(2,128)(2,1)} %param.21) | copy-start | bytes 49156
  23.8 1.4 copy-start.4
  25.2 2.4 %copy-start.18 = (bf16[9,512,128]{2,1,0:T(8,128)(2,1)S(1)}, bf16[9,512,128]{2,1,0:T(8,128)(2,1)}, u32[]{:S(2)}) copy-start(bf16[9,512,128]{2,1,0:T(8,128)(2,1)} %param.26) | copy-start | bytes 3538948
  26.9 1.1 copy-start.19
  56.6 34.7 %all-to-all-start.1 = ((bf16[32,256,128]{2,1,0:T(8,128)(2,1)}), bf16[32,256,128]{2,1,0:T(8,128)(2,1)}, u32[]{:S(2)}, u32[]{:S(2)}) async-start(bf16[32,256,128]{2,1,0:T(8,128)(2,1)} %copy-done.4), calls=%async_computation.1 | async-start | bytes 4194304 | tf_op jit(solution)/shard_map/all_to_all | solution.py:353
  89.5 1.3 copy-start.17
  91.3 35.7 %all-to-all-start.2 = ((bf16[32,128,128]{2,1,0:T(8,128)(2,1)}), bf16[32,128,128]{2,1,0:T(8,128)(2,1)}, u32[]{:S(2)}, u32[]{:S(2)}) async-start(bf16[32,128,128]{2,1,0:T(8,128)(2,1)} %copy-done.5), calls=%async_computation.2 | async-start | bytes 2097152 | tf_op jit(solution)/shard_map/all_to_all | solution.py:353
  125.6 1.4 copy-start.15
  127.9 1.6 copy-start.16
  129.5 44.8 %copy-start.10 = (bf16[4,2,4,2,128]{4,2,1,0,3:T(4,128)(2,1)S(1)}, bf16[4,2,4,2,128]{4,2,1,0,3:T(4,128)(2,1)}, u32[]{:S(2)}) copy-start(bf16[4,2,4,2,128]{4,2,1,0,3:T(4,128)(2,1)} %copy.18) | copy-start | bytes 49156
  129.5 44.8 %copy-start.13 = (s32[1,4]{1,0:T(1,128)S(1)}, s32[1,4]{1,0:T(1,128)}, u32[]{:S(2)}) copy-start(s32[1,4]{1,0:T(1,128)} %param.23) | copy-start | bytes 52
  155.6 32.0 %copy-start.11 = (f32[512]{0:T(512)S(1)}, f32[512]{0:T(512)}, u32[]{:S(2)}) copy-start(f32[512]{0:T(512)} %param.25) | copy-start | bytes 6148
  155.6 32.0 %copy-start.14 = (f32[128]{0:T(128)S(1)}, f32[128]{0:T(128)}, u32[]{:S(2)}) copy-start(f32[128]{0:T(128)} %param.27) | copy-start | bytes 1540
  (1 other events, 1.0 us)

commit v2 on v1

--- a/solution.py
+++ b/solution.py
@@ -1,4 +1,3 @@
-import functools
 import math
 
 import jax
@@ -15,8 +14,8 @@
 BF16 = jnp.bfloat16
 SCALE = math.log2(math.e) / math.sqrt(HD)
 HEADS_STEP = 8
-BQ = 512
-BK = 2048
+BQ = 1024
+LIMIT = 110.0
 
 
 def params(mib, axes=1):
@@ -25,25 +24,17 @@
     )
 
 
-def pack_clip_kernel(q_ref, k_ref, v_ref, out_ref):
+def pack_first_kernel(pick_ref, q_ref, k_ref, v_ref, sink_k_ref, sink_v_ref, out_ref):
     for head in range(HEADS_STEP):
         lanes = slice(head * HD, (head + 1) * HD)
-        out_ref[head, 0:TOK, :] = q_ref[:, lanes]
-        out_ref[head, TOK : 2 * TOK, :] = k_ref[:, lanes]
-        out_ref[head, 2 * TOK : 3 * TOK, :] = v_ref[:, lanes]
-
-
-def pack_clip(q, k, v):
-    spec = pl.BlockSpec((TOK, HEADS_STEP * HD), lambda i: (0, i))
-    return pl.pallas_call(
-        pack_clip_kernel,
-        grid=(HEADS // HEADS_STEP,),
-        in_specs=[spec] * 3,
-        out_specs=pl.BlockSpec((HEADS_STEP, 3 * TOK, HD), lambda i: (i, 0, 0)),
-        out_shape=jax.ShapeDtypeStruct((HEADS, 3 * TOK, HD), BF16),
-        compiler_params=params(24),
-        name="pack_clip",
-    )(q, k, v)
+        out_ref[head, 0:TOK, :] = k_ref[:, lanes]
+        out_ref[head, 192 : 192 + TOK, :] = v_ref[:, lanes]
+        out_ref[head, 384 : 384 + TOK, :] = q_ref[:, lanes]
+        for tile in range(4):
+            rows = slice(tile * 32, tile * 32 + 16)
+            at = TOK + tile * 16
+            out_ref[head, at : at + 16, :] = sink_k_ref[0, rows, lanes]
+            out_ref[head, 192 + at : 208 + at, :] = sink_v_ref[0, rows, lanes]
 
 
 def pack_window_kernel(pick_ref, k_ref, v_ref, out_ref):
@@ -53,145 +44,214 @@
         out_ref[head, TOK : 2 * TOK, :] = v_ref[0, :, lanes]
 
 
-def pack_sink_kernel(pick_ref, k_ref, v_ref, out_ref):
-    for head in range(HEADS_STEP):
-        lanes = slice(head * HD, (head + 1) * HD)
-        for tile in range(4):
-            rows = slice(tile * 32, tile * 32 + 16)
-            out_ref[head, tile * 16 : tile * 16 + 16, :] = k_ref[0, rows, lanes]
-            out_ref[head, 64 + tile * 16 : 80 + tile * 16, :] = v_ref[0, rows, lanes]
-
-
-def pack_cache(pick, keys, values, which):
-    body = pack_window_kernel if which == 1 else pack_sink_kernel
-    rows = 2 * TOK if which == 1 else TOK
-    spec = pl.BlockSpec((1, TOK, HEADS_STEP * HD), lambda i, pick: (pick[which], 0, i))
+def pack(pick, current, keys, values, which):
+    rows = 2 * TOK if which == 1 else 4 * TOK
+    own = pl.BlockSpec((TOK, HEADS_STEP * HD), lambda i, pick: (0, i))
+    cached = pl.BlockSpec((1, TOK, HEADS_STEP * HD), lambda i, pick: (pick[which], 0, i))
     return pl.pallas_call(
-        body,
+        pack_window_kernel if which == 1 else pack_first_kernel,
         grid_spec=pltpu.PrefetchScalarGridSpec(
             num_scalar_prefetch=1,
             grid=(HEADS // HEADS_STEP,),
-            in_specs=[spec] * 2,
+            in_specs=[own] * len(current) + [cached] * 2,
             out_specs=pl.BlockSpec((HEADS_STEP, rows, HD), lambda i, pick: (i, 0, 0)),
         ),
         out_shape=jax.ShapeDtypeStruct((HEADS, rows, HD), BF16),
-        compiler_params=params(24),
-        name="pack_window" if which == 1 else "pack_sink",
-    )(pick, keys, values)
-
-
-def attend_block(q, k_ref, v_ref, top, acc):
+        compiler_params=params(60),
+        name="pack_window" if which == 1 else "pack_first",
+    )(pick, *current, keys, values)
+
+
+def key_blocks(ref, step):
+    sources, rows = ref.shape[0], ref.shape[1]
+    return [
+        ref[j : j + step].reshape(step * rows, HD) for j in range(0, sources, step)
+    ]
+
+
+def score(k, q):
+    return lax.dot_general(k, q, (((1,), (1,)), ((), ())), preferred_element_type=F32)
+
+
+def mix(v, raised):
+    return lax.dot_general(
+        v, raised.astype(BF16), (((0,), (0,)), ((), ())), preferred_element_type=F32
+    )
+
+
+def fold_rows(x):
+    return jnp.sum(x.reshape(x.shape[0] // 8, 8, x.shape[1]), axis=0)
+
+
+def attend_bounded(q, k_ref, v_ref, step, totals_ref, acc_ref, add):
+    keys, values = key_blocks(k_ref, step), key_blocks(v_ref, step)
+    totals = totals_ref[...] if add else None
+    acc = acc_ref[...] if add else None
+    following = score(keys[0], q)
+    for j in range(len(keys)):
+        scores = following
+        if j + 1 < len(keys):
+            following = score(keys[j + 1], q)
+        raised = jnp.exp2(scores * SCALE)
+        mixed, total = mix(values[j], raised), fold_rows(raised)
+        acc = mixed if acc is None else acc + mixed
+        totals = total if totals is None else totals + total
+    totals_ref[...] = totals
+    acc_ref[...] = acc
+
+
+def attend_any(q, k_ref, v_ref, step, top_ref, totals_ref, acc_ref, add):
     sources, rows = k_ref.shape[0], k_ref.shape[1]
-    step = min(BK // rows, sources)
-    count = sources // step
-    width = step * rows
-    ones = jnp.ones((width, HD), BF16)
-
-    def score(j):
-        k = k_ref[j * step : (j + 1) * step].reshape(width, HD)
-        return lax.dot_general(q, k, (((1,), (1,)), ((), ())), preferred_element_type=F32)
-
-    following = score(0)
-    for j in range(count):
-        scores = following
-        if j + 1 < count:
-            following = score(j + 1)
-        high = jnp.max(scores, axis=1, keepdims=True)
-        if top is not None:
-            high = jnp.maximum(top, high)
-        raised = jnp.exp2((scores - high) * SCALE).astype(BF16)
-        v = v_ref[j * step : (j + 1) * step].reshape(width, HD)
-        mixed = jnp.dot(raised, jnp.concatenate([v, ones], axis=1), preferred_element_type=F32)
-        if top is None:
-            acc = mixed
-        else:
-            acc = acc * jnp.exp2((top - high) * SCALE) + mixed
-        top = high
-    return top, acc
-
-
-def attend_first_kernel(q_ref, k_ref, v_ref, top_ref, acc_ref):
+    if not add:
+        top_ref[...] = jnp.full(top_ref.shape, -1e30, F32)
+        totals_ref[...] = jnp.zeros(totals_ref.shape, F32)
+        acc_ref[...] = jnp.zeros(acc_ref.shape, F32)
+
+    def body(j, carry):
+        here = pl.ds(j * step, step)
+        scores = score(k_ref[here].reshape(step * rows, HD), q)
+        before = top_ref[0:1, :]
+        top = jnp.maximum(before, jnp.max(scores, axis=0, keepdims=True))
+        raised = jnp.exp2((scores - top) * SCALE)
+        fade = jnp.exp2((before - top) * SCALE)
+        mixed = mix(v_ref[here].reshape(step * rows, HD), raised)
+        acc_ref[...] = acc_ref[...] * fade + mixed
+        totals_ref[...] = totals_ref[...] * fade + fold_rows(raised)
+        top_ref[...] = jnp.broadcast_to(top, top_ref.shape)
+        return carry
+
+    lax.fori_loop(0, sources // step, body, 0)
+
+
+def bounded(q, k_ref, widest_ref):
+    @pl.when(pl.program_id(0) == 0)
+    def _():
+        widest = jnp.max(jnp.abs(k_ref[...].reshape(-1, HD)), axis=0, keepdims=True)
+        widest_ref[...] = jnp.broadcast_to(widest.astype(F32), widest_ref.shape)
+
+    widest = widest_ref[...].astype(BF16)
+    reach = lax.dot_general(
+        widest, jnp.abs(q), (((1,), (1,)), ((), ())), preferred_element_type=F32
+    )
+    return jnp.max(reach[0:8]) * (1.01 * SCALE) <= LIMIT
+
+
+def attend_first_kernel(q_ref, k_ref, v_ref, slow_ref, top_ref, totals_ref, acc_ref, widest_ref):
     q = q_ref[...].reshape(BQ, HD)
-    top, acc = attend_block(q, k_ref, v_ref, None, None)
-    top_ref[...] = jnp.broadcast_to(top, (BQ, HD))
-    acc_ref[...] = acc
-
-
-def attend_next_kernel(q_ref, k_ref, v_ref, top_in_ref, acc_in_ref, top_ref, acc_ref):
-    q = q_ref[...].reshape(BQ, HD)
-    top, acc = attend_block(q, k_ref, v_ref, top_in_ref[:, :1], acc_in_ref[...])
-    top_ref[...] = jnp.broadcast_to(top, (BQ, HD))
-    acc_ref[...] = acc
+    fits = bounded(q, k_ref, widest_ref)
+    slow_ref[pl.program_id(0)] = jnp.where(fits, 0, 1)
+
+    @pl.when(fits)
+    def _():
+        top_ref[...] = jnp.zeros(top_ref.shape, F32)
+        attend_bounded(q, k_ref, v_ref, 4, totals_ref, acc_ref, False)
+
+    @pl.when(jnp.logical_not(fits))
+    def _():
+        attend_any(q, k_ref, v_ref, 4, top_ref, totals_ref, acc_ref, False)
 
 
 def attend_last_kernel(
-    q_ref, k_ref, v_ref, top_in_ref, acc_in_ref, weight_ref, gather_ref, out_ref, rows_ref
+    q_ref, k_ref, v_ref, slow_ref, top_in_ref, totals_in_ref, acc_in_ref, weight_ref,
+    out_ref, top_ref, totals_ref, acc_ref, widest_ref,
 ):
     q = q_ref[...].reshape(BQ, HD)
-    _, acc = attend_block(q, k_ref, v_ref, top_in_ref[:, :1], acc_in_ref[...])
-    rows_ref[...] = acc[:, :HD] / acc[:, HD:]
-    parts = [rows_ref[pl.ds(px, BQ // 4, stride=4), :].astype(BF16) for px in range(4)]
-    attended = jnp.concatenate(parts, axis=1)
-    moved = jnp.dot(attended, weight_ref[...], preferred_element_type=F32).astype(BF16)
+    fits = bounded(q, k_ref, widest_ref) & (slow_ref[pl.program_id(0)] == 0)
+    totals_ref[...] = totals_in_ref[...]
+    acc_ref[...] = acc_in_ref[...]
+
+    @pl.when(fits)
+    def _():
+        attend_bounded(q, k_ref, v_ref, 8, totals_ref, acc_ref, True)
+
+    @pl.when(jnp.logical_not(fits))
+    def _():
+        top_ref[...] = top_in_ref[...]
+        attend_any(q, k_ref, v_ref, 8, top_ref, totals_ref, acc_ref, True)
+
+    totals = jnp.sum(totals_ref[...], axis=0, keepdims=True)
+    attended = (acc_ref[...] / totals).astype(BF16)
+    moved = lax.dot_general(
+        weight_ref[...], attended, (((0,), (0,)), ((), ())), preferred_element_type=F32
+    )
     wide = attended.astype(F32)
-    squares = jnp.dot((wide * wide).astype(BF16), gather_ref[...], preferred_element_type=F32)
-    dests = BQ // TOK
-    out_ref[:, 0:32, :] = moved[:, :HD].reshape(dests, 32, HD)
-    out_ref[:, 32:64, :] = moved[:, HD:].reshape(dests, 32, HD)
-    out_ref[:, 64:96, :] = squares.astype(BF16).reshape(dests, 32, HD)
-
-
-def attend(kind, first, keys_values, k_rows, k_place, state=(), extra=()):
-    sources = HEADS
-    total = sources * TOK
+    squares = jnp.broadcast_to(jnp.sum(wide * wide, axis=0, keepdims=True), (8, BQ))
+    block = jnp.concatenate([moved, squares], axis=0).astype(BF16)
+    for dest in range(BQ // TOK):
+        out_ref[dest] = block[:, dest * TOK : (dest + 1) * TOK]
+
+
+def attend(kind, queries, keys_values, k_rows, state=(), weight=None):
+    total = HEADS * TOK
     blocks = BQ // TOK
-    q_spec = pl.BlockSpec((blocks, TOK, HD), lambda i: (i, 0, 0))
-    k_spec = pl.BlockSpec((sources, k_rows, HD), lambda i: (0, k_place, 0))
-    v_spec = pl.BlockSpec((sources, k_rows, HD), lambda i: (0, k_place + 1, 0))
+    steps = total // BQ
+    q_spec = pl.BlockSpec((blocks, TOK, HD), lambda i: (i, 3, 0))
+    k_spec = pl.BlockSpec((HEADS, k_rows, HD), lambda i: (0, 0, 0))
+    v_spec = pl.BlockSpec((HEADS, k_rows, HD), lambda i: (0, 1, 0))
     state_specs = [
-        pl.BlockSpec((BQ, HD), lambda i: (i, 0)),
-        pl.BlockSpec((BQ, 2 * HD), lambda i: (i, 0)),
+        pl.BlockSpec(memory_space=pltpu.SMEM),
+        pl.BlockSpec((8, BQ), lambda i: (0, i)),
+        pl.BlockSpec((8, BQ), lambda i: (0, i)),
+        pl.BlockSpec((HD, BQ), lambda i: (0, i)),
     ]
     state_shapes = [
-        jax.ShapeDtypeStruct((total, HD), F32),
-        jax.ShapeDtypeStruct((total, 2 * HD), F32),
+        jax.ShapeDtypeStruct((steps,), jnp.int32),
+        jax.ShapeDtypeStruct((8, total), F32),
+        jax.ShapeDtypeStruct((8, total), F32),
+        jax.ShapeDtypeStruct((HD, total), F32),
     ]
-    in_specs = [q_spec, k_spec, v_spec] + (state_specs if state else [])
-    scratch = []
-    if kind == "last":
+    in_specs = [q_spec, k_spec, v_spec]
+    scratch = [pltpu.VMEM((16, HD), F32)]
+    args = (queries, keys_values, keys_values)
+    if kind == "first":
+        body, out_specs, out_shape = attend_first_kernel, state_specs, state_shapes
+    else:
         body = attend_last_kernel
-        in_specs += [pl.BlockSpec(x.shape, lambda i: (0, 0)) for x in extra]
-        out_specs = pl.BlockSpec((blocks, 96, HD), lambda i: (i, 0, 0))
-        out_shape = jax.ShapeDtypeStruct((sources, 96, HD), BF16)
-        scratch = [pltpu.VMEM((BQ, HD), F32)]
-    else:
-        body = attend_next_kernel if state else attend_first_kernel
-        out_specs, out_shape = state_specs, state_shapes
-    keys = sources * k_rows
+        in_specs += state_specs + [pl.BlockSpec(weight.shape, lambda i: (0, 0))]
+        args += (*state, weight)
+        out_specs = pl.BlockSpec((blocks, 72, HD), lambda i: (i, 0, 0))
+        out_shape = jax.ShapeDtypeStruct((HEADS, 72, HD), BF16)
+        scratch = [
+            pltpu.VMEM((8, BQ), F32),
+            pltpu.VMEM((8, BQ), F32),
+            pltpu.VMEM((HD, BQ), F32),
+        ] + scratch
+    keys = HEADS * k_rows
     return pl.pallas_call(
         body,
-        grid=(total // BQ,),
+        grid=(steps,),
         in_specs=in_specs,
         out_specs=out_specs,
         out_shape=out_shape,
         scratch_shapes=scratch,
         compiler_params=params(48),
         cost_estimate=pl.CostEstimate(
-            flops=8 * total * keys * HD,
+            flops=6 * total * keys * HD,
             transcendentals=total * keys,
             bytes_accessed=8 << 20,
         ),
         name="attend_" + kind,
-    )(first, keys_values, keys_values, *state, *extra)
-
-
-def clean_kernel(owner_ref, parts_ref, noisy_ref, prev_ref, out_ref):
+    )(*args)
+
+
+def clean_kernel(owner_ref, parts_ref, noisy_ref, prev_ref, out_ref, token_ref):
     width = HEADS * HD
     sums = jnp.sum(parts_ref[...].astype(F32), axis=0)
-    scale = 1.0 / jnp.sqrt(sums[64:96] * (1.0 / width) + 1e-06)
-    noisy = noisy_ref[...].astype(F32)
+    scale = 1.0 / jnp.sqrt(sums[64:65] * (1.0 / width) + 1e-06)
+    velocity = sums[0:64] * scale
+    velocity = jnp.concatenate([velocity, jnp.zeros((64, HD), F32)], axis=0)
+    token_ref[...] = jnp.transpose(velocity)
+    lane = lax.broadcasted_iota(jnp.int32, (32, HD), 1)
+    clean = []
+    by_px = [token_ref[pl.ds(px, 32, stride=4), :] for px in range(4)]
+    for i in range(2):
+        moved = jnp.zeros((32, HD), F32)
+        for px in range(4):
+            turn = (px - i) * 32 % HD
+            piece = pltpu.roll(by_px[px], turn, axis=1) if turn else by_px[px]
+            moved = jnp.where(lane // 32 == px, piece, moved)
+        clean.append(noisy_ref[i * 32 : i * 32 + 32, :].astype(F32) - moved)
     prev = prev_ref[...].astype(F32)
-    clean = [noisy[i * 32 : i * 32 + 32] - sums[i * 32 : i * 32 + 32] * scale for i in range(2)]
     owners = [owner_ref[t] for t in range(4)]
     ranks = []
     for t in range(4):
@@ -226,6 +286,7 @@
         in_specs=[pl.BlockSpec(memory_space=pltpu.SMEM), vmem, vmem, vmem],
         out_specs=vmem,
         out_shape=jax.ShapeDtypeStruct((4, 80, HD), BF16),
+        scratch_shapes=[pltpu.VMEM((HD, HD), F32)],
         compiler_params=pltpu.CompilerParams(vmem_limit_bytes=16 << 20),
         name="clean_and_place",
     )(owner, parts, noisy, prev)
@@ -319,13 +380,9 @@
     )(arrived, w_in, b_in, w_out, b_out)
 
 
-def place_velocity_weight(velocity_weight):
+def head_weight(velocity_weight):
     head = lax.axis_index("ctx")
-    mine = lax.dynamic_slice_in_dim(velocity_weight, head * HD, HD, 0).reshape(HD, 2, 32)
-    same = jnp.eye(4, dtype=BF16)
-    placed = mine[None, :, :, None, :] * same[:, None, None, :, None]
-    gather = jnp.broadcast_to(same[:, None, :, None], (4, HD, 4, 32))
-    return placed.reshape(4 * HD, 2 * HD), gather.reshape(4 * HD, HD)
+    return lax.dynamic_slice_in_dim(velocity_weight, head * HD, HD, 0)
 
 
 def place_in_weight(weight):
@@ -370,24 +427,21 @@
     conv_out_bias,
 ):
     pick = clip_pick[0]
-    clip = exchange(pack_clip(clip_queries[0], clip_keys[0], clip_values[0]), "ctx")
-    window = pack_cache(pick, cache_keys[0], cache_values[0], 1)
-    sink = pack_cache(pick, cache_keys[0], cache_values[0], 0)
-    weight, gather = place_velocity_weight(velocity_weight)
+    current = (clip_queries[0], clip_keys[0], clip_values[0])
+    clip = exchange(pack(pick, current, cache_keys[0], cache_values[0], 0), "ctx")
+    window = pack(pick, (), cache_keys[0], cache_values[0], 1)
+    weight = head_weight(velocity_weight)
     w_in = place_in_weight(conv_in_weight)
     w_out = place_out_weight(conv_out_weight)
     noisy = latent_rows(noisy_latent[0])
     prev = latent_rows(prev_latent[0])
 
-    clip, window, sink, weight, gather, w_in, w_out, noisy, prev = lax.optimization_barrier(
-        (clip, window, sink, weight, gather, w_in, w_out, noisy, prev)
+    clip, window, weight, w_in, w_out, noisy, prev = lax.optimization_barrier(
+        (clip, window, weight, w_in, w_out, noisy, prev)
     )
     window = exchange(window, "ctx")
-    state = attend("first", clip, clip, TOK, 1)
-    window, sink = lax.optimization_barrier((window, sink))
-    sink = exchange(sink, "ctx")
-    state = attend("next", clip, window, TOK, 0, state)
-    parts = attend("last", clip, sink, TOK // 2, 0, state, (weight, gather))
+    state = attend("first", clip, clip, 192)
+    parts = attend("last", clip, window, TOK, state, weight)
     parts = exchange(parts, "ctx")
     outgoing = clean_and_place(tile_owner[0], parts, noisy, prev)
     arrived = exchange(outgoing, "grp")

time: 194 us -> 205 us (1.057)
  Pallas kernels: 84.8 us -> 103 us
  waiting for transfers between devices: 25.3 us -> 41.7 us
  local copies, waits for them, and re-layouts: 22.7 us -> 7.97 us
  starting transfers between devices: 25.3 us -> 15.5 us
  other arithmetic: 3.85 us -> 6.77 us
    pallas_call x6 -> x4, Pallas kernels: 78.2 us -> 96.4 us  [the longest x2 85.7 us: attend(): pl.pallas_call(body, grid=(steps,), in_specs=in_specs, out_specs=out_spec...]
    all_to_all x3 -> x2, waiting for transfers between devices: 25.3 us -> 41.7 us  [exchange(): return lax.all_to_all(x, axis, split_axis=0, concat_axis=0, tiled=True)]
    unnamed x46 -> x30, local copies, waits for them, and re-layouts: 18.9 us -> 7.58 us
    all_to_all x3 -> x2, starting transfers between devices: 25.3 us -> 15.5 us  [exchange(): return lax.all_to_all(x, axis, split_axis=0, concat_axis=0, tiled=True)]
    optimization_barrier x2 -> x1, local copies, waits for them, and re-layouts: 2.8 us -> 0.11 us  [local(): lax.optimization_barrier((clip, window, weight, w_in, w_out, noisy, prev))]
  transfers between devices with their start and end apart: 3 -> 2, of which waited for: 2 -> 1; matrix products, arithmetic and copies ran while one was open for 5% -> 3% of each run, Pallas kernels for 26% -> 27%
where the time goes in v2:
time: 205 us
  Pallas kernels  103 us (50%)
  waiting for transfers between devices  41.7 us (20%)
  blocking collectives  29.4 us (14%)
  starting transfers between devices  15.5 us (8%)
  local copies, waits for them, and re-layouts  7.97 us (4%)
  other arithmetic  6.77 us (3%)
    pallas_call x2, Pallas kernels, attend(): pl.pallas_call(body, grid=(steps,), in_specs=in_specs, out_specs=out_spec...  85.7 us
    all_to_all x2, waiting for transfers between devices, exchange(): return lax.all_to_all(x, axis, split_axis=0, concat_axis=0, tiled=True)  41.7 us
    all_to_all x2, blocking collectives, exchange(): return lax.all_to_all(x, axis, split_axis=0, concat_axis=0, tiled=True)  29.4 us
    all_to_all x2, starting transfers between devices, exchange(): return lax.all_to_all(x, axis, split_axis=0, concat_axis=0, tiled=True)  15.5 us
    pallas_call x2, Pallas kernels, pack(): pl.pallas_call(pack_window_kernel if which == 1 else pack_first_kernel, g...  10.7 us
    unnamed x30, local copies, waits for them, and re-layouts  7.58 us
    pallas_call x1, Pallas kernels, decode(): pl.pallas_call(decode_kernel, in_specs=[vmem] * 5, out_specs=vmem, out_sh...  5.94 us
  transfers between devices with their start and end apart: 2, of which 1 were waited for; matrix products, arithmetic and copies ran while one was open for 3% of the time, Pallas kernels for 27%

profile of v2, /device:TPU:1, one launch (start us, length us, event | category | flops | bytes accessed | tf_op | source)
XLA Modules:
  0.0 204.7 jit_solution(5020381696101585078)
XLA Ops:
  0.0 6.0 %pack_first.1 = bf16[32,512,128]{2,1,0:T(8,128)(2,1)} custom-call(s32[2]{0:T(128)} %bitcast.75, bf16[128,4096]{1,0:T(8,128)(2,1)} %bitcast.71, bf16[128,4096]{1,0:T(8,128)(2,1)} %bitcast.72, bf16[128,4096]{1,0:T(8,128)(2,1)} %bitcast.73, bf16[4,128,4096]{2,1,0:T(8,128)(2,1)} %bitcast.67, bf16[4,128,4096]{2,1,0:T(8,128)(2,1)} %bitcast.69), custom_call_target="tpu_custom_call" | custom-call | tf_op jit(solution)/shard_map/pack_first/pallas_call | solution.py:51
  6.0 9.9 %all-to-all-start = ((bf16[32,512,128]{2,1,0:T(8,128)(2,1)}), bf16[32,512,128]{2,1,0:T(8,128)(2,1)}, u32[]{:S(2)}, u32[]{:S(2)}) async-start(bf16[32,512,128]{2,1,0:T(8,128)(2,1)} %pack_first.1), calls=%async_computation | async-start | bytes 8388608 | tf_op jit(solution)/shard_map/all_to_all | solution.py:410
  15.9 4.7 %pack_window.1 = bf16[32,256,128]{2,1,0:T(8,128)(2,1)} custom-call(s32[2]{0:T(128)} %bitcast.76, bf16[4,128,4096]{2,1,0:T(8,128)(2,1)} %bitcast.68, bf16[4,128,4096]{2,1,0:T(8,128)(2,1)} %bitcast.70), custom_call_target="tpu_custom_call" | custom-call | tf_op jit(solution)/shard_map/pack_window/pallas_call | solution.py:51
  20.6 0.1 copy.18.weight_ref
  20.8 1.7 convert_element_type.9
  22.6 1.7 fusion.1
  24.6 1.5 copy-done.10
  26.1 0.1 fusion.10
  26.2 3.0 %maximum_bitcast_fusion = (bf16[1,1024,512]{2,1,0:T(8,128)(2,1)S(1)}, bf16[1,1024,512]{2,1,0:T(8,128)(2,1)S(1)}) fusion(bf16[512,128]{1,0:T(8,128)(2,1)S(1)} %get-tuple-element.38, bf16[512,128]{1,0:T(8,128)(2,1)S(1)} %get-tuple-element.40, bf16[512,128]{1,0:T(8,128)(2,1)S(1)} %get-tuple-element.39, bf16[512,128]{1,0:T(8,128)(2,1)S(1)} %get-tuple-element.37, ...), kind=kLoop, calls=%fused_computation.1 | loop fusion | flops 16777216 | bytes 4194304 | tf_op jit(solution)/shard_map/stack | solution.py:402
  29.2 0.2 pad_maximum_fusion.w_out_ref
  29.4 41.7 %all-to-all-done.q_ref.k_ref.v_ref = bf16[32,512,128]{2,1,0:T(8,128)(2,1)} async-done(((bf16[32,512,128]{2,1,0:T(8,128)(2,1)}), bf16[32,512,128]{2,1,0:T(8,128)(2,1)}, u32[]{:S(2)}, u32[]{:S(2)}) %all-to-all-start) | async-done | bytes 4194336 | tf_op jit(solution)/shard_map/all_to_all | solution.py:410
  71.0 5.6 %all-to-all-start.1 = ((bf16[32,256,128]{2,1,0:T(8,128)(2,1)}), bf16[32,256,128]{2,1,0:T(8,128)(2,1)}, u32[]{:S(2)}, u32[]{:S(2)}) async-start(bf16[32,256,128]{2,1,0:T(8,128)(2,1)} %pack_window.1), calls=%async_computation.1 | async-start | bytes 4194304 | tf_op jit(solution)/shard_map/all_to_all | solution.py:410
  76.6 51.5 %attend_first.1 = (s32[4]{0:T(128)S(1)}, f32[8,4096]{1,0:T(8,128)S(1)}, f32[8,4096]{1,0:T(8,128)S(1)}, f32[128,4096]{1,0:T(8,128)S(1)}) custom-call(bf16[32,512,128]{2,1,0:T(8,128)(2,1)} %all-to-all-done.q_ref.k_ref.v_ref, bf16[32,512,128]{2,1,0:T(8,128)(2,1)} %all-to-all-done.q_ref.k_ref.v_ref, bf16[32,512,128]{2,1,0:T(8,128)(2,1)} %all-to-all-done.q_ref.k_ref.v_ref), custom_call_target="tpu_custom_call" | custom-call | flops 19327352832 | bytes 8388608 | tf_op jit(solution)/shard_map/attend_first/pallas_call | solution.py:220
  128.1 1.4 copy-done.4
  129.5 0.7 copy-done.6
  130.2 0.6 copy-done.8
  130.8 1.6 copy-done.5
  132.4 0.9 copy-done.7
  133.3 0.9 copy-done.9
  134.2 34.2 %attend_last.1 = bf16[32,72,128]{2,1,0:T(8,128)(2,1)S(1)} custom-call(bf16[32,512,128]{2,1,0:T(8,128)(2,1)} %all-to-all-done.q_ref.k_ref.v_ref, bf16[32,256,128]{2,1,0:T(8,128)(2,1)} %all-to-all-done.1.k_ref.v_ref, bf16[32,256,128]{2,1,0:T(8,128)(2,1)} %all-to-all-done.1.k_ref.v_ref, s32[4]{0:T(128)S(1)} %get-tuple-element.18.slow_ref, ...), custom_call_target="tpu_custom_call" | custom-call | flops 12884901888 | bytes 8388608 | tf_op jit(solution)/shard_map/attend_last/pallas_call | solution.py:220
  168.5 17.5 %all_to_all.20.parts_ref = bf16[32,72,128]{2,1,0:T(8,128)(2,1)S(1)} all-to-all(bf16[32,72,128]{2,1,0:T(8,128)(2,1)S(1)} %attend_last.1), channel_id=1, replica_groups=mesh['grp'=4,'ctx'=32] {'ctx'}, dimensions={0} | all-to-all | bytes 1179648 | tf_op jit(solution)/shard_map/all_to_all | solution.py:410
  186.0 0.8 clean_and_place.1
  186.8 11.9 %all_to_all.21.in_ref = bf16[4,80,128]{2,1,0:T(8,128)(2,1)S(1)} all-to-all(bf16[4,80,128]{2,1,0:T(8,128)(2,1)S(1)} %clean_and_place.1), channel_id=1, replica_groups=mesh['grp'=4,'ctx'=32] {'grp'}, dimensions={0} | all-to-all | bytes 163840 | tf_op jit(solution)/shard_map/all_to_all | solution.py:410
  198.7 5.9 %decode.1 = bf16[4096,128]{1,0:T(8,128)(2,1)} custom-call(bf16[4,80,128]{2,1,0:T(8,128)(2,1)S(1)} %all_to_all.21.in_ref, bf16[768,512]{1,0:T(8,128)(2,1)S(1)} %bitcast.59, f32[1,512]{1,0:T(1,128)S(1)} %bitcast.62, bf16[2,1024,512]{2,1,0:T(8,128)(2,1)S(1)} %pad_maximum_fusion.w_out_ref, f32[1,128]{1,0:T(1,128)S(1)} %bitcast.64), custom_call_target="tpu_custom_call" | custom-call | tf_op jit(solution)/shard_map/decode/pallas_call | solution.py:368
  (35 shorter events, 0.4 us)
Async XLA Ops:
  0.0 20.6 %copy-start = (bf16[4096,64]{0,1:T(8,128)(2,1)S(1)}, bf16[4096,64]{0,1:T(8,128)(2,1)}, u32[]{:S(2)}) copy-start(bf16[4096,64]{0,1:T(8,128)(2,1)} %param.22) | copy-start | bytes 1572868
  6.0 65.0 %all-to-all-start = ((bf16[32,512,128]{2,1,0:T(8,128)(2,1)}), bf16[32,512,128]{2,1,0:T(8,128)(2,1)}, u32[]{:S(2)}, u32[]{:S(2)}) async-start(bf16[32,512,128]{2,1,0:T(8,128)(2,1)} %pack_first.1), calls=%async_computation | async-start | bytes 8388608 | tf_op jit(solution)/shard_map/all_to_all | solution.py:410
  15.9 4.9 %copy-start.11 = (bf16[9,512,128]{2,1,0:T(8,128)(2,1)S(1)}, bf16[9,512,128]{2,1,0:T(8,128)(2,1)}, u32[]{:S(2)}) copy-start(bf16[9,512,128]{2,1,0:T(8,128)(2,1)} %param.26) | copy-start | bytes 3538948
  20.6 1.8 copy-start.13
  20.6 1.9 copy-start.14
  20.6 1.9 copy-start.12
  24.4 1.7 copy-start.10
  71.0 59.8 %all-to-all-start.1 = ((bf16[32,256,128]{2,1,0:T(8,128)(2,1)}), bf16[32,256,128]{2,1,0:T(8,128)(2,1)}, u32[]{:S(2)}, u32[]{:S(2)}) async-start(bf16[32,256,128]{2,1,0:T(8,128)(2,1)} %pack_window.1), calls=%async_computation.1 | async-start | bytes 4194304 | tf_op jit(solution)/shard_map/all_to_all | solution.py:410
  128.1 1.4 copy-start.4
  129.5 0.7 copy-start.6
  130.2 0.7 copy-start.8
  130.8 1.6 copy-start.5
  132.4 0.9 copy-start.7
  133.3 0.9 copy-start.9
  134.2 51.8 %copy-start.2 = (s32[1,4]{1,0:T(1,128)S(1)}, s32[1,4]{1,0:T(1,128)}, u32[]{:S(2)}) copy-start(s32[1,4]{1,0:T(1,128)} %param.23) | copy-start | bytes 52
  134.2 64.5 %copy-start.1 = (f32[512]{0:T(512)S(1)}, f32[512]{0:T(512)}, u32[]{:S(2)}) copy-start(f32[512]{0:T(512)} %param.25) | copy-start | bytes 6148
  134.2 64.5 %copy-start.3 = (f32[128]{0:T(128)S(1)}, f32[128]{0:T(128)}, u32[]{:S(2)}) copy-start(f32[128]{0:T(128)} %param.27) | copy-start | bytes 1540

commit v3 on v2

--- a/solution.py
+++ b/solution.py
@@ -14,7 +14,7 @@
 BF16 = jnp.bfloat16
 SCALE = math.log2(math.e) / math.sqrt(HD)
 HEADS_STEP = 8
-BQ = 1024
+BQ = 2048
 LIMIT = 110.0
 
 
@@ -25,7 +25,7 @@
 
 
 def pack_first_kernel(pick_ref, q_ref, k_ref, v_ref, sink_k_ref, sink_v_ref, out_ref):
-    for head in range(HEADS_STEP):
+    for head in range(out_ref.shape[0]):
         lanes = slice(head * HD, (head + 1) * HD)
         out_ref[head, 0:TOK, :] = k_ref[:, lanes]
         out_ref[head, 192 : 192 + TOK, :] = v_ref[:, lanes]
@@ -37,6 +37,24 @@
             out_ref[head, 192 + at : 208 + at, :] = sink_v_ref[0, rows, lanes]
 
 
+def pack_first(pick, current, keys, values):
+    heads = 2 * HEADS_STEP
+    own = pl.BlockSpec((TOK, heads * HD), lambda i, pick: (0, i))
+    cached = pl.BlockSpec((1, TOK, heads * HD), lambda i, pick: (pick[0], 0, i))
+    return pl.pallas_call(
+        pack_first_kernel,
+        grid_spec=pltpu.PrefetchScalarGridSpec(
+            num_scalar_prefetch=1,
+            grid=(HEADS // heads,),
+            in_specs=[own] * 3 + [cached] * 2,
+            out_specs=pl.BlockSpec((heads, 4 * TOK, HD), lambda i, pick: (i, 0, 0)),
+        ),
+        out_shape=jax.ShapeDtypeStruct((HEADS, 4 * TOK, HD), BF16),
+        compiler_params=params(60),
+        name="pack_first",
+    )(pick, *current, keys, values)
+
+
 def pack_window_kernel(pick_ref, k_ref, v_ref, out_ref):
     for head in range(HEADS_STEP):
         lanes = slice(head * HD, (head + 1) * HD)
@@ -44,22 +62,20 @@
         out_ref[head, TOK : 2 * TOK, :] = v_ref[0, :, lanes]
 
 
-def pack(pick, current, keys, values, which):
-    rows = 2 * TOK if which == 1 else 4 * TOK
-    own = pl.BlockSpec((TOK, HEADS_STEP * HD), lambda i, pick: (0, i))
-    cached = pl.BlockSpec((1, TOK, HEADS_STEP * HD), lambda i, pick: (pick[which], 0, i))
+def pack_window(pick, keys, values):
+    cached = pl.BlockSpec((1, TOK, HEADS_STEP * HD), lambda i, pick: (pick[1], 0, i))
     return pl.pallas_call(
-        pack_window_kernel if which == 1 else pack_first_kernel,
+        pack_window_kernel,
         grid_spec=pltpu.PrefetchScalarGridSpec(
             num_scalar_prefetch=1,
             grid=(HEADS // HEADS_STEP,),
-            in_specs=[own] * len(current) + [cached] * 2,
-            out_specs=pl.BlockSpec((HEADS_STEP, rows, HD), lambda i, pick: (i, 0, 0)),
+            in_specs=[cached] * 2,
+            out_specs=pl.BlockSpec((HEADS_STEP, 2 * TOK, HD), lambda i, pick: (i, 0, 0)),
         ),
-        out_shape=jax.ShapeDtypeStruct((HEADS, rows, HD), BF16),
+        out_shape=jax.ShapeDtypeStruct((HEADS, 2 * TOK, HD), BF16),
         compiler_params=params(60),
-        name="pack_window" if which == 1 else "pack_first",
-    )(pick, *current, keys, values)
+        name="pack_window",
+    )(pick, keys, values)
 
 
 def key_blocks(ref, step):
@@ -83,10 +99,8 @@
     return jnp.sum(x.reshape(x.shape[0] // 8, 8, x.shape[1]), axis=0)
 
 
-def attend_bounded(q, k_ref, v_ref, step, totals_ref, acc_ref, add):
+def attend_bounded(q, k_ref, v_ref, step, totals, acc):
     keys, values = key_blocks(k_ref, step), key_blocks(v_ref, step)
-    totals = totals_ref[...] if add else None
-    acc = acc_ref[...] if add else None
     following = score(keys[0], q)
     for j in range(len(keys)):
         scores = following
@@ -96,16 +110,11 @@
         mixed, total = mix(values[j], raised), fold_rows(raised)
         acc = mixed if acc is None else acc + mixed
         totals = total if totals is None else totals + total
-    totals_ref[...] = totals
-    acc_ref[...] = acc
-
-
-def attend_any(q, k_ref, v_ref, step, top_ref, totals_ref, acc_ref, add):
+    return totals, acc
+
+
+def attend_any(q, k_ref, v_ref, step, top_ref, totals_ref, acc_ref):
     sources, rows = k_ref.shape[0], k_ref.shape[1]
-    if not add:
-        top_ref[...] = jnp.full(top_ref.shape, -1e30, F32)
-        totals_ref[...] = jnp.zeros(totals_ref.shape, F32)
-        acc_ref[...] = jnp.zeros(acc_ref.shape, F32)
 
     def body(j, carry):
         here = pl.ds(j * step, step)
@@ -123,51 +132,48 @@
     lax.fori_loop(0, sources // step, body, 0)
 
 
-def bounded(q, k_ref, widest_ref):
-    @pl.when(pl.program_id(0) == 0)
-    def _():
-        widest = jnp.max(jnp.abs(k_ref[...].reshape(-1, HD)), axis=0, keepdims=True)
-        widest_ref[...] = jnp.broadcast_to(widest.astype(F32), widest_ref.shape)
-
-    widest = widest_ref[...].astype(BF16)
+def bounded(q, k_ref):
+    widest = jnp.max(jnp.abs(k_ref[...].reshape(-1, HD)), axis=0, keepdims=True)
     reach = lax.dot_general(
-        widest, jnp.abs(q), (((1,), (1,)), ((), ())), preferred_element_type=F32
-    )
-    return jnp.max(reach[0:8]) * (1.01 * SCALE) <= LIMIT
-
-
-def attend_first_kernel(q_ref, k_ref, v_ref, slow_ref, top_ref, totals_ref, acc_ref, widest_ref):
+        jnp.broadcast_to(widest, (16, HD)),
+        jnp.abs(q),
+        (((1,), (1,)), ((), ())),
+        preferred_element_type=F32,
+    )
+    return jnp.max(reach) * (1.01 * SCALE) <= LIMIT
+
+
+def attend_first_kernel(q_ref, k_ref, v_ref, slow_ref, top_ref, totals_ref, acc_ref):
     q = q_ref[...].reshape(BQ, HD)
-    fits = bounded(q, k_ref, widest_ref)
+    fits = bounded(q, k_ref)
+    top_ref[...] = jnp.zeros(top_ref.shape, F32)
+    totals_ref[...], acc_ref[...] = attend_bounded(q, k_ref, v_ref, 8, None, None)
     slow_ref[pl.program_id(0)] = jnp.where(fits, 0, 1)
-
-    @pl.when(fits)
-    def _():
-        top_ref[...] = jnp.zeros(top_ref.shape, F32)
-        attend_bounded(q, k_ref, v_ref, 4, totals_ref, acc_ref, False)
 
     @pl.when(jnp.logical_not(fits))
     def _():
-        attend_any(q, k_ref, v_ref, 4, top_ref, totals_ref, acc_ref, False)
+        top_ref[...] = jnp.full(top_ref.shape, -1e30, F32)
+        totals_ref[...] = jnp.zeros(totals_ref.shape, F32)
+        acc_ref[...] = jnp.zeros(acc_ref.shape, F32)
+        attend_any(q, k_ref, v_ref, 4, top_ref, totals_ref, acc_ref)
 
 
 def attend_last_kernel(
     q_ref, k_ref, v_ref, slow_ref, top_in_ref, totals_in_ref, acc_in_ref, weight_ref,
-    out_ref, top_ref, totals_ref, acc_ref, widest_ref,
+    out_ref, top_ref, totals_ref, acc_ref,
 ):
     q = q_ref[...].reshape(BQ, HD)
-    fits = bounded(q, k_ref, widest_ref) & (slow_ref[pl.program_id(0)] == 0)
-    totals_ref[...] = totals_in_ref[...]
-    acc_ref[...] = acc_in_ref[...]
-
-    @pl.when(fits)
-    def _():
-        attend_bounded(q, k_ref, v_ref, 8, totals_ref, acc_ref, True)
+    fits = bounded(q, k_ref) & (slow_ref[pl.program_id(0)] == 0)
+    totals_ref[...], acc_ref[...] = attend_bounded(
+        q, k_ref, v_ref, 8, totals_in_ref[...], acc_in_ref[...]
+    )
 
     @pl.when(jnp.logical_not(fits))
     def _():
         top_ref[...] = top_in_ref[...]
-        attend_any(q, k_ref, v_ref, 8, top_ref, totals_ref, acc_ref, True)
+        totals_ref[...] = totals_in_ref[...]
+        acc_ref[...] = acc_in_ref[...]
+        attend_any(q, k_ref, v_ref, 8, top_ref, totals_ref, acc_ref)
 
     totals = jnp.sum(totals_ref[...], axis=0, keepdims=True)
     attended = (acc_ref[...] / totals).astype(BF16)
@@ -201,7 +207,7 @@
         jax.ShapeDtypeStruct((HD, total), F32),
     ]
     in_specs = [q_spec, k_spec, v_spec]
-    scratch = [pltpu.VMEM((16, HD), F32)]
+    scratch = []
     args = (queries, keys_values, keys_values)
     if kind == "first":
         body, out_specs, out_shape = attend_first_kernel, state_specs, state_shapes
@@ -215,7 +221,7 @@
             pltpu.VMEM((8, BQ), F32),
             pltpu.VMEM((8, BQ), F32),
             pltpu.VMEM((HD, BQ), F32),
-        ] + scratch
+        ]
     keys = HEADS * k_rows
     return pl.pallas_call(
         body,
@@ -224,7 +230,7 @@
         out_specs=out_specs,
         out_shape=out_shape,
         scratch_shapes=scratch,
-        compiler_params=params(48),
+        compiler_params=params(60),
         cost_estimate=pl.CostEstimate(
             flops=6 * total * keys * HD,
             transcendentals=total * keys,
@@ -299,12 +305,12 @@
 
 
 def decode_kernel(
-    in_ref, w_in_ref, b_in_ref, w_out_ref, b_out_ref, out_ref, latent_ref, part_ref, wide_ref
+    mine_ref, in_ref, w_in_ref, b_in_ref, w_out_ref, b_out_ref, out_ref, latent_ref, part_ref, wide_ref
 ):
     tiles = 8
     flags = []
     for tile in range(tiles):
-        block = in_ref[tile // 2, (tile % 2) * 40 : (tile % 2) * 40 + 40, :].astype(F32)
+        block = in_ref[tile // 2, mine_ref[0], (tile % 2) * 40 : (tile % 2) * 40 + 40, :].astype(F32)
         for frames in range(2):
             for i in range(2):
                 at = frames * 16 + i * 8
@@ -363,11 +369,11 @@
         out_ref[rows, :] = jnp.where(flags[tile] > 0.5, wide_ref[rows, :], 0.0).astype(BF16)
 
 
-def decode(arrived, w_in, b_in, w_out, b_out):
+def decode(mine, arrived, w_in, b_in, w_out, b_out):
     vmem = pl.BlockSpec(memory_space=pltpu.VMEM)
     return pl.pallas_call(
         decode_kernel,
-        in_specs=[vmem] * 5,
+        in_specs=[pl.BlockSpec(memory_space=pltpu.SMEM)] + [vmem] * 5,
         out_specs=vmem,
         out_shape=jax.ShapeDtypeStruct((8 * 512, HD), BF16),
         scratch_shapes=[
@@ -377,7 +383,7 @@
         ],
         compiler_params=pltpu.CompilerParams(vmem_limit_bytes=48 << 20),
         name="decode",
-    )(arrived, w_in, b_in, w_out, b_out)
+    )(mine, arrived, w_in, b_in, w_out, b_out)
 
 
 def head_weight(velocity_weight):
@@ -428,8 +434,8 @@
 ):
     pick = clip_pick[0]
     current = (clip_queries[0], clip_keys[0], clip_values[0])
-    clip = exchange(pack(pick, current, cache_keys[0], cache_values[0], 0), "ctx")
-    window = pack(pick, (), cache_keys[0], cache_values[0], 1)
+    clip = exchange(pack_first(pick, current, cache_keys[0], cache_values[0]), "ctx")
+    window = pack_window(pick, cache_keys[0], cache_values[0])
     weight = head_weight(velocity_weight)
     w_in = place_in_weight(conv_in_weight)
     w_out = place_out_weight(conv_out_weight)
@@ -444,9 +450,10 @@
     parts = attend("last", clip, window, TOK, state, weight)
     parts = exchange(parts, "ctx")
     outgoing = clean_and_place(tile_owner[0], parts, noisy, prev)
-    arrived = exchange(outgoing, "grp")
+    arrived = lax.all_gather(outgoing, "grp", axis=0)
+    mine = lax.axis_index("grp").reshape(1)
     decoded = decode(
-        arrived, w_in, conv_in_bias.reshape(1, -1), w_out, conv_out_bias.reshape(1, -1)
+        mine, arrived, w_in, conv_in_bias.reshape(1, -1), w_out, conv_out_bias.reshape(1, -1)
     )
     return decoded.reshape(1, 1, 4, 2, 2, 256, 128)
 

time: 205 us -> 221 us (1.078)
  Pallas kernels: 103 us -> 125 us
  blocking collectives: 29.4 us -> 10.7 us
  waiting for transfers between devices: 41.7 us -> 51.1 us
  starting transfers between devices: 15.5 us -> 23.4 us
  local copies, waits for them, and re-layouts: 7.97 us -> 2.48 us
    all_to_all x2 -> x0, blocking collectives: 29.4 us -> none  [exchange(): return lax.all_to_all(x, axis, split_axis=0, concat_axis=0, tiled=True)]
    pallas_call x2, Pallas kernels: 85.7 us -> 108 us  [attend(): pl.pallas_call(body, grid=(steps,), in_specs=in_specs, out_specs=out_spec...]
    all_gather x0 -> x1, blocking collectives: none -> 10.7 us  [local(): arrived = lax.all_gather(outgoing, 'grp', axis=0)]
    all_to_all x2 -> x3, waiting for transfers between devices: 41.7 us -> 51.1 us  [exchange(): return lax.all_to_all(x, axis, split_axis=0, concat_axis=0, tiled=True)]
    all_to_all x2 -> x3, starting transfers between devices: 15.5 us -> 23.4 us  [exchange(): return lax.all_to_all(x, axis, split_axis=0, concat_axis=0, tiled=True)]
    unnamed x30 -> x18, local copies, waits for them, and re-layouts: 7.58 us -> 1.49 us
  transfers between devices with their start and end apart: 2 -> 3, of which waited for: 1 -> 2; matrix products, arithmetic and copies ran while one was open for 3% -> 4% of each run, Pallas kernels for 27% -> 31%
where the time goes in v3:
time: 221 us; the launch traced here: 220 us
  Pallas kernels  125 us (57%)
  waiting for transfers between devices  51.1 us (23%)
  starting transfers between devices  23.4 us (11%)
  blocking collectives  10.7 us (5%)
  other arithmetic  6.77 us (3%)
  local copies, waits for them, and re-layouts  2.48 us (1%)
    pallas_call x2, Pallas kernels, attend(): pl.pallas_call(body, grid=(steps,), in_specs=in_specs, out_specs=out_spec...  108 us
    all_to_all x3, waiting for transfers between devices, exchange(): return lax.all_to_all(x, axis, split_axis=0, concat_axis=0, tiled=True)  51.1 us
    all_to_all x3, starting transfers between devices, exchange(): return lax.all_to_all(x, axis, split_axis=0, concat_axis=0, tiled=True)  23.4 us
    all_gather x1, blocking collectives, local(): arrived = lax.all_gather(outgoing, 'grp', axis=0)  10.7 us
    pallas_call x1, Pallas kernels, decode(): pl.pallas_call(decode_kernel, in_specs=[pl.BlockSpec(memory_space=pltpu.S...  5.89 us
    pallas_call x1, Pallas kernels, pack_first(): pl.pallas_call(pack_first_kernel, grid_spec=pltpu.PrefetchScalarGridSpec(...  5.03 us
    pallas_call x1, Pallas kernels, pack_window(): pl.pallas_call(pack_window_kernel, grid_spec=pltpu.PrefetchScalarGridSpec...  4.72 us
  transfers between devices with their start and end apart: 3, of which 2 were waited for; matrix products, arithmetic and copies ran while one was open for 4% of the time, Pallas kernels for 31%

profile of v3, /device:TPU:1, one launch (start us, length us, event | category | flops | bytes accessed | tf_op | source)
XLA Modules:
  0.0 220.1 jit_solution(7782180334123623341)
XLA Ops:
  0.0 5.0 %pack_first.1 = bf16[32,512,128]{2,1,0:T(8,128)(2,1)} custom-call(s32[2]{0:T(128)} %bitcast.78, bf16[128,4096]{1,0:T(8,128)(2,1)} %bitcast.74, bf16[128,4096]{1,0:T(8,128)(2,1)} %bitcast.75, bf16[128,4096]{1,0:T(8,128)(2,1)} %bitcast.76, bf16[4,128,4096]{2,1,0:T(8,128)(2,1)} %bitcast.70, bf16[4,128,4096]{2,1,0:T(8,128)(2,1)} %bitcast.72), custom_call_target="tpu_custom_call" | custom-call | tf_op jit(solution)/shard_map/pack_first/pallas_call | solution.py:44
  5.0 9.9 %all-to-all-start = ((bf16[32,512,128]{2,1,0:T(8,128)(2,1)}), bf16[32,512,128]{2,1,0:T(8,128)(2,1)}, u32[]{:S(2)}, u32[]{:S(2)}) async-start(bf16[32,512,128]{2,1,0:T(8,128)(2,1)} %pack_first.1), calls=%async_computation | async-start | bytes 8388608 | tf_op jit(solution)/shard_map/all_to_all | solution.py:416
  14.9 0.0 copy-start.5
  14.9 4.7 %pack_window.1 = bf16[32,256,128]{2,1,0:T(8,128)(2,1)} custom-call(s32[2]{0:T(128)} %bitcast.79, bf16[4,128,4096]{2,1,0:T(8,128)(2,1)} %bitcast.71, bf16[4,128,4096]{2,1,0:T(8,128)(2,1)} %bitcast.73), custom_call_target="tpu_custom_call" | custom-call | tf_op jit(solution)/shard_map/pack_window/pallas_call | solution.py:67
  19.7 0.7 copy.21.weight_ref
  20.4 0.0 copy-done.5
  20.4 1.7 convert_element_type.9
  22.2 0.1 pad.4
  22.2 1.7 fusion.1
  24.2 1.5 copy-done.4
  25.6 0.1 fusion.2
  25.7 0.1 fusion.10
  25.8 3.0 %maximum_bitcast_fusion = (bf16[1,1024,512]{2,1,0:T(8,128)(2,1)S(1)}, bf16[1,1024,512]{2,1,0:T(8,128)(2,1)S(1)}) fusion(bf16[512,128]{1,0:T(8,128)(2,1)S(1)} %get-tuple-element.38, bf16[512,128]{1,0:T(8,128)(2,1)S(1)} %get-tuple-element.40, bf16[512,128]{1,0:T(8,128)(2,1)S(1)} %get-tuple-element.39, bf16[512,128]{1,0:T(8,128)(2,1)S(1)} %get-tuple-element.37, ...), kind=kLoop, calls=%fused_computation.1 | loop fusion | flops 16777216 | bytes 4194304 | tf_op jit(solution)/shard_map/stack | solution.py:408
  28.8 0.2 pad_maximum_fusion.w_out_ref
  29.0 41.0 %all-to-all-done.q_ref.k_ref.v_ref = bf16[32,512,128]{2,1,0:T(8,128)(2,1)} async-done(((bf16[32,512,128]{2,1,0:T(8,128)(2,1)}), bf16[32,512,128]{2,1,0:T(8,128)(2,1)}, u32[]{:S(2)}, u32[]{:S(2)}) %all-to-all-start) | async-done | bytes 4194336 | tf_op jit(solution)/shard_map/all_to_all | solution.py:416
  70.0 5.6 %all-to-all-start.1 = ((bf16[32,256,128]{2,1,0:T(8,128)(2,1)}), bf16[32,256,128]{2,1,0:T(8,128)(2,1)}, u32[]{:S(2)}, u32[]{:S(2)}) async-start(bf16[32,256,128]{2,1,0:T(8,128)(2,1)} %pack_window.1), calls=%async_computation.1 | async-start | bytes 4194304 | tf_op jit(solution)/shard_map/all_to_all | solution.py:416
  75.6 64.4 %attend_first.1 = (s32[2]{0:T(128)}, f32[8,4096]{1,0:T(8,128)}, f32[8,4096]{1,0:T(8,128)}, f32[128,4096]{1,0:T(8,128)}) custom-call(bf16[32,512,128]{2,1,0:T(8,128)(2,1)} %all-to-all-done.q_ref.k_ref.v_ref, bf16[32,512,128]{2,1,0:T(8,128)(2,1)} %all-to-all-done.q_ref.k_ref.v_ref, bf16[32,512,128]{2,1,0:T(8,128)(2,1)} %all-to-all-done.q_ref.k_ref.v_ref), custom_call_target="tpu_custom_call" | custom-call | flops 19327352832 | bytes 8388608 | tf_op jit(solution)/shard_map/attend_first/pallas_call | solution.py:226
  140.0 0.0 all-to-all-done.1.k_ref.v_ref
  140.0 44.1 %attend_last.1 = bf16[32,72,128]{2,1,0:T(8,128)(2,1)} custom-call(bf16[32,512,128]{2,1,0:T(8,128)(2,1)} %all-to-all-done.q_ref.k_ref.v_ref, bf16[32,256,128]{2,1,0:T(8,128)(2,1)} %all-to-all-done.1.k_ref.v_ref, bf16[32,256,128]{2,1,0:T(8,128)(2,1)} %all-to-all-done.1.k_ref.v_ref, s32[2]{0:T(128)} %get-tuple-element.18.slow_ref, ...), custom_call_target="tpu_custom_call" | custom-call | flops 12884901888 | bytes 8388608 | tf_op jit(solution)/shard_map/attend_last/pallas_call | solution.py:226
  184.1 7.9 %all-to-all-start.2 = ((bf16[32,72,128]{2,1,0:T(8,128)(2,1)}), bf16[32,72,128]{2,1,0:T(8,128)(2,1)}, u32[]{:S(2)}, u32[]{:S(2)}) async-start(bf16[32,72,128]{2,1,0:T(8,128)(2,1)} %attend_last.1), calls=%async_computation.2 | async-start | bytes 1179648 | tf_op jit(solution)/shard_map/all_to_all | solution.py:416
  192.1 10.1 %all-to-all-done.2.parts_ref = bf16[32,72,128]{2,1,0:T(8,128)(2,1)} async-done(((bf16[32,72,128]{2,1,0:T(8,128)(2,1)}), bf16[32,72,128]{2,1,0:T(8,128)(2,1)}, u32[]{:S(2)}, u32[]{:S(2)}) %all-to-all-start.2) | async-done | bytes 589856 | tf_op jit(solution)/shard_map/all_to_all | solution.py:416
  202.2 1.4 clean_and_place.1
  203.5 10.7 %all-gather = bf16[16,80,128]{2,1,0:T(8,128)(2,1)S(1)} all-gather(bf16[4,80,128]{2,1,0:T(8,128)(2,1)S(1)} %clean_and_place.1), channel_id=2, replica_groups=mesh['grp'=4,'ctx'=32] {'grp'}, dimensions={0}, use_global_device_ids=true | all-gather | bytes 409600 | tf_op jit(solution)/shard_map/all_gather | solution.py:453
  214.2 5.9 %decode.1 = bf16[4096,128]{1,0:T(8,128)(2,1)} custom-call(s32[1]{0:T(128)} %bitcast.mine_ref, bf16[4,4,80,128]{3,2,1,0:T(8,128)(2,1)S(1)} %bitcast.62, bf16[768,512]{1,0:T(8,128)(2,1)S(1)} %bitcast.61, f32[1,512]{1,0:T(1,128)S(1)} %bitcast.65, bf16[2,1024,512]{2,1,0:T(8,128)(2,1)S(1)} %pad_maximum_fusion.w_out_ref, f32[1,128]{1,0:T(1,128)S(1)} %bitcast.67), custom_call_target="tpu_custom_call" | custom-call | tf_op jit(solution)/shard_map/decode/pallas_call | solution.py:374
  (24 shorter events, 0.3 us)
Async XLA Ops:
  0.0 19.7 %copy-start = (bf16[4096,64]{0,1:T(8,128)(2,1)S(1)}, bf16[4096,64]{0,1:T(8,128)(2,1)}, u32[]{:S(2)}) copy-start(bf16[4096,64]{0,1:T(8,128)(2,1)} %param.22) | copy-start | bytes 1572868
  5.0 65.0 %all-to-all-start = ((bf16[32,512,128]{2,1,0:T(8,128)(2,1)}), bf16[32,512,128]{2,1,0:T(8,128)(2,1)}, u32[]{:S(2)}, u32[]{:S(2)}) async-start(bf16[32,512,128]{2,1,0:T(8,128)(2,1)} %pack_first.1), calls=%async_computation | async-start | bytes 8388608 | tf_op jit(solution)/shard_map/all_to_all | solution.py:416
  14.9 5.5 %copy-start.5 = (bf16[9,512,128]{2,1,0:T(8,128)(2,1)S(1)}, bf16[9,512,128]{2,1,0:T(8,128)(2,1)}, u32[]{:S(2)}) copy-start(bf16[9,512,128]{2,1,0:T(8,128)(2,1)} %param.26) | copy-start | bytes 3538948
  19.6 2.4 %copy-start.7 = (bf16[1,4,2,1024]{3,2,1,0:T(2,128)(2,1)S(1)}, bf16[1,4,2,1024]{3,2,1,0:T(2,128)(2,1)}, u32[]{:S(2)}) copy-start(bf16[1,4,2,1024]{3,2,1,0:T(2,128)(2,1)} %param.20) | copy-start | bytes 49156
  19.6 2.5 %copy-start.8 = (bf16[1,4,2,1024]{3,2,1,0:T(2,128)(2,1)S(1)}, bf16[1,4,2,1024]{3,2,1,0:T(2,128)(2,1)}, u32[]{:S(2)}) copy-start(bf16[1,4,2,1024]{3,2,1,0:T(2,128)(2,1)} %param.21) | copy-start | bytes 49156
  19.6 2.5 %copy-start.6 = (bf16[432,512]{1,0:T(8,128)(2,1)S(1)}, bf16[432,512]{1,0:T(8,128)(2,1)}, u32[]{:S(2)}) copy-start(bf16[432,512]{1,0:T(8,128)(2,1)} %param.24) | copy-start | bytes 1327108
  24.0 1.7 copy-start.4
  70.0 70.0 %all-to-all-start.1 = ((bf16[32,256,128]{2,1,0:T(8,128)(2,1)}), bf16[32,256,128]{2,1,0:T(8,128)(2,1)}, u32[]{:S(2)}, u32[]{:S(2)}) async-start(bf16[32,256,128]{2,1,0:T(8,128)(2,1)} %pack_window.1), calls=%async_computation.1 | async-start | bytes 4194304 | tf_op jit(solution)/shard_map/all_to_all | solution.py:416
  140.0 62.1 %copy-start.2 = (s32[1,4]{1,0:T(1,128)S(1)}, s32[1,4]{1,0:T(1,128)}, u32[]{:S(2)}) copy-start(s32[1,4]{1,0:T(1,128)} %param.23) | copy-start | bytes 52
  184.1 30.1 %copy-start.1 = (f32[512]{0:T(512)S(1)}, f32[512]{0:T(512)}, u32[]{:S(2)}) copy-start(f32[512]{0:T(512)} %param.25) | copy-start | bytes 6148
  184.1 30.1 %copy-start.3 = (f32[128]{0:T(128)S(1)}, f32[128]{0:T(128)}, u32[]{:S(2)}) copy-start(f32[128]{0:T(128)} %param.27) | copy-start | bytes 1540
  184.1 18.0 %all-to-all-start.2 = ((bf16[32,72,128]{2,1,0:T(8,128)(2,1)}), bf16[32,72,128]{2,1,0:T(8,128)(2,1)}, u32[]{:S(2)}, u32[]{:S(2)}) async-start(bf16[32,72,128]{2,1,0:T(8,128)(2,1)} %attend_last.1), calls=%async_computation.2 | async-start | bytes 1179648 | tf_op jit(solution)/shard_map/all_to_all | solution.py:416

commit v4 on v3

--- a/solution.py
+++ b/solution.py
@@ -240,7 +240,7 @@
     )(*args)
 
 
-def clean_kernel(owner_ref, parts_ref, noisy_ref, prev_ref, out_ref, token_ref):
+def clean_kernel(parts_ref, noisy_ref, out_ref, token_ref):
     width = HEADS * HD
     sums = jnp.sum(parts_ref[...].astype(F32), axis=0)
     scale = 1.0 / jnp.sqrt(sums[64:65] * (1.0 / width) + 1e-06)
@@ -248,7 +248,6 @@
     velocity = jnp.concatenate([velocity, jnp.zeros((64, HD), F32)], axis=0)
     token_ref[...] = jnp.transpose(velocity)
     lane = lax.broadcasted_iota(jnp.int32, (32, HD), 1)
-    clean = []
     by_px = [token_ref[pl.ds(px, 32, stride=4), :] for px in range(4)]
     for i in range(2):
         moved = jnp.zeros((32, HD), F32)
@@ -256,46 +255,21 @@
             turn = (px - i) * 32 % HD
             piece = pltpu.roll(by_px[px], turn, axis=1) if turn else by_px[px]
             moved = jnp.where(lane // 32 == px, piece, moved)
-        clean.append(noisy_ref[i * 32 : i * 32 + 32, :].astype(F32) - moved)
-    prev = prev_ref[...].astype(F32)
-    owners = [owner_ref[t] for t in range(4)]
-    ranks = []
-    for t in range(4):
-        rank = jnp.int32(0)
-        for earlier in range(t):
-            rank = rank + jnp.where(owners[earlier] == owners[t], 1, 0)
-        ranks.append(rank)
-    zero = jnp.zeros((8, HD), F32)
-    for owner in range(4):
-        rows = []
-        for slot in range(2):
-            picked = [zero] * 5
-            for t in range(4):
-                here = (owners[t] == owner) & (ranks[t] == slot)
-                piece = slice(t * 8, t * 8 + 8)
-                pieces = (
-                    prev[0:32][piece],
-                    prev[32:64][piece],
-                    clean[0][piece],
-                    clean[1][piece],
-                    jnp.ones((8, HD), F32),
-                )
-                picked = [jnp.where(here, new, old) for new, old in zip(pieces, picked)]
-            rows += picked
-        out_ref[owner] = jnp.concatenate(rows, axis=0).astype(BF16)
-
-
-def clean_and_place(owner, parts, noisy, prev):
+        rows = slice(i * 32, i * 32 + 32)
+        out_ref[rows, :] = (noisy_ref[rows, :].astype(F32) - moved).astype(BF16)
+
+
+def clean_rows(parts, noisy):
     vmem = pl.BlockSpec(memory_space=pltpu.VMEM)
     return pl.pallas_call(
         clean_kernel,
-        in_specs=[pl.BlockSpec(memory_space=pltpu.SMEM), vmem, vmem, vmem],
+        in_specs=[vmem, vmem],
         out_specs=vmem,
-        out_shape=jax.ShapeDtypeStruct((4, 80, HD), BF16),
+        out_shape=jax.ShapeDtypeStruct((64, HD), BF16),
         scratch_shapes=[pltpu.VMEM((HD, HD), F32)],
         compiler_params=pltpu.CompilerParams(vmem_limit_bytes=16 << 20),
-        name="clean_and_place",
-    )(owner, parts, noisy, prev)
+        name="clean_rows",
+    )(parts, noisy)
 
 
 def shift_rows(x, by):
@@ -305,23 +279,41 @@
 
 
 def decode_kernel(
-    mine_ref, in_ref, w_in_ref, b_in_ref, w_out_ref, b_out_ref, out_ref, latent_ref, part_ref, wide_ref
+    mine_ref, prev_ref, clean_ref, w_in_ref, b_in_ref, w_out_ref, b_out_ref,
+    out_ref, latent_ref, column_ref, part_ref, wide_ref,
 ):
     tiles = 8
+    mine = mine_ref[0].astype(F32)
     flags = []
-    for tile in range(tiles):
-        block = in_ref[tile // 2, mine_ref[0], (tile % 2) * 40 : (tile % 2) * 40 + 40, :].astype(F32)
-        for frames in range(2):
-            for i in range(2):
-                at = frames * 16 + i * 8
-                latent_ref[pl.ds(tile * 32 + frames * 16 + i, 8, stride=2), :] = block[at : at + 8]
-        flags.append(block[32:33])
+    for sender in range(4):
+        old = prev_ref[sender].astype(F32)
+        new = clean_ref[sender].astype(F32)
+        owners = [old[64 + t : 65 + t] for t in range(4)]
+        ranks = []
+        for t in range(4):
+            rank = jnp.zeros((1, HD), F32)
+            for earlier in range(t):
+                rank = rank + jnp.where(owners[earlier] == owners[t], 1.0, 0.0)
+            ranks.append(rank)
+        for slot in range(2):
+            here = [
+                jnp.where((owners[t] == mine) & (ranks[t] == slot), 1.0, 0.0) for t in range(4)
+            ]
+            flags.append(here[0] + here[1] + here[2] + here[3])
+            masks = [jnp.broadcast_to(h, (8, HD)) > 0.5 for h in here]
+            tile = sender * 2 + slot
+            for frames, source in ((0, old), (1, new)):
+                for i in range(2):
+                    picked = jnp.zeros((8, HD), F32)
+                    for t in range(4):
+                        at = i * 32 + t * 8
+                        picked = jnp.where(masks[t], source[at : at + 8], picked)
+                    latent_ref[pl.ds(tile * 32 + frames * 16 + i, 8, stride=2), :] = picked
     latent = latent_ref[...].reshape(tiles * 4, 8, HD)
     by_row = [shift_rows(latent, 1), latent, shift_rows(latent, -1)]
     by_row = [x.reshape(tiles * 32, HD) for x in by_row]
     lane = lax.broadcasted_iota(jnp.int32, (tiles * 32, HD), 1)
     low = lane < 64
-    hidden = []
     for x in range(8):
         turn = (16 - 16 * x) % HD
         pair = [
@@ -341,19 +333,16 @@
         columns = jnp.concatenate(
             [taps[:, dt : dt + 2].reshape(TOK, 2 * HD).astype(BF16) for dt in range(3)], axis=1
         )
-        mid = jnp.dot(columns, w_in_ref[...], preferred_element_type=F32) + b_in_ref[...]
-        hidden.append(mid / (1.0 + jnp.exp(-mid)))
+        column_ref[x * TOK : (x + 1) * TOK, :] = columns
+    mid = jnp.dot(column_ref[...], w_in_ref[...], preferred_element_type=F32) + b_in_ref[...]
+    hidden = mid / (1.0 + jnp.exp(-mid))
+    grouped = hidden.reshape(8 * TOK // 8, 8, 512)
+    here = hidden.astype(BF16)
     bias = b_out_ref[...]
     for a in range(2):
-        for x in range(8):
-            here = hidden[x]
-            grouped = here.reshape(16, 8, 512)
-            other = shift_rows(grouped, 1 if a == 0 else -1).reshape(TOK, 512)
-            pair = [other, here] if a == 0 else [here, other]
-            rows = jnp.concatenate([p.astype(BF16) for p in pair], axis=1)
-            part_ref[x * TOK : (x + 1) * TOK, :] = jnp.dot(
-                rows, w_out_ref[a], preferred_element_type=F32
-            )
+        other = shift_rows(grouped, 1 if a == 0 else -1).reshape(8 * TOK, 512).astype(BF16)
+        rows = jnp.concatenate([other, here] if a == 0 else [here, other], axis=1)
+        part_ref[...] = jnp.dot(rows, w_out_ref[a], preferred_element_type=F32)
         for x in range(8):
             at = x * TOK
             first = part_ref[at : at + TOK, 128:256] + bias
@@ -369,21 +358,22 @@
         out_ref[rows, :] = jnp.where(flags[tile] > 0.5, wide_ref[rows, :], 0.0).astype(BF16)
 
 
-def decode(mine, arrived, w_in, b_in, w_out, b_out):
+def decode(mine, prev, clean, w_in, b_in, w_out, b_out):
     vmem = pl.BlockSpec(memory_space=pltpu.VMEM)
     return pl.pallas_call(
         decode_kernel,
-        in_specs=[pl.BlockSpec(memory_space=pltpu.SMEM)] + [vmem] * 5,
+        in_specs=[pl.BlockSpec(memory_space=pltpu.SMEM)] + [vmem] * 6,
         out_specs=vmem,
         out_shape=jax.ShapeDtypeStruct((8 * 512, HD), BF16),
         scratch_shapes=[
             pltpu.VMEM((256, HD), F32),
+            pltpu.VMEM((8 * TOK, 768), BF16),
             pltpu.VMEM((8 * TOK, 512), F32),
             pltpu.VMEM((8 * 512, HD), F32),
         ],
         compiler_params=pltpu.CompilerParams(vmem_limit_bytes=48 << 20),
         name="decode",
-    )(mine, arrived, w_in, b_in, w_out, b_out)
+    )(mine, prev, clean, w_in, b_in, w_out, b_out)
 
 
 def head_weight(velocity_weight):
@@ -440,7 +430,10 @@
     w_in = place_in_weight(conv_in_weight)
     w_out = place_out_weight(conv_out_weight)
     noisy = latent_rows(noisy_latent[0])
-    prev = latent_rows(prev_latent[0])
+    owners = jnp.broadcast_to(tile_owner[0].astype(BF16)[:, None], (4, HD))
+    owners = jnp.pad(owners, ((0, 4), (0, 0)))
+    prev = jnp.concatenate([latent_rows(prev_latent[0]), owners], axis=0)
+    prev = lax.all_gather(prev, "grp", axis=0)
 
     clip, window, weight, w_in, w_out, noisy, prev = lax.optimization_barrier(
         (clip, window, weight, w_in, w_out, noisy, prev)
@@ -449,11 +442,10 @@
     state = attend("first", clip, clip, 192)
     parts = attend("last", clip, window, TOK, state, weight)
     parts = exchange(parts, "ctx")
-    outgoing = clean_and_place(tile_owner[0], parts, noisy, prev)
-    arrived = lax.all_gather(outgoing, "grp", axis=0)
+    clean = lax.all_gather(clean_rows(parts, noisy), "grp", axis=0)
     mine = lax.axis_index("grp").reshape(1)
     decoded = decode(
-        mine, arrived, w_in, conv_in_bias.reshape(1, -1), w_out, conv_out_bias.reshape(1, -1)
+        mine, prev, clean, w_in, conv_in_bias.reshape(1, -1), w_out, conv_out_bias.reshape(1, -1)
     )
     return decoded.reshape(1, 1, 4, 2, 2, 256, 128)
 

time: 221 us -> 230 us (1.041)
  blocking collectives: 10.7 us -> 54.9 us
  waiting for transfers between devices: 51.1 us -> 10.3 us
  starting transfers between devices: 23.4 us -> 28.7 us
    all_gather x1 -> x2, blocking collectives: 10.7 us -> 54.9 us  [the longest x1 45.1 us: local(): prev = lax.all_gather(prev, 'grp', axis=0)]
    all_to_all x3, waiting for transfers between devices: 51.1 us -> 10.3 us  [exchange(): return lax.all_to_all(x, axis, split_axis=0, concat_axis=0, tiled=True)]
    all_to_all x3, starting transfers between devices: 23.4 us -> 28.7 us  [exchange(): return lax.all_to_all(x, axis, split_axis=0, concat_axis=0, tiled=True)]
  transfers between devices with their start and end apart: 3 -> 3, of which waited for: 2 -> 1; matrix products, arithmetic and copies ran while one was open for 4% -> 3% of each run, Pallas kernels for 31% -> 30%
where the time goes in v4:
time: 230 us; the launch traced here: 229 us
  Pallas kernels  126 us (55%)
  blocking collectives  54.9 us (24%)
  starting transfers between devices  28.7 us (12%)
  waiting for transfers between devices  10.3 us (4%)
  other arithmetic  6.93 us (3%)
  local copies, waits for them, and re-layouts  2.48 us (1%)
    pallas_call x2, Pallas kernels, attend(): pl.pallas_call(body, grid=(steps,), in_specs=in_specs, out_specs=out_spec...  109 us
    all_gather x1, blocking collectives, local(): prev = lax.all_gather(prev, 'grp', axis=0)  45.1 us
    all_to_all x3, starting transfers between devices, exchange(): return lax.all_to_all(x, axis, split_axis=0, concat_axis=0, tiled=True)  28.7 us
    all_to_all x3, waiting for transfers between devices, exchange(): return lax.all_to_all(x, axis, split_axis=0, concat_axis=0, tiled=True)  10.3 us
    all_gather x1, blocking collectives, local(): clean = lax.all_gather(clean_rows(parts, noisy), 'grp', axis=0)  9.73 us
    pallas_call x1, Pallas kernels, decode(): pl.pallas_call(decode_kernel, in_specs=[pl.BlockSpec(memory_space=pltpu.S...  5.87 us
    pallas_call x1, Pallas kernels, pack_first(): pl.pallas_call(pack_first_kernel, grid_spec=pltpu.PrefetchScalarGridSpec(...  5.03 us
    pallas_call x1, Pallas kernels, pack_window(): pl.pallas_call(pack_window_kernel, grid_spec=pltpu.PrefetchScalarGridSpec...  4.72 us
  transfers between devices with their start and end apart: 3, of which 1 were waited for; matrix products, arithmetic and copies ran while one was open for 3% of the time, Pallas kernels for 30%

profile of v4, /device:TPU:1, one launch (start us, length us, event | category | flops | bytes accessed | tf_op | source)
XLA Modules:
  0.0 229.3 jit_solution(7225692934418613757)
XLA Ops:
  0.0 5.0 %pack_first.1 = bf16[32,512,128]{2,1,0:T(8,128)(2,1)} custom-call(s32[2]{0:T(128)} %bitcast.80, bf16[128,4096]{1,0:T(8,128)(2,1)} %bitcast.74, bf16[128,4096]{1,0:T(8,128)(2,1)} %bitcast.75, bf16[128,4096]{1,0:T(8,128)(2,1)} %bitcast.76, bf16[4,128,4096]{2,1,0:T(8,128)(2,1)} %bitcast.70, bf16[4,128,4096]{2,1,0:T(8,128)(2,1)} %bitcast.72), custom_call_target="tpu_custom_call" | custom-call | tf_op jit(solution)/shard_map/pack_first/pallas_call | solution.py:44
  5.0 9.9 %all-to-all-start = ((bf16[32,512,128]{2,1,0:T(8,128)(2,1)}), bf16[32,512,128]{2,1,0:T(8,128)(2,1)}, u32[]{:S(2)}, u32[]{:S(2)}) async-start(bf16[32,512,128]{2,1,0:T(8,128)(2,1)} %pack_first.1), calls=%async_computation | async-start | bytes 8388608 | tf_op jit(solution)/shard_map/all_to_all | solution.py:406
  14.9 4.7 %pack_window.1 = bf16[32,256,128]{2,1,0:T(8,128)(2,1)} custom-call(s32[2]{0:T(128)} %bitcast.81, bf16[4,128,4096]{2,1,0:T(8,128)(2,1)} %bitcast.71, bf16[4,128,4096]{2,1,0:T(8,128)(2,1)} %bitcast.73), custom_call_target="tpu_custom_call" | custom-call | tf_op jit(solution)/shard_map/pack_window/pallas_call | solution.py:67
  19.7 0.7 copy.18.weight_ref
  20.4 1.7 convert_element_type.21
  22.2 0.1 pad.10
  22.3 0.1 compare_select_fusion
  22.3 0.1 pad_maximum_fusion.1
  22.4 45.1 %all-gather = bf16[288,128]{1,0:T(8,128)(2,1)S(1)} all-gather(bf16[72,128]{1,0:T(8,128)(2,1)S(1)} %pad_maximum_fusion.1), channel_id=2, replica_groups=mesh['grp'=4,'ctx'=32] {'grp'}, dimensions={0}, use_global_device_ids=true | all-gather | bytes 92160 | tf_op jit(solution)/shard_map/all_gather | solution.py:436
  67.6 1.7 fusion.1
  69.5 1.5 copy-done.3
  71.0 0.1 fusion.2
  71.0 0.1 fusion.10
  71.1 3.0 %maximum_bitcast_fusion = (bf16[1,1024,512]{2,1,0:T(8,128)(2,1)S(1)}, bf16[1,1024,512]{2,1,0:T(8,128)(2,1)S(1)}) fusion(bf16[512,128]{1,0:T(8,128)(2,1)S(1)} %get-tuple-element.38, bf16[512,128]{1,0:T(8,128)(2,1)S(1)} %get-tuple-element.40, bf16[512,128]{1,0:T(8,128)(2,1)S(1)} %get-tuple-element.39, bf16[512,128]{1,0:T(8,128)(2,1)S(1)} %get-tuple-element.37, ...), kind=kLoop, calls=%fused_computation.1 | loop fusion | flops 16777216 | bytes 4194304 | tf_op jit(solution)/shard_map/stack | solution.py:398
  74.1 0.2 pad_maximum_fusion.w_out_ref
  74.3 11.0 %all-to-all-start.1 = ((bf16[32,256,128]{2,1,0:T(8,128)(2,1)}), bf16[32,256,128]{2,1,0:T(8,128)(2,1)}, u32[]{:S(2)}, u32[]{:S(2)}) async-start(bf16[32,256,128]{2,1,0:T(8,128)(2,1)} %pack_window.1), calls=%async_computation.1 | async-start | bytes 4194304 | tf_op jit(solution)/shard_map/all_to_all | solution.py:406
  85.3 64.7 %attend_first.1 = (s32[2]{0:T(128)}, f32[8,4096]{1,0:T(8,128)}, f32[8,4096]{1,0:T(8,128)}, f32[128,4096]{1,0:T(8,128)}) custom-call(bf16[32,512,128]{2,1,0:T(8,128)(2,1)} %all-to-all-done.q_ref.k_ref.v_ref, bf16[32,512,128]{2,1,0:T(8,128)(2,1)} %all-to-all-done.q_ref.k_ref.v_ref, bf16[32,512,128]{2,1,0:T(8,128)(2,1)} %all-to-all-done.q_ref.k_ref.v_ref), custom_call_target="tpu_custom_call" | custom-call | flops 19327352832 | bytes 8388608 | tf_op jit(solution)/shard_map/attend_first/pallas_call | solution.py:226
  150.0 0.0 copy-start.2
  150.0 44.2 %attend_last.1 = bf16[32,72,128]{2,1,0:T(8,128)(2,1)} custom-call(bf16[32,512,128]{2,1,0:T(8,128)(2,1)} %all-to-all-done.q_ref.k_ref.v_ref, bf16[32,256,128]{2,1,0:T(8,128)(2,1)} %all-to-all-done.1.k_ref.v_ref, bf16[32,256,128]{2,1,0:T(8,128)(2,1)} %all-to-all-done.1.k_ref.v_ref, s32[2]{0:T(128)} %get-tuple-element.19.slow_ref, ...), custom_call_target="tpu_custom_call" | custom-call | flops 12884901888 | bytes 8388608 | tf_op jit(solution)/shard_map/attend_last/pallas_call | solution.py:226
  194.2 7.8 %all-to-all-start.2 = ((bf16[32,72,128]{2,1,0:T(8,128)(2,1)}), bf16[32,72,128]{2,1,0:T(8,128)(2,1)}, u32[]{:S(2)}, u32[]{:S(2)}) async-start(bf16[32,72,128]{2,1,0:T(8,128)(2,1)} %attend_last.1), calls=%async_computation.2 | async-start | bytes 1179648 | tf_op jit(solution)/shard_map/all_to_all | solution.py:406
  202.1 10.3 %all-to-all-done.2.parts_ref = bf16[32,72,128]{2,1,0:T(8,128)(2,1)} async-done(((bf16[32,72,128]{2,1,0:T(8,128)(2,1)}), bf16[32,72,128]{2,1,0:T(8,128)(2,1)}, u32[]{:S(2)}, u32[]{:S(2)}) %all-to-all-start.2) | async-done | bytes 589856 | tf_op jit(solution)/shard_map/all_to_all | solution.py:406
  212.4 1.3 clean_rows.1
  213.7 9.7 %all-gather.1 = bf16[256,128]{1,0:T(8,128)(2,1)S(1)} all-gather(bf16[64,128]{1,0:T(8,128)(2,1)S(1)} %clean_rows.1), channel_id=3, replica_groups=mesh['grp'=4,'ctx'=32] {'grp'}, dimensions={0}, use_global_device_ids=true | all-gather | bytes 81920 | tf_op jit(solution)/shard_map/all_gather | solution.py:445
  223.5 5.9 %decode.1 = bf16[4096,128]{1,0:T(8,128)(2,1)} custom-call(s32[1]{0:T(128)} %bitcast.mine_ref, bf16[4,72,128]{2,1,0:T(8,128)(2,1)S(1)} %bitcast.63, bf16[4,64,128]{2,1,0:T(8,128)(2,1)S(1)} %bitcast.64, bf16[768,512]{1,0:T(8,128)(2,1)S(1)} %bitcast.62, f32[1,512]{1,0:T(1,128)S(1)} %bitcast.66, bf16[2,1024,512]{2,1,0:T(8,128)(2,1)S(1)} %pad_maximum_fusion.w_out_ref, ...), custom_call_target="tpu_custom_call" | custom-call | tf_op jit(solution)/shard_map/decode/pallas_call | solution.py:363
  (28 shorter events, 0.3 us)
Async XLA Ops:
  0.0 19.7 %copy-start = (bf16[4096,64]{0,1:T(8,128)(2,1)S(1)}, bf16[4096,64]{0,1:T(8,128)(2,1)}, u32[]{:S(2)}) copy-start(bf16[4096,64]{0,1:T(8,128)(2,1)} %param.22) | copy-start | bytes 1572868
  5.0 69.3 %all-to-all-start = ((bf16[32,512,128]{2,1,0:T(8,128)(2,1)}), bf16[32,512,128]{2,1,0:T(8,128)(2,1)}, u32[]{:S(2)}, u32[]{:S(2)}) async-start(bf16[32,512,128]{2,1,0:T(8,128)(2,1)} %pack_first.1), calls=%async_computation | async-start | bytes 8388608 | tf_op jit(solution)/shard_map/all_to_all | solution.py:406
  14.9 5.5 %copy-start.4 = (bf16[9,512,128]{2,1,0:T(8,128)(2,1)S(1)}, bf16[9,512,128]{2,1,0:T(8,128)(2,1)}, u32[]{:S(2)}) copy-start(bf16[9,512,128]{2,1,0:T(8,128)(2,1)} %param.26) | copy-start | bytes 3538948
  19.6 2.4 %copy-start.6 = (bf16[1,4,2,1024]{3,2,1,0:T(2,128)(2,1)S(1)}, bf16[1,4,2,1024]{3,2,1,0:T(2,128)(2,1)}, u32[]{:S(2)}) copy-start(bf16[1,4,2,1024]{3,2,1,0:T(2,128)(2,1)} %param.20) | copy-start | bytes 49156
  19.6 2.5 %copy-start.7 = (bf16[1,4,2,1024]{3,2,1,0:T(2,128)(2,1)S(1)}, bf16[1,4,2,1024]{3,2,1,0:T(2,128)(2,1)}, u32[]{:S(2)}) copy-start(bf16[1,4,2,1024]{3,2,1,0:T(2,128)(2,1)} %param.21) | copy-start | bytes 49156
  19.6 2.5 %copy-start.5 = (bf16[432,512]{1,0:T(8,128)(2,1)S(1)}, bf16[432,512]{1,0:T(8,128)(2,1)}, u32[]{:S(2)}) copy-start(bf16[432,512]{1,0:T(8,128)(2,1)} %param.24) | copy-start | bytes 1327108
  20.4 1.8 copy-start.8
  69.3 1.7 copy-start.3
  74.3 75.7 %all-to-all-start.1 = ((bf16[32,256,128]{2,1,0:T(8,128)(2,1)}), bf16[32,256,128]{2,1,0:T(8,128)(2,1)}, u32[]{:S(2)}, u32[]{:S(2)}) async-start(bf16[32,256,128]{2,1,0:T(8,128)(2,1)} %pack_window.1), calls=%async_computation.1 | async-start | bytes 4194304 | tf_op jit(solution)/shard_map/all_to_all | solution.py:406
  150.0 73.4 %copy-start.1 = (f32[512]{0:T(512)S(1)}, f32[512]{0:T(512)}, u32[]{:S(2)}) copy-start(f32[512]{0:T(512)} %param.25) | copy-start | bytes 6148
  150.0 73.4 %copy-start.2 = (f32[128]{0:T(128)S(1)}, f32[128]{0:T(128)}, u32[]{:S(2)}) copy-start(f32[128]{0:T(128)} %param.27) | copy-start | bytes 1540
  194.2 18.1 %all-to-all-start.2 = ((bf16[32,72,128]{2,1,0:T(8,128)(2,1)}), bf16[32,72,128]{2,1,0:T(8,128)(2,1)}, u32[]{:S(2)}, u32[]{:S(2)}) async-start(bf16[32,72,128]{2,1,0:T(8,128)(2,1)} %attend_last.1), calls=%async_computation.2 | async-start | bytes 1179648 | tf_op jit(solution)/shard_map/all_to_all | solution.py:406

commit v5 on v4

--- a/solution.py
+++ b/solution.py
@@ -16,6 +16,7 @@
 HEADS_STEP = 8
 BQ = 2048
 LIMIT = 110.0
+SPLIT = 4
 
 
 def params(mib, axes=1):
@@ -78,10 +79,12 @@
     )(pick, keys, values)
 
 
-def key_blocks(ref, step):
-    sources, rows = ref.shape[0], ref.shape[1]
+def key_blocks(refs, step):
+    rows = refs[0].shape[1]
     return [
-        ref[j : j + step].reshape(step * rows, HD) for j in range(0, sources, step)
+        ref[j : j + step].reshape(step * rows, HD)
+        for ref in refs
+        for j in range(0, ref.shape[0], step)
     ]
 
 
@@ -99,8 +102,8 @@
     return jnp.sum(x.reshape(x.shape[0] // 8, 8, x.shape[1]), axis=0)
 
 
-def attend_bounded(q, k_ref, v_ref, step, totals, acc):
-    keys, values = key_blocks(k_ref, step), key_blocks(v_ref, step)
+def attend_bounded(q, k_refs, v_refs, step, totals, acc):
+    keys, values = key_blocks(k_refs, step), key_blocks(v_refs, step)
     following = score(keys[0], q)
     for j in range(len(keys)):
         scores = following
@@ -113,27 +116,31 @@
     return totals, acc
 
 
-def attend_any(q, k_ref, v_ref, step, top_ref, totals_ref, acc_ref):
-    sources, rows = k_ref.shape[0], k_ref.shape[1]
-
-    def body(j, carry):
-        here = pl.ds(j * step, step)
-        scores = score(k_ref[here].reshape(step * rows, HD), q)
-        before = top_ref[0:1, :]
-        top = jnp.maximum(before, jnp.max(scores, axis=0, keepdims=True))
-        raised = jnp.exp2((scores - top) * SCALE)
-        fade = jnp.exp2((before - top) * SCALE)
-        mixed = mix(v_ref[here].reshape(step * rows, HD), raised)
-        acc_ref[...] = acc_ref[...] * fade + mixed
-        totals_ref[...] = totals_ref[...] * fade + fold_rows(raised)
-        top_ref[...] = jnp.broadcast_to(top, top_ref.shape)
-        return carry
-
-    lax.fori_loop(0, sources // step, body, 0)
-
-
-def bounded(q, k_ref):
-    widest = jnp.max(jnp.abs(k_ref[...].reshape(-1, HD)), axis=0, keepdims=True)
+def attend_any(q, k_refs, v_refs, step, top_ref, totals_ref, acc_ref):
+    for k_ref, v_ref in zip(k_refs, v_refs):
+        sources, rows = k_ref.shape[0], k_ref.shape[1]
+
+        def body(j, carry, k_ref=k_ref, v_ref=v_ref, rows=rows):
+            here = pl.ds(j * step, step)
+            scores = score(k_ref[here].reshape(step * rows, HD), q)
+            before = top_ref[0:1, :]
+            top = jnp.maximum(before, jnp.max(scores, axis=0, keepdims=True))
+            raised = jnp.exp2((scores - top) * SCALE)
+            fade = jnp.exp2((before - top) * SCALE)
+            mixed = mix(v_ref[here].reshape(step * rows, HD), raised)
+            acc_ref[...] = acc_ref[...] * fade + mixed
+            totals_ref[...] = totals_ref[...] * fade + fold_rows(raised)
+            top_ref[...] = jnp.broadcast_to(top, top_ref.shape)
+            return carry
+
+        lax.fori_loop(0, sources // step, body, 0)
+
+
+def bounded(q, k_refs):
+    widest = [jnp.max(jnp.abs(k[...].reshape(-1, HD)), axis=0, keepdims=True) for k in k_refs]
+    while len(widest) > 1:
+        widest = [jnp.maximum(*widest[:2])] + widest[2:]
+    widest = widest[0]
     reach = lax.dot_general(
         jnp.broadcast_to(widest, (16, HD)),
         jnp.abs(q),
@@ -143,11 +150,13 @@
     return jnp.max(reach) * (1.01 * SCALE) <= LIMIT
 
 
-def attend_first_kernel(q_ref, k_ref, v_ref, slow_ref, top_ref, totals_ref, acc_ref):
+def attend_first_kernel(q_ref, *refs):
+    k_refs, v_refs = refs[:SPLIT], refs[SPLIT : 2 * SPLIT]
+    slow_ref, top_ref, totals_ref, acc_ref = refs[2 * SPLIT :]
     q = q_ref[...].reshape(BQ, HD)
-    fits = bounded(q, k_ref)
+    fits = bounded(q, k_refs)
     top_ref[...] = jnp.zeros(top_ref.shape, F32)
-    totals_ref[...], acc_ref[...] = attend_bounded(q, k_ref, v_ref, 8, None, None)
+    totals_ref[...], acc_ref[...] = attend_bounded(q, k_refs, v_refs, 8, None, None)
     slow_ref[pl.program_id(0)] = jnp.where(fits, 0, 1)
 
     @pl.when(jnp.logical_not(fits))
@@ -155,17 +164,17 @@
         top_ref[...] = jnp.full(top_ref.shape, -1e30, F32)
         totals_ref[...] = jnp.zeros(totals_ref.shape, F32)
         acc_ref[...] = jnp.zeros(acc_ref.shape, F32)
-        attend_any(q, k_ref, v_ref, 4, top_ref, totals_ref, acc_ref)
-
-
-def attend_last_kernel(
-    q_ref, k_ref, v_ref, slow_ref, top_in_ref, totals_in_ref, acc_in_ref, weight_ref,
-    out_ref, top_ref, totals_ref, acc_ref,
-):
+        attend_any(q, k_refs, v_refs, 4, top_ref, totals_ref, acc_ref)
+
+
+def attend_last_kernel(q_ref, *refs):
+    k_refs, v_refs = refs[:SPLIT], refs[SPLIT : 2 * SPLIT]
+    slow_ref, top_in_ref, totals_in_ref, acc_in_ref, weight_ref = refs[2 * SPLIT : 2 * SPLIT + 5]
+    out_ref, top_ref, totals_ref, acc_ref = refs[2 * SPLIT + 5 :]
     q = q_ref[...].reshape(BQ, HD)
-    fits = bounded(q, k_ref) & (slow_ref[pl.program_id(0)] == 0)
+    fits = bounded(q, k_refs) & (slow_ref[pl.program_id(0)] == 0)
     totals_ref[...], acc_ref[...] = attend_bounded(
-        q, k_ref, v_ref, 8, totals_in_ref[...], acc_in_ref[...]
+        q, k_refs, v_refs, 8, totals_in_ref[...], acc_in_ref[...]
     )
 
     @pl.when(jnp.logical_not(fits))
@@ -173,7 +182,7 @@
         top_ref[...] = top_in_ref[...]
         totals_ref[...] = totals_in_ref[...]
         acc_ref[...] = acc_in_ref[...]
-        attend_any(q, k_ref, v_ref, 8, top_ref, totals_ref, acc_ref)
+        attend_any(q, k_refs, v_refs, 8, top_ref, totals_ref, acc_ref)
 
     totals = jnp.sum(totals_ref[...], axis=0, keepdims=True)
     attended = (acc_ref[...] / totals).astype(BF16)
@@ -192,8 +201,11 @@
     blocks = BQ // TOK
     steps = total // BQ
     q_spec = pl.BlockSpec((blocks, TOK, HD), lambda i: (i, 3, 0))
-    k_spec = pl.BlockSpec((HEADS, k_rows, HD), lambda i: (0, 0, 0))
-    v_spec = pl.BlockSpec((HEADS, k_rows, HD), lambda i: (0, 1, 0))
+    kv_specs = [
+        pl.BlockSpec((HEADS // SPLIT, k_rows, HD), lambda i, part=part, place=place: (part, place, 0))
+        for place in range(2)
+        for part in range(SPLIT)
+    ]
     state_specs = [
         pl.BlockSpec(memory_space=pltpu.SMEM),
         pl.BlockSpec((8, BQ), lambda i: (0, i)),
@@ -206,9 +218,9 @@
         jax.ShapeDtypeStruct((8, total), F32),
         jax.ShapeDtypeStruct((HD, total), F32),
     ]
-    in_specs = [q_spec, k_spec, v_spec]
+    in_specs = [q_spec] + kv_specs
     scratch = []
-    args = (queries, keys_values, keys_values)
+    args = (queries,) + (keys_values,) * (2 * SPLIT)
     if kind == "first":
         body, out_specs, out_shape = attend_first_kernel, state_specs, state_shapes
     else:
@@ -240,9 +252,11 @@
     )(*args)
 
 
-def clean_kernel(parts_ref, noisy_ref, out_ref, token_ref):
+def clean_kernel(*refs):
+    parts, (noisy_ref, prev_ref, out_ref, token_ref) = refs[:SPLIT], refs[SPLIT:]
     width = HEADS * HD
-    sums = jnp.sum(parts_ref[...].astype(F32), axis=0)
+    sums = [jnp.sum(part[...].astype(F32), axis=0) for part in parts]
+    sums = (sums[0] + sums[1]) + (sums[2] + sums[3])
     scale = 1.0 / jnp.sqrt(sums[64:65] * (1.0 / width) + 1e-06)
     velocity = sums[0:64] * scale
     velocity = jnp.concatenate([velocity, jnp.zeros((64, HD), F32)], axis=0)
@@ -257,19 +271,25 @@
             moved = jnp.where(lane // 32 == px, piece, moved)
         rows = slice(i * 32, i * 32 + 32)
         out_ref[rows, :] = (noisy_ref[rows, :].astype(F32) - moved).astype(BF16)
-
-
-def clean_rows(parts, noisy):
-    vmem = pl.BlockSpec(memory_space=pltpu.VMEM)
+    out_ref[64:136, :] = prev_ref[...]
+
+
+def clean_rows(parts, noisy, prev):
+    part_specs = [
+        pl.BlockSpec((HEADS // SPLIT, 72, HD), lambda i, part=part: (part, 0, 0))
+        for part in range(SPLIT)
+    ]
     return pl.pallas_call(
         clean_kernel,
-        in_specs=[vmem, vmem],
-        out_specs=vmem,
-        out_shape=jax.ShapeDtypeStruct((64, HD), BF16),
+        grid=(1,),
+        in_specs=part_specs
+        + [pl.BlockSpec((64, HD), lambda i: (0, 0)), pl.BlockSpec((72, HD), lambda i: (0, 0))],
+        out_specs=pl.BlockSpec((136, HD), lambda i: (0, 0)),
+        out_shape=jax.ShapeDtypeStruct((136, HD), BF16),
         scratch_shapes=[pltpu.VMEM((HD, HD), F32)],
-        compiler_params=pltpu.CompilerParams(vmem_limit_bytes=16 << 20),
+        compiler_params=params(16),
         name="clean_rows",
-    )(parts, noisy)
+    )(*(parts,) * SPLIT, noisy, prev)
 
 
 def shift_rows(x, by):
@@ -279,15 +299,15 @@
 
 
 def decode_kernel(
-    mine_ref, prev_ref, clean_ref, w_in_ref, b_in_ref, w_out_ref, b_out_ref,
-    out_ref, latent_ref, column_ref, part_ref, wide_ref,
+    mine_ref, in_ref, w_in_ref, b_in_ref, w_out_ref, b_out_ref,
+    out_hbm, latent_ref, column_ref, part_ref, wide_ref, out_ref, out_sem,
 ):
     tiles = 8
     mine = mine_ref[0].astype(F32)
     flags = []
     for sender in range(4):
-        old = prev_ref[sender].astype(F32)
-        new = clean_ref[sender].astype(F32)
+        new = in_ref[sender, 0:64, :].astype(F32)
+        old = in_ref[sender, 64:136, :].astype(F32)
         owners = [old[64 + t : 65 + t] for t in range(4)]
         ranks = []
         for t in range(4):
@@ -353,27 +373,37 @@
                 second = second + part_ref[at + TOK : at + 2 * TOK, 384:512]
             wide_ref[pl.ds(a * 16 + 2 * x, TOK, stride=32), :] = first
             wide_ref[pl.ds(a * 16 + 2 * x + 1, TOK, stride=32), :] = second
+    copies = []
     for tile in range(tiles):
         rows = slice(tile * 512, tile * 512 + 512)
         out_ref[rows, :] = jnp.where(flags[tile] > 0.5, wide_ref[rows, :], 0.0).astype(BF16)
-
-
-def decode(mine, prev, clean, w_in, b_in, w_out, b_out):
+        here = pl.ds(tile * 512, 512)
+        copies.append(
+            pltpu.make_async_copy(out_ref.at[here], out_hbm.at[here], out_sem.at[tile])
+        )
+        copies[tile].start()
+    for copy in copies:
+        copy.wait()
+
+
+def decode(mine, arrived, w_in, b_in, w_out, b_out):
     vmem = pl.BlockSpec(memory_space=pltpu.VMEM)
     return pl.pallas_call(
         decode_kernel,
-        in_specs=[pl.BlockSpec(memory_space=pltpu.SMEM)] + [vmem] * 6,
-        out_specs=vmem,
+        in_specs=[pl.BlockSpec(memory_space=pltpu.SMEM)] + [vmem] * 5,
+        out_specs=pl.BlockSpec(memory_space=pltpu.HBM),
         out_shape=jax.ShapeDtypeStruct((8 * 512, HD), BF16),
         scratch_shapes=[
             pltpu.VMEM((256, HD), F32),
             pltpu.VMEM((8 * TOK, 768), BF16),
             pltpu.VMEM((8 * TOK, 512), F32),
             pltpu.VMEM((8 * 512, HD), F32),
+            pltpu.VMEM((8 * 512, HD), BF16),
+            pltpu.SemaphoreType.DMA((8,)),
         ],
         compiler_params=pltpu.CompilerParams(vmem_limit_bytes=48 << 20),
         name="decode",
-    )(mine, prev, clean, w_in, b_in, w_out, b_out)
+    )(mine, arrived, w_in, b_in, w_out, b_out)
 
 
 def head_weight(velocity_weight):
@@ -433,7 +463,6 @@
     owners = jnp.broadcast_to(tile_owner[0].astype(BF16)[:, None], (4, HD))
     owners = jnp.pad(owners, ((0, 4), (0, 0)))
     prev = jnp.concatenate([latent_rows(prev_latent[0]), owners], axis=0)
-    prev = lax.all_gather(prev, "grp", axis=0)
 
     clip, window, weight, w_in, w_out, noisy, prev = lax.optimization_barrier(
         (clip, window, weight, w_in, w_out, noisy, prev)
@@ -442,10 +471,10 @@
     state = attend("first", clip, clip, 192)
     parts = attend("last", clip, window, TOK, state, weight)
     parts = exchange(parts, "ctx")
-    clean = lax.all_gather(clean_rows(parts, noisy), "grp", axis=0)
+    arrived = lax.all_gather(clean_rows(parts, noisy, prev), "grp", axis=0)
     mine = lax.axis_index("grp").reshape(1)
     decoded = decode(
-        mine, prev, clean, w_in, conv_in_bias.reshape(1, -1), w_out, conv_out_bias.reshape(1, -1)
+        mine, arrived, w_in, conv_in_bias.reshape(1, -1), w_out, conv_out_bias.reshape(1, -1)
     )
     return decoded.reshape(1, 1, 4, 2, 2, 256, 128)
 

time: 230 us -> 234 us (1.017); the launches traced: 229 us -> 230 us
  blocking collectives: 54.9 us -> 9.89 us
  waiting for transfers between devices: 10.3 us -> 53.4 us
  Pallas kernels: 126 us -> 136 us
  starting transfers between devices: 28.7 us -> 23.1 us
    all_gather x2 -> x1, blocking collectives: 54.9 us -> 9.89 us  [local(): arrived = lax.all_gather(clean_rows(parts, noisy, prev), 'grp', axis=0)]
    all_to_all x3, waiting for transfers between devices: 10.3 us -> 53.4 us  [exchange(): return lax.all_to_all(x, axis, split_axis=0, concat_axis=0, tiled=True)]
    pallas_call x2, Pallas kernels: 109 us -> 120 us  [attend(): pl.pallas_call(body, grid=(steps,), in_specs=in_specs, out_specs=out_spec...]
    all_to_all x3, starting transfers between devices: 28.7 us -> 23.1 us  [exchange(): return lax.all_to_all(x, axis, split_axis=0, concat_axis=0, tiled=True)]
  transfers between devices with their start and end apart: 3 -> 3, of which waited for: 1 -> 2; matrix products, arithmetic and copies ran while one was open for 3% -> 3% of each run, Pallas kernels for 30% -> 36%
where the time goes in v5:
time: 234 us; the launch traced here: 230 us
  Pallas kernels  136 us (58%)
  waiting for transfers between devices  53.4 us (23%)
  starting transfers between devices  23.1 us (10%)
  blocking collectives  9.89 us (4%)
  other arithmetic  5.11 us (2%)
    pallas_call x2, Pallas kernels, attend(): pl.pallas_call(body, grid=(steps,), in_specs=in_specs, out_specs=out_spec...  120 us
    all_to_all x3, waiting for transfers between devices, exchange(): return lax.all_to_all(x, axis, split_axis=0, concat_axis=0, tiled=True)  53.4 us
    all_to_all x3, starting transfers between devices, exchange(): return lax.all_to_all(x, axis, split_axis=0, concat_axis=0, tiled=True)  23.1 us
    all_gather x1, blocking collectives, local(): arrived = lax.all_gather(clean_rows(parts, noisy, prev), 'grp', axis=0)  9.89 us
    pallas_call x1, Pallas kernels, decode(): pl.pallas_call(decode_kernel, in_specs=[pl.BlockSpec(memory_space=pltpu.S...  5.77 us
    pallas_call x1, Pallas kernels, pack_first(): pl.pallas_call(pack_first_kernel, grid_spec=pltpu.PrefetchScalarGridSpec(...  5.02 us
  transfers between devices with their start and end apart: 3, of which 2 were waited for; matrix products, arithmetic and copies ran while one was open for 3% of the time, Pallas kernels for 36%

profile of v5, /device:TPU:1, one launch (start us, length us, event | category | flops | bytes accessed | tf_op | source)
XLA Modules:
  0.0 229.8 jit_solution(4006338203889942382)
XLA Ops:
  0.0 5.0 %pack_first.1 = bf16[32,512,128]{2,1,0:T(8,128)(2,1)} custom-call(s32[2]{0:T(128)} %bitcast.78, bf16[128,4096]{1,0:T(8,128)(2,1)} %bitcast.73, bf16[128,4096]{1,0:T(8,128)(2,1)} %bitcast.74, bf16[128,4096]{1,0:T(8,128)(2,1)} %bitcast.75, bf16[4,128,4096]{2,1,0:T(8,128)(2,1)} %bitcast.69, bf16[4,128,4096]{2,1,0:T(8,128)(2,1)} %bitcast.71), custom_call_target="tpu_custom_call" | custom-call | tf_op jit(solution)/shard_map/pack_first/pallas_call | solution.py:45
  5.0 9.9 %all-to-all-start = ((bf16[32,512,128]{2,1,0:T(8,128)(2,1)}), bf16[32,512,128]{2,1,0:T(8,128)(2,1)}, u32[]{:S(2)}, u32[]{:S(2)}) async-start(bf16[32,512,128]{2,1,0:T(8,128)(2,1)} %pack_first.1), calls=%async_computation | async-start | bytes 8388608 | tf_op jit(solution)/shard_map/all_to_all | solution.py:436
  14.9 4.7 %pack_window.1 = bf16[32,256,128]{2,1,0:T(8,128)(2,1)} custom-call(s32[2]{0:T(128)} %bitcast.79, bf16[4,128,4096]{2,1,0:T(8,128)(2,1)} %bitcast.70, bf16[4,128,4096]{2,1,0:T(8,128)(2,1)} %bitcast.72), custom_call_target="tpu_custom_call" | custom-call | tf_op jit(solution)/shard_map/pack_window/pallas_call | solution.py:68
  19.6 0.7 copy.18.refs_12_
  20.3 1.5 convert_element_type.21
  21.9 1.0 pad.10
  22.9 0.1 compare_select_fusion
  22.9 0.1 fusion.1
  23.3 0.1 fusion.2
  23.3 0.1 fusion.10
  23.4 3.0 %maximum_bitcast_fusion = (bf16[1,1024,512]{2,1,0:T(8,128)(2,1)S(1)}, bf16[1,1024,512]{2,1,0:T(8,128)(2,1)S(1)}) fusion(bf16[512,128]{1,0:T(8,128)(2,1)S(1)} %get-tuple-element.38, bf16[512,128]{1,0:T(8,128)(2,1)S(1)} %get-tuple-element.40, bf16[512,128]{1,0:T(8,128)(2,1)S(1)} %get-tuple-element.39, bf16[512,128]{1,0:T(8,128)(2,1)S(1)} %get-tuple-element.37, ...), kind=kLoop, calls=%fused_computation.1 | loop fusion | flops 16777216 | bytes 4194304 | tf_op jit(solution)/shard_map/stack | solution.py:428
  26.4 0.2 pad_maximum_fusion.w_out_ref
  26.6 0.1 pad_maximum_fusion.1.refs_5_
  26.7 43.3 %all-to-all-done.q_ref.refs_0_.refs_1_.refs_2_.refs_3_.refs_4_.refs_5_.refs_6_.refs_7_ = bf16[32,512,128]{2,1,0:T(8,128)(2,1)} async-done(((bf16[32,512,128]{2,1,0:T(8,128)(2,1)}), bf16[32,512,128]{2,1,0:T(8,128)(2,1)}, u32[]{:S(2)}, u32[]{:S(2)}) %all-to-all-start) | async-done | bytes 4194336 | tf_op jit(solution)/shard_map/all_to_all | solution.py:436
  70.0 5.6 %all-to-all-start.1 = ((bf16[32,256,128]{2,1,0:T(8,128)(2,1)}), bf16[32,256,128]{2,1,0:T(8,128)(2,1)}, u32[]{:S(2)}, u32[]{:S(2)}) async-start(bf16[32,256,128]{2,1,0:T(8,128)(2,1)} %pack_window.1), calls=%async_computation.1 | async-start | bytes 4194304 | tf_op jit(solution)/shard_map/all_to_all | solution.py:436
  75.6 77.7 %attend_first.1 = (s32[2]{0:T(128)}, f32[8,4096]{1,0:T(8,128)}, f32[8,4096]{1,0:T(8,128)}, f32[128,4096]{1,0:T(8,128)}) custom-call(bf16[32,512,128]{2,1,0:T(8,128)(2,1)} %all-to-all-done.q_ref.refs_0_.refs_1_.refs_2_.refs_3_.refs_4_.refs_5_.refs_6_.refs_7_, ...), custom_call_target="tpu_custom_call" | custom-call | flops 19327352832 | bytes 8388608 | tf_op jit(solution)/shard_map/attend_first/pallas_call | solution.py:238
  153.3 42.5 %attend_last.1 = bf16[32,72,128]{2,1,0:T(8,128)(2,1)} custom-call(bf16[32,512,128]{2,1,0:T(8,128)(2,1)} %all-to-all-done.q_ref.refs_0_.refs_1_.refs_2_.refs_3_.refs_4_.refs_5_.refs_6_.refs_7_, bf16[32,256,128]{2,1,0:T(8,128)(2,1)} %all-to-all-done.1.refs_0_.refs_1_.refs_2_.refs_3_.refs_4_.refs_5_.refs_6_.refs_7_, ...), custom_call_target="tpu_custom_call" | custom-call | flops 12884901888 | bytes 8388608 | tf_op jit(solution)/shard_map/attend_last/pallas_call | solution.py:238
  195.8 0.0 copy-start.2
  195.8 0.0 copy-start.3
  195.8 7.7 %all-to-all-start.2 = ((bf16[32,72,128]{2,1,0:T(8,128)(2,1)}), bf16[32,72,128]{2,1,0:T(8,128)(2,1)S(1)}, u32[]{:S(2)}, u32[]{:S(2)}) async-start(bf16[32,72,128]{2,1,0:T(8,128)(2,1)} %attend_last.1), calls=%async_computation.2 | async-start | bytes 1179648 | tf_op jit(solution)/shard_map/all_to_all | solution.py:436
  203.5 10.1 %all-to-all-done.2.refs_0_.refs_1_.refs_2_.refs_3_ = bf16[32,72,128]{2,1,0:T(8,128)(2,1)S(1)} async-done(((bf16[32,72,128]{2,1,0:T(8,128)(2,1)}), bf16[32,72,128]{2,1,0:T(8,128)(2,1)S(1)}, u32[]{:S(2)}, u32[]{:S(2)}) %all-to-all-start.2) | async-done | bytes 589856 | tf_op jit(solution)/shard_map/all_to_all | solution.py:436
  213.6 0.3 clean_rows.1
  213.9 9.9 %all-gather = bf16[544,128]{1,0:T(8,128)(2,1)S(1)} all-gather(bf16[136,128]{1,0:T(8,128)(2,1)S(1)} %clean_rows.1), channel_id=2, replica_groups=mesh['grp'=4,'ctx'=32] {'grp'}, dimensions={0}, use_global_device_ids=true | all-gather | bytes 174080 | tf_op jit(solution)/shard_map/all_gather | solution.py:474
  223.8 5.8 %decode.1 = bf16[4096,128]{1,0:T(8,128)(2,1)} custom-call(s32[1]{0:T(128)} %bitcast.mine_ref, bf16[4,136,128]{2,1,0:T(8,128)(2,1)S(1)} %bitcast.63, bf16[768,512]{1,0:T(8,128)(2,1)S(1)} %bitcast.62, f32[1,512]{1,0:T(1,128)S(1)} %bitcast.65, bf16[2,1024,512]{2,1,0:T(8,128)(2,1)S(1)} %pad_maximum_fusion.w_out_ref, f32[1,128]{1,0:T(1,128)S(1)} %bitcast.66), custom_call_target="tpu_custom_call" | custom-call | tf_op jit(solution)/shard_map/decode/pallas_call | solution.py:391
  (25 shorter events, 0.3 us)
Async XLA Ops:
  0.0 19.6 %copy-start = (bf16[4096,64]{0,1:T(8,128)(2,1)S(1)}, bf16[4096,64]{0,1:T(8,128)(2,1)}, u32[]{:S(2)}) copy-start(bf16[4096,64]{0,1:T(8,128)(2,1)} %param.22) | copy-start | bytes 1572868
  5.0 65.0 %all-to-all-start = ((bf16[32,512,128]{2,1,0:T(8,128)(2,1)}), bf16[32,512,128]{2,1,0:T(8,128)(2,1)}, u32[]{:S(2)}, u32[]{:S(2)}) async-start(bf16[32,512,128]{2,1,0:T(8,128)(2,1)} %pack_first.1), calls=%async_computation | async-start | bytes 8388608 | tf_op jit(solution)/shard_map/all_to_all | solution.py:436
  19.5 2.2 copy-start.5
  19.5 2.3 copy-start.6
  19.5 2.3 %copy-start.4 = (bf16[432,512]{1,0:T(8,128)(2,1)S(1)}, bf16[432,512]{1,0:T(8,128)(2,1)}, u32[]{:S(2)}) copy-start(bf16[432,512]{1,0:T(8,128)(2,1)} %param.24) | copy-start | bytes 1327108
  20.3 2.5 %copy-start.7 = (s32[1,4]{1,0:T(1,128)S(1)}, s32[1,4]{1,0:T(1,128)}, u32[]{:S(2)}) copy-start(s32[1,4]{1,0:T(1,128)} %param.23) | copy-start | bytes 52
  70.0 83.3 %all-to-all-start.1 = ((bf16[32,256,128]{2,1,0:T(8,128)(2,1)}), bf16[32,256,128]{2,1,0:T(8,128)(2,1)}, u32[]{:S(2)}, u32[]{:S(2)}) async-start(bf16[32,256,128]{2,1,0:T(8,128)(2,1)} %pack_window.1), calls=%async_computation.1 | async-start | bytes 4194304 | tf_op jit(solution)/shard_map/all_to_all | solution.py:436
  195.8 27.9 %copy-start.2 = (f32[512]{0:T(512)S(1)}, f32[512]{0:T(512)}, u32[]{:S(2)}) copy-start(f32[512]{0:T(512)} %param.25) | copy-start | bytes 6148
  195.8 27.9 %copy-start.3 = (f32[128]{0:T(128)S(1)}, f32[128]{0:T(128)}, u32[]{:S(2)}) copy-start(f32[128]{0:T(128)} %param.27) | copy-start | bytes 1540
  195.8 17.7 %all-to-all-start.2 = ((bf16[32,72,128]{2,1,0:T(8,128)(2,1)}), bf16[32,72,128]{2,1,0:T(8,128)(2,1)S(1)}, u32[]{:S(2)}, u32[]{:S(2)}) async-start(bf16[32,72,128]{2,1,0:T(8,128)(2,1)} %attend_last.1), calls=%async_computation.2 | async-start | bytes 1179648 | tf_op jit(solution)/shard_map/all_to_all | solution.py:436
  213.6 10.2 %copy-start.1 = (bf16[3,4,64,512]{3,2,1,0:T(8,128)(2,1)S(1)}, bf16[3,4,64,512]{3,2,1,0:T(8,128)(2,1)}, u32[]{:S(2)}) copy-start(bf16[3,4,64,512]{3,2,1,0:T(8,128)(2,1)} %pad.10) | copy-start | bytes 2359300

commit v6 on v5

--- a/solution.py
+++ b/solution.py
@@ -17,6 +17,7 @@
 BQ = 2048
 LIMIT = 110.0
 SPLIT = 4
+KV_SPLIT = 1
 
 
 def params(mib, axes=1):
@@ -151,8 +152,8 @@
 
 
 def attend_first_kernel(q_ref, *refs):
-    k_refs, v_refs = refs[:SPLIT], refs[SPLIT : 2 * SPLIT]
-    slow_ref, top_ref, totals_ref, acc_ref = refs[2 * SPLIT :]
+    k_refs, v_refs = refs[:KV_SPLIT], refs[KV_SPLIT : 2 * KV_SPLIT]
+    slow_ref, top_ref, totals_ref, acc_ref = refs[2 * KV_SPLIT :]
     q = q_ref[...].reshape(BQ, HD)
     fits = bounded(q, k_refs)
     top_ref[...] = jnp.zeros(top_ref.shape, F32)
@@ -168,9 +169,9 @@
 
 
 def attend_last_kernel(q_ref, *refs):
-    k_refs, v_refs = refs[:SPLIT], refs[SPLIT : 2 * SPLIT]
-    slow_ref, top_in_ref, totals_in_ref, acc_in_ref, weight_ref = refs[2 * SPLIT : 2 * SPLIT + 5]
-    out_ref, top_ref, totals_ref, acc_ref = refs[2 * SPLIT + 5 :]
+    k_refs, v_refs = refs[:KV_SPLIT], refs[KV_SPLIT : 2 * KV_SPLIT]
+    slow_ref, top_in_ref, totals_in_ref, acc_in_ref, weight_ref = refs[2 * KV_SPLIT : 2 * KV_SPLIT + 5]
+    out_ref, top_ref, totals_ref, acc_ref = refs[2 * KV_SPLIT + 5 :]
     q = q_ref[...].reshape(BQ, HD)
     fits = bounded(q, k_refs) & (slow_ref[pl.program_id(0)] == 0)
     totals_ref[...], acc_ref[...] = attend_bounded(
@@ -202,9 +203,9 @@
     steps = total // BQ
     q_spec = pl.BlockSpec((blocks, TOK, HD), lambda i: (i, 3, 0))
     kv_specs = [
-        pl.BlockSpec((HEADS // SPLIT, k_rows, HD), lambda i, part=part, place=place: (part, place, 0))
+        pl.BlockSpec((HEADS // KV_SPLIT, k_rows, HD), lambda i, part=part, place=place: (part, place, 0))
         for place in range(2)
-        for part in range(SPLIT)
+        for part in range(KV_SPLIT)
     ]
     state_specs = [
         pl.BlockSpec(memory_space=pltpu.SMEM),
@@ -220,7 +221,7 @@
     ]
     in_specs = [q_spec] + kv_specs
     scratch = []
-    args = (queries,) + (keys_values,) * (2 * SPLIT)
+    args = (queries,) + (keys_values,) * (2 * KV_SPLIT)
     if kind == "first":
         body, out_specs, out_shape = attend_first_kernel, state_specs, state_shapes
     else:

time: 234 us -> 219 us (0.936); the launches traced: 230 us -> 218 us
  Pallas kernels: 136 us -> 124 us
    pallas_call x2, Pallas kernels: 120 us -> 108 us  [attend(): pl.pallas_call(body, grid=(steps,), in_specs=in_specs, out_specs=out_spec...]
  transfers between devices with their start and end apart: 3 -> 3, of which waited for: 2 -> 2; matrix products, arithmetic and copies ran while one was open for 3% -> 3% of each run, Pallas kernels for 36% -> 32%
where the time goes in v6:
time: 219 us; the launch traced here: 218 us
  Pallas kernels  124 us (57%)
  waiting for transfers between devices  53.4 us (24%)
  starting transfers between devices  23.2 us (11%)
  blocking collectives  10.1 us (5%)
  other arithmetic  5.11 us (2%)
    pallas_call x2, Pallas kernels, attend(): pl.pallas_call(body, grid=(steps,), in_specs=in_specs, out_specs=out_spec...  108 us
    all_to_all x3, waiting for transfers between devices, exchange(): return lax.all_to_all(x, axis, split_axis=0, concat_axis=0, tiled=True)  53.4 us
    all_to_all x3, starting transfers between devices, exchange(): return lax.all_to_all(x, axis, split_axis=0, concat_axis=0, tiled=True)  23.2 us
    all_gather x1, blocking collectives, local(): arrived = lax.all_gather(clean_rows(parts, noisy, prev), 'grp', axis=0)  10.1 us
    pallas_call x1, Pallas kernels, decode(): pl.pallas_call(decode_kernel, in_specs=[pl.BlockSpec(memory_space=pltpu.S...  5.77 us
    pallas_call x1, Pallas kernels, pack_first(): pl.pallas_call(pack_first_kernel, grid_spec=pltpu.PrefetchScalarGridSpec(...  5.02 us
    pallas_call x1, Pallas kernels, pack_window(): pl.pallas_call(pack_window_kernel, grid_spec=pltpu.PrefetchScalarGridSpec...  4.65 us
  transfers between devices with their start and end apart: 3, of which 2 were waited for; matrix products, arithmetic and copies ran while one was open for 3% of the time, Pallas kernels for 32%

profile of v6, /device:TPU:1, one launch (start us, length us, event | category | flops | bytes accessed | tf_op | source)
XLA Modules:
  0.0 218.4 jit_solution(6134010247739570826)
XLA Ops:
  0.0 5.0 %pack_first.1 = bf16[32,512,128]{2,1,0:T(8,128)(2,1)} custom-call(s32[2]{0:T(128)} %bitcast.78, bf16[128,4096]{1,0:T(8,128)(2,1)} %bitcast.73, bf16[128,4096]{1,0:T(8,128)(2,1)} %bitcast.74, bf16[128,4096]{1,0:T(8,128)(2,1)} %bitcast.75, bf16[4,128,4096]{2,1,0:T(8,128)(2,1)} %bitcast.69, bf16[4,128,4096]{2,1,0:T(8,128)(2,1)} %bitcast.71), custom_call_target="tpu_custom_call" | custom-call | tf_op jit(solution)/shard_map/pack_first/pallas_call | solution.py:46
  5.0 9.9 %all-to-all-start = ((bf16[32,512,128]{2,1,0:T(8,128)(2,1)}), bf16[32,512,128]{2,1,0:T(8,128)(2,1)}, u32[]{:S(2)}, u32[]{:S(2)}) async-start(bf16[32,512,128]{2,1,0:T(8,128)(2,1)} %pack_first.1), calls=%async_computation | async-start | bytes 8388608 | tf_op jit(solution)/shard_map/all_to_all | solution.py:437
  14.9 4.7 %pack_window.1 = bf16[32,256,128]{2,1,0:T(8,128)(2,1)} custom-call(s32[2]{0:T(128)} %bitcast.79, bf16[4,128,4096]{2,1,0:T(8,128)(2,1)} %bitcast.70, bf16[4,128,4096]{2,1,0:T(8,128)(2,1)} %bitcast.72), custom_call_target="tpu_custom_call" | custom-call | tf_op jit(solution)/shard_map/pack_window/pallas_call | solution.py:69
  19.6 0.7 copy.18.refs_6_
  20.3 1.5 convert_element_type.21
  21.9 0.0 copy-done.4
  21.9 1.0 pad.10
  22.9 0.1 compare_select_fusion
  22.9 0.1 fusion.1
  23.3 0.1 fusion.2
  23.3 0.1 fusion.10
  23.4 3.0 %maximum_bitcast_fusion = (bf16[1,1024,512]{2,1,0:T(8,128)(2,1)S(1)}, bf16[1,1024,512]{2,1,0:T(8,128)(2,1)S(1)}) fusion(bf16[512,128]{1,0:T(8,128)(2,1)S(1)} %get-tuple-element.38, bf16[512,128]{1,0:T(8,128)(2,1)S(1)} %get-tuple-element.40, bf16[512,128]{1,0:T(8,128)(2,1)S(1)} %get-tuple-element.39, bf16[512,128]{1,0:T(8,128)(2,1)S(1)} %get-tuple-element.37, ...), kind=kLoop, calls=%fused_computation.1 | loop fusion | flops 16777216 | bytes 4194304 | tf_op jit(solution)/shard_map/stack | solution.py:429
  26.4 0.2 pad_maximum_fusion.w_out_ref
  26.6 0.1 pad_maximum_fusion.1.refs_5_
  26.7 43.3 %all-to-all-done.q_ref.refs_0_.refs_1_ = bf16[32,512,128]{2,1,0:T(8,128)(2,1)} async-done(((bf16[32,512,128]{2,1,0:T(8,128)(2,1)}), bf16[32,512,128]{2,1,0:T(8,128)(2,1)}, u32[]{:S(2)}, u32[]{:S(2)}) %all-to-all-start) | async-done | bytes 4194336 | tf_op jit(solution)/shard_map/all_to_all | solution.py:437
  70.0 5.6 %all-to-all-start.1 = ((bf16[32,256,128]{2,1,0:T(8,128)(2,1)}), bf16[32,256,128]{2,1,0:T(8,128)(2,1)}, u32[]{:S(2)}, u32[]{:S(2)}) async-start(bf16[32,256,128]{2,1,0:T(8,128)(2,1)} %pack_window.1), calls=%async_computation.1 | async-start | bytes 4194304 | tf_op jit(solution)/shard_map/all_to_all | solution.py:437
  75.6 64.4 %attend_first.1 = (s32[2]{0:T(128)}, f32[8,4096]{1,0:T(8,128)}, f32[8,4096]{1,0:T(8,128)}, f32[128,4096]{1,0:T(8,128)}) custom-call(bf16[32,512,128]{2,1,0:T(8,128)(2,1)} %all-to-all-done.q_ref.refs_0_.refs_1_, bf16[32,512,128]{2,1,0:T(8,128)(2,1)} %all-to-all-done.q_ref.refs_0_.refs_1_, bf16[32,512,128]{2,1,0:T(8,128)(2,1)} %all-to-all-done.q_ref.refs_0_.refs_1_), custom_call_target="tpu_custom_call" | custom-call | flops 19327352832 | bytes 8388608 | tf_op jit(solution)/shard_map/attend_first/pallas_call | solution.py:239
  140.0 0.0 all-to-all-done.1.refs_0_.refs_1_
  140.0 44.1 %attend_last.1 = bf16[32,72,128]{2,1,0:T(8,128)(2,1)} custom-call(bf16[32,512,128]{2,1,0:T(8,128)(2,1)} %all-to-all-done.q_ref.refs_0_.refs_1_, bf16[32,256,128]{2,1,0:T(8,128)(2,1)} %all-to-all-done.1.refs_0_.refs_1_, bf16[32,256,128]{2,1,0:T(8,128)(2,1)} %all-to-all-done.1.refs_0_.refs_1_, s32[2]{0:T(128)} %get-tuple-element.18.refs_2_, ...), custom_call_target="tpu_custom_call" | custom-call | flops 12884901888 | bytes 8388608 | tf_op jit(solution)/shard_map/attend_last/pallas_call | solution.py:239
  184.1 7.8 %all-to-all-start.2 = ((bf16[32,72,128]{2,1,0:T(8,128)(2,1)}), bf16[32,72,128]{2,1,0:T(8,128)(2,1)S(1)}, u32[]{:S(2)}, u32[]{:S(2)}) async-start(bf16[32,72,128]{2,1,0:T(8,128)(2,1)} %attend_last.1), calls=%async_computation.2 | async-start | bytes 1179648 | tf_op jit(solution)/shard_map/all_to_all | solution.py:437
  191.9 10.1 %all-to-all-done.2.refs_0_.refs_1_.refs_2_.refs_3_ = bf16[32,72,128]{2,1,0:T(8,128)(2,1)S(1)} async-done(((bf16[32,72,128]{2,1,0:T(8,128)(2,1)}), bf16[32,72,128]{2,1,0:T(8,128)(2,1)S(1)}, u32[]{:S(2)}, u32[]{:S(2)}) %all-to-all-start.2) | async-done | bytes 589856 | tf_op jit(solution)/shard_map/all_to_all | solution.py:437
  202.0 0.3 clean_rows.1
  202.3 10.1 %all-gather = bf16[544,128]{1,0:T(8,128)(2,1)S(1)} all-gather(bf16[136,128]{1,0:T(8,128)(2,1)S(1)} %clean_rows.1), channel_id=2, replica_groups=mesh['grp'=4,'ctx'=32] {'grp'}, dimensions={0}, use_global_device_ids=true | all-gather | bytes 174080 | tf_op jit(solution)/shard_map/all_gather | solution.py:475
  212.4 5.8 %decode.1 = bf16[4096,128]{1,0:T(8,128)(2,1)} custom-call(s32[1]{0:T(128)} %bitcast.mine_ref, bf16[4,136,128]{2,1,0:T(8,128)(2,1)S(1)} %bitcast.63, bf16[768,512]{1,0:T(8,128)(2,1)S(1)} %bitcast.62, f32[1,512]{1,0:T(1,128)S(1)} %bitcast.65, bf16[2,1024,512]{2,1,0:T(8,128)(2,1)S(1)} %pad_maximum_fusion.w_out_ref, f32[1,128]{1,0:T(1,128)S(1)} %bitcast.66), custom_call_target="tpu_custom_call" | custom-call | tf_op jit(solution)/shard_map/decode/pallas_call | solution.py:392
  (25 shorter events, 0.3 us)
Async XLA Ops:
  0.0 19.6 %copy-start = (bf16[4096,64]{0,1:T(8,128)(2,1)S(1)}, bf16[4096,64]{0,1:T(8,128)(2,1)}, u32[]{:S(2)}) copy-start(bf16[4096,64]{0,1:T(8,128)(2,1)} %param.22) | copy-start | bytes 1572868
  5.0 65.0 %all-to-all-start = ((bf16[32,512,128]{2,1,0:T(8,128)(2,1)}), bf16[32,512,128]{2,1,0:T(8,128)(2,1)}, u32[]{:S(2)}, u32[]{:S(2)}) async-start(bf16[32,512,128]{2,1,0:T(8,128)(2,1)} %pack_first.1), calls=%async_computation | async-start | bytes 8388608 | tf_op jit(solution)/shard_map/all_to_all | solution.py:437
  19.5 2.2 %copy-start.5 = (bf16[1,4,2,1024]{3,2,1,0:T(2,128)(2,1)S(1)}, bf16[1,4,2,1024]{3,2,1,0:T(2,128)(2,1)}, u32[]{:S(2)}) copy-start(bf16[1,4,2,1024]{3,2,1,0:T(2,128)(2,1)} %param.20) | copy-start | bytes 49156
  19.5 2.3 %copy-start.6 = (bf16[1,4,2,1024]{3,2,1,0:T(2,128)(2,1)S(1)}, bf16[1,4,2,1024]{3,2,1,0:T(2,128)(2,1)}, u32[]{:S(2)}) copy-start(bf16[1,4,2,1024]{3,2,1,0:T(2,128)(2,1)} %param.21) | copy-start | bytes 49156
  19.5 2.3 %copy-start.4 = (bf16[432,512]{1,0:T(8,128)(2,1)S(1)}, bf16[432,512]{1,0:T(8,128)(2,1)}, u32[]{:S(2)}) copy-start(bf16[432,512]{1,0:T(8,128)(2,1)} %param.24) | copy-start | bytes 1327108
  20.3 2.5 %copy-start.7 = (s32[1,4]{1,0:T(1,128)S(1)}, s32[1,4]{1,0:T(1,128)}, u32[]{:S(2)}) copy-start(s32[1,4]{1,0:T(1,128)} %param.23) | copy-start | bytes 52
  70.0 70.0 %all-to-all-start.1 = ((bf16[32,256,128]{2,1,0:T(8,128)(2,1)}), bf16[32,256,128]{2,1,0:T(8,128)(2,1)}, u32[]{:S(2)}, u32[]{:S(2)}) async-start(bf16[32,256,128]{2,1,0:T(8,128)(2,1)} %pack_window.1), calls=%async_computation.1 | async-start | bytes 4194304 | tf_op jit(solution)/shard_map/all_to_all | solution.py:437
  184.1 28.3 %copy-start.2 = (f32[512]{0:T(512)S(1)}, f32[512]{0:T(512)}, u32[]{:S(2)}) copy-start(f32[512]{0:T(512)} %param.25) | copy-start | bytes 6148
  184.1 28.3 %copy-start.3 = (f32[128]{0:T(128)S(1)}, f32[128]{0:T(128)}, u32[]{:S(2)}) copy-start(f32[128]{0:T(128)} %param.27) | copy-start | bytes 1540
  184.1 17.9 %all-to-all-start.2 = ((bf16[32,72,128]{2,1,0:T(8,128)(2,1)}), bf16[32,72,128]{2,1,0:T(8,128)(2,1)S(1)}, u32[]{:S(2)}, u32[]{:S(2)}) async-start(bf16[32,72,128]{2,1,0:T(8,128)(2,1)} %attend_last.1), calls=%async_computation.2 | async-start | bytes 1179648 | tf_op jit(solution)/shard_map/all_to_all | solution.py:437
  202.0 10.4 %copy-start.1 = (bf16[3,4,64,512]{3,2,1,0:T(8,128)(2,1)S(1)}, bf16[3,4,64,512]{3,2,1,0:T(8,128)(2,1)}, u32[]{:S(2)}) copy-start(bf16[3,4,64,512]{3,2,1,0:T(8,128)(2,1)} %pad.10) | copy-start | bytes 2359300

commit v7 on v6

--- a/solution.py
+++ b/solution.py
@@ -26,35 +26,61 @@
     )
 
 
-def pack_first_kernel(pick_ref, q_ref, k_ref, v_ref, sink_k_ref, sink_v_ref, out_ref):
-    for head in range(out_ref.shape[0]):
+def pack_first_kernel(
+    pick_ref, q_ref, k_ref, v_ref, sink_k_ref, sink_v_ref, out_hbm, out_ref, out_sem
+):
+    steps, heads = out_ref.shape[0], out_ref.shape[1]
+    part = heads // SPLIT
+    here = pl.program_id(0)
+
+    def store(step, n):
+        return pltpu.make_async_copy(
+            out_ref.at[step, pl.ds(n * part, part)],
+            out_hbm.at[pl.ds(step * heads + n * part, part)],
+            out_sem.at[step, n],
+        )
+
+    for head in range(heads):
         lanes = slice(head * HD, (head + 1) * HD)
-        out_ref[head, 0:TOK, :] = k_ref[:, lanes]
-        out_ref[head, 192 : 192 + TOK, :] = v_ref[:, lanes]
-        out_ref[head, 384 : 384 + TOK, :] = q_ref[:, lanes]
+        out_ref[here, head, 0:TOK, :] = k_ref[:, lanes]
+        out_ref[here, head, 192 : 192 + TOK, :] = v_ref[:, lanes]
+        out_ref[here, head, 384 : 384 + TOK, :] = q_ref[:, lanes]
         for tile in range(4):
-            rows = slice(tile * 32, tile * 32 + 16)
             at = TOK + tile * 16
-            out_ref[head, at : at + 16, :] = sink_k_ref[0, rows, lanes]
-            out_ref[head, 192 + at : 208 + at, :] = sink_v_ref[0, rows, lanes]
+            out_ref[here, head, at : at + 16, :] = sink_k_ref[0, tile, 0, :, lanes]
+            out_ref[here, head, 192 + at : 208 + at, :] = sink_v_ref[0, tile, 0, :, lanes]
+        if head % part == part - 1:
+            store(here, head // part).start()
+
+    @pl.when(here == steps - 1)
+    def _():
+        for step in range(steps):
+            for n in range(SPLIT):
+                store(step, n).wait()
 
 
 def pack_first(pick, current, keys, values):
     heads = 2 * HEADS_STEP
+    steps = HEADS // heads
     own = pl.BlockSpec((TOK, heads * HD), lambda i, pick: (0, i))
-    cached = pl.BlockSpec((1, TOK, heads * HD), lambda i, pick: (pick[0], 0, i))
+    cached = pl.BlockSpec((1, 4, 1, 16, heads * HD), lambda i, pick: (pick[0], 0, 0, 0, i))
+    by_frame = [x.reshape(x.shape[0], 4, 2, 16, x.shape[2]) for x in (keys, values)]
     return pl.pallas_call(
         pack_first_kernel,
         grid_spec=pltpu.PrefetchScalarGridSpec(
             num_scalar_prefetch=1,
-            grid=(HEADS // heads,),
+            grid=(steps,),
             in_specs=[own] * 3 + [cached] * 2,
-            out_specs=pl.BlockSpec((heads, 4 * TOK, HD), lambda i, pick: (i, 0, 0)),
+            out_specs=pl.BlockSpec(memory_space=pltpu.HBM),
+            scratch_shapes=[
+                pltpu.VMEM((steps, heads, 4 * TOK, HD), BF16),
+                pltpu.SemaphoreType.DMA((steps, SPLIT)),
+            ],
         ),
         out_shape=jax.ShapeDtypeStruct((HEADS, 4 * TOK, HD), BF16),
         compiler_params=params(60),
         name="pack_first",
-    )(pick, *current, keys, values)
+    )(pick, *current, *by_frame)
 
 
 def pack_window_kernel(pick_ref, k_ref, v_ref, out_ref):

time: 219 us -> 218 us (level)
  no operation moved by 1% of the time
where the time goes in v7:
time: 218 us
  Pallas kernels  124 us (57%)
  waiting for transfers between devices  53.3 us (24%)
  starting transfers between devices  23.2 us (11%)
  blocking collectives  10.1 us (5%)
  other arithmetic  5.1 us (2%)
    pallas_call x2, Pallas kernels, attend(): pl.pallas_call(body, grid=(steps,), in_specs=in_specs, out_specs=out_spec...  109 us
    all_to_all x3, waiting for transfers between devices, exchange(): return lax.all_to_all(x, axis, split_axis=0, concat_axis=0, tiled=True)  53.3 us
    all_to_all x3, starting transfers between devices, exchange(): return lax.all_to_all(x, axis, split_axis=0, concat_axis=0, tiled=True)  23.2 us
    all_gather x1, blocking collectives, local(): arrived = lax.all_gather(clean_rows(parts, noisy, prev), 'grp', axis=0)  10.1 us
    pallas_call x1, Pallas kernels, decode(): pl.pallas_call(decode_kernel, in_specs=[pl.BlockSpec(memory_space=pltpu.S...  5.77 us
    pallas_call x1, Pallas kernels, pack_window(): pl.pallas_call(pack_window_kernel, grid_spec=pltpu.PrefetchScalarGridSpec...  4.79 us
    pallas_call x1, Pallas kernels, pack_first(): pl.pallas_call(pack_first_kernel, grid_spec=pltpu.PrefetchScalarGridSpec(...  4.49 us
  transfers between devices with their start and end apart: 3, of which 2 were waited for; matrix products, arithmetic and copies ran while one was open for 3% of the time, Pallas kernels for 32%

profile of v7, /device:TPU:1, one launch (start us, length us, event | category | flops | bytes accessed | tf_op | source)
XLA Modules:
  0.0 217.9 jit_solution(9367290190724887389)
XLA Ops:
  0.0 4.5 %pack_first.1 = bf16[32,512,128]{2,1,0:T(8,128)(2,1)} custom-call(s32[2]{0:T(128)} %bitcast.80, bf16[128,4096]{1,0:T(8,128)(2,1)} %bitcast.75, bf16[128,4096]{1,0:T(8,128)(2,1)} %bitcast.76, bf16[128,4096]{1,0:T(8,128)(2,1)} %bitcast.77, bf16[4,4,2,16,4096]{4,3,2,1,0:T(8,128)(2,1)} %bitcast.71, bf16[4,4,2,16,4096]{4,3,2,1,0:T(8,128)(2,1)} %bitcast.73), custom_call_target="tpu_custom_call" | custom-call | tf_op jit(solution)/shard_map/pack_first/pallas_call | solution.py:68
  4.5 9.9 %all-to-all-start = ((bf16[32,512,128]{2,1,0:T(8,128)(2,1)}), bf16[32,512,128]{2,1,0:T(8,128)(2,1)}, u32[]{:S(2)}, u32[]{:S(2)}) async-start(bf16[32,512,128]{2,1,0:T(8,128)(2,1)} %pack_first.1), calls=%async_computation | async-start | bytes 8388608 | tf_op jit(solution)/shard_map/all_to_all | solution.py:463
  14.4 0.0 copy-start.5
  14.4 0.0 copy-start.6
  14.4 0.7 copy.18.refs_6_
  15.2 1.4 convert_element_type.21
  16.7 4.8 %pack_window.1 = bf16[32,256,128]{2,1,0:T(8,128)(2,1)} custom-call(s32[2]{0:T(128)} %bitcast.81, bf16[4,128,4096]{2,1,0:T(8,128)(2,1)} %bitcast.72, bf16[4,128,4096]{2,1,0:T(8,128)(2,1)} %bitcast.74), custom_call_target="tpu_custom_call" | custom-call | tf_op jit(solution)/shard_map/pack_window/pallas_call | solution.py:95
  21.5 1.0 pad.10
  22.5 0.1 compare_select_fusion
  22.6 0.1 fusion.1
  22.9 0.1 fusion.2
  23.0 0.1 fusion.10
  23.1 3.0 %maximum_bitcast_fusion = (bf16[1,1024,512]{2,1,0:T(8,128)(2,1)S(1)}, bf16[1,1024,512]{2,1,0:T(8,128)(2,1)S(1)}) fusion(bf16[512,128]{1,0:T(8,128)(2,1)S(1)} %get-tuple-element.38, bf16[512,128]{1,0:T(8,128)(2,1)S(1)} %get-tuple-element.40, bf16[512,128]{1,0:T(8,128)(2,1)S(1)} %get-tuple-element.39, bf16[512,128]{1,0:T(8,128)(2,1)S(1)} %get-tuple-element.37, ...), kind=kLoop, calls=%fused_computation.1 | loop fusion | flops 16777216 | bytes 4194304 | tf_op jit(solution)/shard_map/stack | solution.py:455
  26.1 0.2 pad_maximum_fusion.w_out_ref
  26.3 0.1 pad_maximum_fusion.1.refs_5_
  26.3 43.2 %all-to-all-done.q_ref.refs_0_.refs_1_ = bf16[32,512,128]{2,1,0:T(8,128)(2,1)} async-done(((bf16[32,512,128]{2,1,0:T(8,128)(2,1)}), bf16[32,512,128]{2,1,0:T(8,128)(2,1)}, u32[]{:S(2)}, u32[]{:S(2)}) %all-to-all-start) | async-done | bytes 4194336 | tf_op jit(solution)/shard_map/all_to_all | solution.py:463
  69.5 5.6 %all-to-all-start.1 = ((bf16[32,256,128]{2,1,0:T(8,128)(2,1)}), bf16[32,256,128]{2,1,0:T(8,128)(2,1)}, u32[]{:S(2)}, u32[]{:S(2)}) async-start(bf16[32,256,128]{2,1,0:T(8,128)(2,1)} %pack_window.1), calls=%async_computation.1 | async-start | bytes 4194304 | tf_op jit(solution)/shard_map/all_to_all | solution.py:463
  75.1 64.4 %attend_first.1 = (s32[2]{0:T(128)}, f32[8,4096]{1,0:T(8,128)}, f32[8,4096]{1,0:T(8,128)}, f32[128,4096]{1,0:T(8,128)}) custom-call(bf16[32,512,128]{2,1,0:T(8,128)(2,1)} %all-to-all-done.q_ref.refs_0_.refs_1_, bf16[32,512,128]{2,1,0:T(8,128)(2,1)} %all-to-all-done.q_ref.refs_0_.refs_1_, bf16[32,512,128]{2,1,0:T(8,128)(2,1)} %all-to-all-done.q_ref.refs_0_.refs_1_), custom_call_target="tpu_custom_call" | custom-call | flops 19327352832 | bytes 8388608 | tf_op jit(solution)/shard_map/attend_first/pallas_call | solution.py:265
  139.5 44.1 %attend_last.1 = bf16[32,72,128]{2,1,0:T(8,128)(2,1)} custom-call(bf16[32,512,128]{2,1,0:T(8,128)(2,1)} %all-to-all-done.q_ref.refs_0_.refs_1_, bf16[32,256,128]{2,1,0:T(8,128)(2,1)} %all-to-all-done.1.refs_0_.refs_1_, bf16[32,256,128]{2,1,0:T(8,128)(2,1)} %all-to-all-done.1.refs_0_.refs_1_, s32[2]{0:T(128)} %get-tuple-element.18.refs_2_, ...), custom_call_target="tpu_custom_call" | custom-call | flops 12884901888 | bytes 8388608 | tf_op jit(solution)/shard_map/attend_last/pallas_call | solution.py:265
  183.6 7.8 %all-to-all-start.2 = ((bf16[32,72,128]{2,1,0:T(8,128)(2,1)}), bf16[32,72,128]{2,1,0:T(8,128)(2,1)S(1)}, u32[]{:S(2)}, u32[]{:S(2)}) async-start(bf16[32,72,128]{2,1,0:T(8,128)(2,1)} %attend_last.1), calls=%async_computation.2 | async-start | bytes 1179648 | tf_op jit(solution)/shard_map/all_to_all | solution.py:463
  191.4 10.1 %all-to-all-done.2.refs_0_.refs_1_.refs_2_.refs_3_ = bf16[32,72,128]{2,1,0:T(8,128)(2,1)S(1)} async-done(((bf16[32,72,128]{2,1,0:T(8,128)(2,1)}), bf16[32,72,128]{2,1,0:T(8,128)(2,1)S(1)}, u32[]{:S(2)}, u32[]{:S(2)}) %all-to-all-start.2) | async-done | bytes 589856 | tf_op jit(solution)/shard_map/all_to_all | solution.py:463
  201.5 0.3 clean_rows.1
  201.8 10.1 %all-gather = bf16[544,128]{1,0:T(8,128)(2,1)S(1)} all-gather(bf16[136,128]{1,0:T(8,128)(2,1)S(1)} %clean_rows.1), channel_id=2, replica_groups=mesh['grp'=4,'ctx'=32] {'grp'}, dimensions={0}, use_global_device_ids=true | all-gather | bytes 174080 | tf_op jit(solution)/shard_map/all_gather | solution.py:501
  211.9 5.8 %decode.1 = bf16[4096,128]{1,0:T(8,128)(2,1)} custom-call(s32[1]{0:T(128)} %bitcast.mine_ref, bf16[4,136,128]{2,1,0:T(8,128)(2,1)S(1)} %bitcast.65, bf16[768,512]{1,0:T(8,128)(2,1)S(1)} %bitcast.64, f32[1,512]{1,0:T(1,128)S(1)} %bitcast.67, bf16[2,1024,512]{2,1,0:T(8,128)(2,1)S(1)} %pad_maximum_fusion.w_out_ref, f32[1,128]{1,0:T(1,128)S(1)} %bitcast.68), custom_call_target="tpu_custom_call" | custom-call | tf_op jit(solution)/shard_map/decode/pallas_call | solution.py:418
  (25 shorter events, 0.3 us)
Async XLA Ops:
  0.0 14.4 %copy-start = (bf16[4096,64]{0,1:T(8,128)(2,1)S(1)}, bf16[4096,64]{0,1:T(8,128)(2,1)}, u32[]{:S(2)}) copy-start(bf16[4096,64]{0,1:T(8,128)(2,1)} %param.22) | copy-start | bytes 1572868
  4.5 65.0 %all-to-all-start = ((bf16[32,512,128]{2,1,0:T(8,128)(2,1)}), bf16[32,512,128]{2,1,0:T(8,128)(2,1)}, u32[]{:S(2)}, u32[]{:S(2)}) async-start(bf16[32,512,128]{2,1,0:T(8,128)(2,1)} %pack_first.1), calls=%async_computation | async-start | bytes 8388608 | tf_op jit(solution)/shard_map/all_to_all | solution.py:463
  14.4 2.2 %copy-start.5 = (bf16[1,4,2,1024]{3,2,1,0:T(2,128)(2,1)S(1)}, bf16[1,4,2,1024]{3,2,1,0:T(2,128)(2,1)}, u32[]{:S(2)}) copy-start(bf16[1,4,2,1024]{3,2,1,0:T(2,128)(2,1)} %param.20) | copy-start | bytes 49156
  14.4 2.3 %copy-start.6 = (bf16[1,4,2,1024]{3,2,1,0:T(2,128)(2,1)S(1)}, bf16[1,4,2,1024]{3,2,1,0:T(2,128)(2,1)}, u32[]{:S(2)}) copy-start(bf16[1,4,2,1024]{3,2,1,0:T(2,128)(2,1)} %param.21) | copy-start | bytes 49156
  16.7 4.8 %copy-start.4 = (bf16[432,512]{1,0:T(8,128)(2,1)S(1)}, bf16[432,512]{1,0:T(8,128)(2,1)}, u32[]{:S(2)}) copy-start(bf16[432,512]{1,0:T(8,128)(2,1)} %param.24) | copy-start | bytes 1327108
  16.7 5.8 %copy-start.7 = (s32[1,4]{1,0:T(1,128)S(1)}, s32[1,4]{1,0:T(1,128)}, u32[]{:S(2)}) copy-start(s32[1,4]{1,0:T(1,128)} %param.23) | copy-start | bytes 52
  69.5 70.0 %all-to-all-start.1 = ((bf16[32,256,128]{2,1,0:T(8,128)(2,1)}), bf16[32,256,128]{2,1,0:T(8,128)(2,1)}, u32[]{:S(2)}, u32[]{:S(2)}) async-start(bf16[32,256,128]{2,1,0:T(8,128)(2,1)} %pack_window.1), calls=%async_computation.1 | async-start | bytes 4194304 | tf_op jit(solution)/shard_map/all_to_all | solution.py:463
  183.6 28.3 %copy-start.2 = (f32[512]{0:T(512)S(1)}, f32[512]{0:T(512)}, u32[]{:S(2)}) copy-start(f32[512]{0:T(512)} %param.25) | copy-start | bytes 6148
  183.6 28.3 %copy-start.3 = (f32[128]{0:T(128)S(1)}, f32[128]{0:T(128)}, u32[]{:S(2)}) copy-start(f32[128]{0:T(128)} %param.27) | copy-start | bytes 1540
  183.6 17.9 %all-to-all-start.2 = ((bf16[32,72,128]{2,1,0:T(8,128)(2,1)}), bf16[32,72,128]{2,1,0:T(8,128)(2,1)S(1)}, u32[]{:S(2)}, u32[]{:S(2)}) async-start(bf16[32,72,128]{2,1,0:T(8,128)(2,1)} %attend_last.1), calls=%async_computation.2 | async-start | bytes 1179648 | tf_op jit(solution)/shard_map/all_to_all | solution.py:463
  201.5 10.4 %copy-start.1 = (bf16[3,4,64,512]{3,2,1,0:T(8,128)(2,1)S(1)}, bf16[3,4,64,512]{3,2,1,0:T(8,128)(2,1)}, u32[]{:S(2)}) copy-start(bf16[3,4,64,512]{3,2,1,0:T(8,128)(2,1)} %pad.10) | copy-start | bytes 2359300
